TPU v7x, 32 devices: a whole 2x2x4 slice. The times are simulated.
32 devices in a mesh: tm: 16 (over z, y, x), order: 2 (over core).
Axes of the slice: x: 2, y: 2, z: 4, core: 2. Of those that a mesh axis runs over, the one named last changes fastest.
Arguments:
- solution: float32 [16, 2, 5760], P(None, 'order'), may hold values from -6 to 6
- residual: float32 [16, 2, 5760], P(None, 'order'), may hold values from -3 to 3
- direction: float32 [16, 2, 5760], P(None, 'order'), may hold values from -6 to 6
- precond: float32 [2, 5760], P('order'), may hold values from 0.25 to 4
- design: bfloat16 [4, 1024, 2, 5760], P(None, 'tm', 'order'), may hold values from -0.078125 to 0.078125
- epoch_counts: int32 [16], P('tm'), may hold values from 32 to 64, as said below
- segment_orders: int32 [4, 2], replicated, may hold values from 1 to 2, as said below
- pole_life: float32 [4, 2, 2], replicated, may hold values from 8 to 8192
- zero_ratio: float32 [4, 2, 2], replicated, may hold values from 0.1 to 2
- fir_taps: float32 [4, 9], replicated, may hold values from -2 to 2
Outputs:
- new_solution: float32 [16, 2, 5760], P(None, 'order', 'tm')
- new_residual: float32 [16, 2, 5760], P(None, 'order', 'tm')
- new_direction: float32 [16, 2, 5760], P(None, 'order', 'tm')
Inputs may be any that keep to these rules, and one draw needn't show every extreme that they name: `epoch_counts`: valid epochs at the start of each block of 64 epochs; some block is complete. `segment_orders`: active sections of each segment; some segment of some component has all 2.
All inputs are finite; a program needn't handle non-finite values.
Results may differ from a plain program's by a relative error of at most 0.00105.
The roundings to bfloat16 on the way count: a program that leaves them out, or rounds other values in their place, can miss the bound.
Values may be sent and summed in bfloat16 or wider, within the bound.
No kernel may reach another device: no remote copies, remote signals or barrier semaphores. Data moves between devices by JAX's collectives and lax.ppermute only.
A program may use at most 64 MiB of HBM per device.

v0:
```python
import jax
import jax.numpy as jnp
from jax import lax
from jax.sharding import PartitionSpec as P

HIGHEST = lax.Precision.HIGHEST


def prefix(value, axis, join, neutral, backward):
    count, mine = (lax.axis_size(axis), lax.axis_index(axis))
    pieces = jax.tree.map(lambda part: lax.all_gather(part, axis), value)
    if backward:
        pieces = jax.tree.map(lambda part: part[::-1], pieces)
        mine = count - 1 - mine
    subtotal = jax.tree.map(
        lambda part, zero: jnp.full_like(part, 0) + jnp.asarray(zero, part.dtype), value, neutral
    )

    def lap(position, subtotal):
        longer = join(subtotal, jax.tree.map(lambda part: part[position], pieces))
        return jax.tree.map(lambda new, old: jnp.where(position < mine, new, old), longer, subtotal)

    return lax.fori_loop(0, count - 1, lap, subtotal)


def shifted(shard, axis, by):
    count = lax.axis_size(axis)
    pairs = [(i, i + by) for i in range(count) if 0 <= i + by < count]
    return lax.ppermute(shard, axis, pairs)


def filter_rates(segment_orders, pole_life, zero_ratio):
    components = pole_life.shape[0]
    sections = pole_life.shape[2]
    pole_all = jnp.exp(-1.0 / pole_life)
    active = jnp.arange(sections)[None, None, :] < segment_orders[:, :, None]
    pole_rate = jnp.where(active, pole_all, jnp.zeros_like(pole_all)).reshape(components, -1)
    zero_all = 1.0 - zero_ratio * (1.0 - pole_all)
    zero_rate = jnp.where(active, zero_all, jnp.zeros_like(zero_all)).reshape(components, -1)
    return (pole_rate, zero_rate)


def section_tables(pole_rate, length):
    steps_after = (jnp.arange(length)[None, :] - jnp.arange(length)[:, None]).astype(jnp.float32)
    powers = jnp.power(pole_rate[:, :, None, None], jnp.maximum(steps_after, 0.0)[None, None])
    triangle = jnp.where((steps_after >= 0.0)[None, None], powers, jnp.zeros_like(powers))
    exponent = (jnp.arange(length) + 1).astype(jnp.float32)
    decay = jnp.power(pole_rate[:, :, None], exponent[None, None, :])
    return (triangle, decay)


def local_cascade(series, initial, zero_rate, triangle, decay):
    length = series.shape[2]
    current = series
    ends = [series[:, :, length - 1]]
    for section in range(zero_rate.shape[1]):
        before = jnp.concatenate(
            [initial[:, :, section][:, :, None], current[:, :, : length - 1]], axis=2
        )
        driven = current - zero_rate[:, section][None, :, None] * before
        output = jnp.einsum("bcs,cst->bct", driven, triangle[:, section], precision=HIGHEST)
        output = output + decay[:, section][None] * initial[:, :, section + 1][:, :, None]
        ends.append(output[:, :, length - 1])
        current = output
    return (current, jnp.stack(ends, axis=2))


def compose(earlier, following):
    first_map, first_end = earlier
    second_map, second_end = following
    joined_map = jnp.einsum("ckm,cml->ckl", second_map, first_map, precision=HIGHEST)
    joined_end = jnp.einsum("ckm,cmb->ckb", second_map, first_end, precision=HIGHEST) + second_end
    return (joined_map, joined_end)


def cascade_pass(series, pole_rate, zero_rate, backward):
    count, components, length = series.shape
    states = zero_rate.shape[1] + 1
    ordered = jnp.flip(series, 2) if backward else series
    triangle, decay = section_tables(pole_rate, length)
    driven_out, driven_end = local_cascade(
        ordered, jnp.zeros((count, components, states), jnp.float32), zero_rate, triangle, decay
    )
    impulses = jnp.broadcast_to(
        jnp.eye(states, dtype=jnp.float32)[:, None, :], (states, components, states)
    )
    response, response_end = local_cascade(
        jnp.zeros((states, components, length), jnp.float32), impulses, zero_rate, triangle, decay
    )
    block_map = jnp.transpose(response_end, (1, 2, 0))
    block_end = jnp.transpose(driven_end, (1, 2, 0))
    identity = jnp.broadcast_to(jnp.eye(states, dtype=jnp.float32), (components, states, states))
    carried = prefix(
        (block_map, block_end), "tm", compose, (identity, jnp.zeros_like(block_end)), backward
    )
    output = driven_out + jnp.einsum("mct,cmb->bct", response, carried[1], precision=HIGHEST)
    return jnp.flip(output, 2) if backward else output


def fir_pass(series, fir_taps, backward):
    length = series.shape[2]
    fir_reach = fir_taps.shape[1] - 1
    ordered = jnp.flip(series, 2) if backward else series
    rim = shifted(ordered[:, :, length - fir_reach :], "tm", -1 if backward else 1)
    extended = jnp.concatenate([rim, ordered], axis=2)
    lag_table = jnp.arange(length)[None, :] + fir_reach - jnp.arange(length + fir_reach)[:, None]
    selector = (lag_table[None] == jnp.arange(fir_reach + 1)[:, None, None]).astype(jnp.float32)
    banded = jnp.einsum("ck,kst->cst", fir_taps, selector, precision=HIGHEST)
    output = jnp.einsum("bcs,cst->bct", extended, banded, precision=HIGHEST)
    return jnp.flip(output, 2) if backward else output


def filter_both(series, pole_rate, zero_rate, fir_taps):
    whitened = cascade_pass(series, pole_rate, zero_rate, False)
    filtered = fir_pass(whitened, fir_taps, False)
    returned = fir_pass(filtered, fir_taps, True)
    return cascade_pass(returned, pole_rate, zero_rate, True)


def order_sums(values):
    return lax.psum(values, "order")


def pcg_update(current, remaining, search, inverse_diag, normal, reducer):
    energy, curvature = reducer(
        (
            jnp.sum(remaining * inverse_diag[None, :] * remaining, axis=1),
            jnp.sum(search * normal, axis=1),
        )
    )
    step_length = (energy / curvature)[:, None]
    new_solution = current + step_length * search
    new_residual = remaining - step_length * normal
    conditioned = inverse_diag[None, :] * new_residual
    (energy_next,) = reducer((jnp.sum(new_residual * conditioned, axis=1),))
    new_direction = conditioned + (energy_next / energy)[:, None] * search
    return (new_solution, new_residual, new_direction)


def shards(
    solution,
    residual,
    direction,
    precond,
    design,
    epoch_counts,
    segment_orders,
    pole_life,
    zero_ratio,
    fir_taps,
):
    count = direction.shape[0]
    design_rows = design[:, :, 0, :]
    components = design_rows.shape[0]
    length = design_rows.shape[1]
    search = direction[:, 0, :]
    search_low = search.astype(jnp.bfloat16)
    predicted = jnp.einsum(
        "ctn,jn->jct", design_rows, search_low, preferred_element_type=jnp.float32
    )
    live_mask = (jnp.arange(length) < epoch_counts[0]).astype(jnp.float32)
    pole_rate, zero_rate = filter_rates(segment_orders, pole_life, zero_ratio)
    flattened = predicted.reshape(count, components * length)
    complete = lax.psum(flattened, "order")
    complete = complete.reshape(count, components, length) * live_mask[None, None, :]
    weighted = (
        filter_both(complete, pole_rate, zero_rate, fir_taps) * live_mask[None, None, :]
    ).astype(jnp.bfloat16)
    partial_normal = jnp.einsum(
        "ctn,jct->jn", design_rows, weighted, preferred_element_type=jnp.float32
    )
    share_width = partial_normal.shape[1] // lax.axis_size("tm")
    share_start = lax.axis_index("tm") * share_width
    normal = lax.psum(partial_normal, "tm")
    complete_update = pcg_update(
        solution[:, 0, :], residual[:, 0, :], search, precond[0], normal, order_sums
    )
    updated = tuple(
        (
            lax.dynamic_slice_in_dim(vector, share_start, share_width, 1)
            for vector in complete_update
        )
    )
    return tuple((vector[:, None, :] for vector in updated))


def solution(mesh):
    placed = (
        P(None, "order", None),
        P(None, "order", None),
        P(None, "order", None),
        P("order", None),
        P(None, "tm", "order", None),
        P("tm"),
        P(),
        P(),
        P(),
        P(),
    )
    return jax.shard_map(
        shards,
        mesh=mesh,
        in_specs=placed,
        out_specs=(P(None, "order", "tm"), P(None, "order", "tm"), P(None, "order", "tm")),
        check_vma=False,
    )
```

profile of v0, /device:TPU:0, one launch (start us, length us, event | category | flops | bytes accessed | tf_op | source)
XLA Modules:
  0.0 362.1 jit_solution(17933225995034671679)
XLA Ops:
  7.9 0.9 subtract_select_fusion
  12.0 1.2 convert_element_type.62
  14.2 3.7 %psum.36 = f32[16,4,64]{2,0,1:T(8,128)S(1)} all-reduce(f32[16,4,64]{2,0,1:T(8,128)S(1)} %copy.44), channel_id=1, replica_groups=mesh['tm'=16,'order'=2] {'order'}, use_global_device_ids=true, to_apply=%region_2.3 | all-reduce | flops 4096 | bytes 32768 | tf_op jit(solution)/shard_map/psum | solution.py:164
  18.6 1.5 power_select_fusion
  20.9 1.0 fusion.26
  22.6 1.0 fusion.25
  25.0 1.0 fusion.24
  27.4 1.0 fusion.23
  29.6 1.4 stack.10
  31.0 1.4 copy.45
  32.5 1.0 fusion.22
  34.1 1.0 fusion.21
  35.8 0.9 fusion.20
  37.4 1.0 fusion.19
  39.1 1.5 stack.11
  41.5 45.8 %all-gather.1 = f32[64,5,16]{2,1,0:T(8,128)} all-gather(f32[4,5,16]{2,1,0:T(8,128)S(1)} %copy.46), channel_id=3, replica_groups=mesh['tm'=16,'order'=2] {'tm'}, dimensions={0}, use_global_device_ids=true | all-gather | bytes 21760 | tf_op jit(solution)/shard_map/all_gather | solution.py:11
  87.3 37.2 %all-gather = f32[64,5,5]{2,1,0:T(8,128)S(1)} all-gather(f32[4,5,5]{2,1,0:T(8,128)} %copy.45), channel_id=2, replica_groups=mesh['tm'=16,'order'=2] {'tm'}, dimensions={0}, use_global_device_ids=true | all-gather | bytes 6800 | tf_op jit(solution)/shard_map/all_gather | solution.py:11
  125.2 24.4 %while.28 = (s32[]{:T(128)}, f32[4,5,16]{2,1,0:T(8,128)S(1)}, s32[]{:T(128)}, f32[16,4,5,5]{3,1,2,0:T(4,128)}, f32[16,4,5,16]{3,2,1,0:T(8,128)}, /*index=5*/s32[]{:T(128)}, s32[]{:T(128)}) while((s32[]{:T(128)}, f32[4,5,16]{2,1,0:T(8,128)S(1)}, s32[]{:T(128)}, f32[16,4,5,5]{3,1,2,0:T(4,128)}, f32[16,4,5,16]{3,2,1,0:T(8,128)}, ...), condition=%wide.region_4.5_spmd.clone, body=%wide.region_3.4_spmd.clone.sunk | while | flops 20484 | bytes 51083 | solution.py:23
  125.9 0.9 fusion.123
  137.3 0.9 fusion.123
  142.1 0.9 fusion.123
  147.0 0.9 fusion.123
  149.9 3.8 %collective-permute-start = (f32[16,4,8]{2,0,1:T(8,128)S(1)}, f32[16,4,8]{2,0,1:T(8,128)S(1)}, u32[]{:S(2)}, u32[]{:S(2)}) collective-permute-start(f32[16,4,8]{2,0,1:T(8,128)S(1)} %slice.290), channel_id=1, source_target_pairs={{0,2},{2,4},{4,6},{6,8},{8,10},{10,12},{12,14},{14,16},{16,18},{18... | collective-permute-start | bytes 6152 | tf_op jit(solution)/shard_map/ppermute | solution.py:29
  153.8 1.0 convolution_bitcast_fusion.1
  156.5 1.3 collective-permute-start.1
  157.8 1.6 rev.16
  160.1 2.7 collective-permute-done.1
  162.7 1.3 convolution_bitcast_fusion.3
  164.7 1.0 fusion.17
  166.4 0.9 fusion.16
  168.0 0.9 fusion.15
  170.0 0.9 stack.12
  171.0 42.1 %all-gather.2 = f32[64,5,16]{2,1,0:T(8,128)} all-gather(f32[4,5,16]{2,1,0:T(8,128)S(1)} %copy.51), channel_id=4, replica_groups=mesh['tm'=16,'order'=2] {'tm'}, dimensions={0}, use_global_device_ids=true | all-gather | bytes 21760 | tf_op jit(solution)/shard_map/all_gather | solution.py:11
  213.1 1.7 rev.17
  214.8 24.4 %while.29 = (s32[]{:T(128)}, f32[4,5,16]{2,1,0:T(8,128)S(1)}, s32[]{:T(128)}, f32[16,4,5,5]{3,1,2,0:T(4,128)}, f32[16,4,5,16]{3,2,1,0:T(8,128)}, /*index=5*/s32[]{:T(128)}, s32[]{:T(128)}) while((s32[]{:T(128)}, f32[4,5,16]{2,1,0:T(8,128)S(1)}, s32[]{:T(128)}, f32[16,4,5,5]{3,1,2,0:T(4,128)}, f32[16,4,5,16]{3,2,1,0:T(8,128)}, ...), condition=%wide.region_6.7_spmd.clone, body=%wide.region_5.6_spmd.clone.sunk | while | flops 20484 | bytes 51083 | solution.py:23
  220.4 0.9 fusion.126
  223.6 0.9 fusion.126
  228.5 0.9 fusion.126
  231.8 0.9 fusion.126
  236.7 0.9 fusion.126
  239.5 1.8 convolution_bitcast_fusion
  241.4 1.9 copy_bitcast_fusion
  243.4 1.2 fusion.27
  244.5 100.4 %all-reduce.12.cloned.1.call-done = f32[16,5760]{1,0:T(8,128)} async-done(((f32[16,5760]{1,0:T(8,128)}), f32[16,5760]{1,0:T(8,128)}) %all-reduce.12.cloned.1.call-update) | async-done | bytes 368656 | tf_op jit(solution)/shard_map/psum | solution.py:174
  345.0 1.1 multiply_reduce_fusion.1
  346.1 2.5 all-reduce.9
  348.6 1.4 multiply_reduce_fusion
  349.9 2.5 psum.39
  (161 shorter events, 63.9 us)
Async XLA Ops:
  7.2 6.1 %copy-start = (bf16[4,64,1,5760]{3,1,2,0:T(8,128)(2,1)S(1)}, bf16[4,64,1,5760]{3,1,2,0:T(8,128)(2,1)}, u32[]{:S(2)}) copy-start(bf16[4,64,1,5760]{3,1,2,0:T(8,128)(2,1)} %param.18) | copy-start | bytes 8847364
  7.2 337.8 %all-reduce.12.cloned.1.call-start = ((), (), s32[]{:S(2)}) async-start(), calls=%async_computation | async-start | bytes 737280 | tf_op jit(solution)/shard_map/psum | solution.py:174
  8.8 0.7 copy-start.7
  10.8 7.2 %copy-start.9 = (f32[64]{0:T(128)}, f32[64]{0:T(128)S(1)}, u32[]{:S(2)}) copy-start(f32[64]{0:T(128)S(1)} %compare_convert_fusion) | copy-start | bytes 772
  87.2 79.1 %copy-start.6 = (f32[4,64]{1,0:T(4,128)S(1)}, f32[4,64]{1,0:T(4,128)}, u32[]{:S(2)}) copy-start(f32[4,64]{1,0:T(4,128)} %get-tuple-element.276) | copy-start | bytes 3076
  87.2 80.7 %copy-start.5 = (f32[4,64]{1,0:T(4,128)S(1)}, f32[4,64]{1,0:T(4,128)}, u32[]{:S(2)}) copy-start(f32[4,64]{1,0:T(4,128)} %get-tuple-element.275) | copy-start | bytes 3076
  87.3 82.4 %copy-start.4 = (f32[4,64]{1,0:T(4,128)S(1)}, f32[4,64]{1,0:T(4,128)}, u32[]{:S(2)}) copy-start(f32[4,64]{1,0:T(4,128)} %get-tuple-element.274) | copy-start | bytes 3076
  87.3 82.4 %copy-start.8 = (f32[4]{0:T(128)S(1)}, f32[4]{0:T(128)}, u32[]{:S(2)}) copy-start(f32[4]{0:T(128)} %get-tuple-element.285) | copy-start | bytes 52
  149.9 5.4 %collective-permute-start = (f32[16,4,8]{2,0,1:T(8,128)S(1)}, f32[16,4,8]{2,0,1:T(8,128)S(1)}, u32[]{:S(2)}, u32[]{:S(2)}) collective-permute-start(f32[16,4,8]{2,0,1:T(8,128)S(1)} %slice.290), channel_id=1, source_target_pairs={{0,2},{2,4},{4,6},{6,8},{8,10},{10,12},{12,14},{14,16},{16,18},{18... | collective-permute-start | bytes 6152 | tf_op jit(solution)/shard_map/ppermute | solution.py:29
  154.8 0.6 copy-start.2
  156.5 6.3 %collective-permute-start.1 = (f32[16,4,8]{2,0,1:T(8,128)}, f32[16,4,8]{2,0,1:T(8,128)}, u32[]{:S(2)}, u32[]{:S(2)}) collective-permute-start(f32[16,4,8]{2,0,1:T(8,128)} %slice.256), channel_id=1, source_target_pairs={{2,0},{4,2},{6,4},{8,6},{10,8},{12,10},{14,12},{16,14},{18,16},{20... | collective-permute-start | bytes 6152 | tf_op jit(solution)/shard_map/ppermute | solution.py:29
  169.9 71.5 %copy-start.1 = (f32[16,1,5760]{2,1,0:T(1,128)S(1)}, f32[16,1,5760]{2,1,0:T(1,128)}, u32[]{:S(2)}) copy-start(f32[16,1,5760]{2,1,0:T(1,128)} %param.16) | copy-start | bytes 1105924
  214.8 28.6 %copy-start.3 = (f32[1,5760]{1,0:T(1,128)S(1)}, f32[1,5760]{1,0:T(1,128)}, u32[]{:S(2)}) copy-start(f32[1,5760]{1,0:T(1,128)} %param.17) | copy-start | bytes 69124
Sparse Core Ops, SparseCore 0:
  241.5 103.4 all-reduce.11
where the time goes:
time: 368 us; the launch traced here: 362 us
  blocking collectives  134 us (36%)
  waiting for transfers between devices  104 us (28%)
  local copies, waits for them, and re-layouts  51.3 us (14%)
  matrix products  42.8 us (12%)
  between operations  15 us (4%)
  other arithmetic  9.58 us (3%)
  starting transfers between devices  5.12 us (1%)
    all_gather x3, blocking collectives, prefix(): pieces = jax.tree.map(lambda part: lax.all_gather(part, axis), value)  125 us
    psum x1, waiting for transfers between devices, shards(): normal = lax.psum(partial_normal, 'tm')  100 us
    dot_general x30, matrix products, compose(): jnp.einsum('ckm,cmb->ckb', second_map, first_end, precision=HIGHEST)  26.3 us
    squeeze x30, local copies, waits for them, and re-layouts, lap(): longer = join(subtotal, jax.tree.map(lambda part: part[position], pieces))  21.3 us
    dot_general x12, matrix products, local_cascade(): jnp.einsum('bcs,cst->bct', driven, triangle[:, section], precision=HIGHEST)  10.8 us
  transfers between devices with their start and end apart: 3, of which 3 were waited for; matrix products, arithmetic and copies ran while one was open for 2% of the time, Pallas kernels for 0%

commit v1 on v0

v1 whole, which is shorter than its diff:
```python
import functools

import jax
import jax.numpy as jnp
from jax import lax
from jax.experimental import pallas as pl
from jax.experimental.pallas import tpu as pltpu
from jax.sharding import PartitionSpec as P

HIGHEST = lax.Precision.HIGHEST
F32 = jnp.float32
BF16 = jnp.bfloat16
LANES = 128
SLOT = 16
VMEM_LIMIT = 48 * 1024 * 1024


def vmem():
    return pl.BlockSpec(memory_space=pltpu.VMEM)


def smem():
    return pl.BlockSpec(memory_space=pltpu.SMEM)


def call(kernel, outs, *args, specs=None, scratch=()):
    return pl.pallas_call(
        kernel,
        out_shape=outs,
        in_specs=specs or [vmem()] * len(args),
        out_specs=jax.tree.map(lambda _: vmem(), outs),
        scratch_shapes=scratch,
        compiler_params=pltpu.CompilerParams(vmem_limit_bytes=VMEM_LIMIT),
    )(*args)


def shape(*dims):
    return jax.ShapeDtypeStruct(dims, F32)


def predict_kernel(direction_ref, residual_ref, precond_ref, design_ref, out_ref):
    search = direction_ref[...]
    high = search.astype(BF16)
    rest = search - high.astype(F32)
    middle = rest.astype(BF16)
    low = (rest - middle.astype(F32)).astype(BF16)
    stacked = jnp.concatenate([high, middle, low], axis=0)
    count = search.shape[0]
    sums = lax.dot_general(
        design_ref[...], stacked, (((1,), (1,)), ((), ())), preferred_element_type=F32
    )
    length = sums.shape[0] * count // (LANES // 2)
    pieces = [sums[start : start + length] for start in range(0, sums.shape[0], length)]
    coarse = [piece[:, :count] for piece in pieces]
    fine = [piece[:, count : 2 * count] + piece[:, 2 * count :] for piece in pieces]
    out_ref[:length, :] = jnp.concatenate(coarse + fine, axis=1)
    remaining = residual_ref[...]
    energy = jnp.sum(remaining * precond_ref[...] * remaining, axis=1, keepdims=True)
    out_ref[length:, :] = jnp.broadcast_to(energy, (count, LANES))


def rows_of(value):
    return lax.broadcasted_iota(jnp.int32, value.shape, 0)


def down(value, by):
    moved = pltpu.roll(value, by, 0)
    return jnp.where(rows_of(value) >= by, moved, 0.0)


def up(value, by):
    length = value.shape[0]
    moved = pltpu.roll(value, length - by, 0)
    return jnp.where(rows_of(value) < length - by, moved, 0.0)


def recur(value, powers, move):
    by = 1
    for power in powers:
        value = value + power * move(value, by)
        by *= 2
    return value


def forward_block(series, starts, history, poles, zeros, taps):
    length = series.shape[0]
    first = rows_of(series) == 0
    current, states = (series, [series[length - 1 :]])
    for section, (powers, zero) in enumerate(zip(poles, zeros)):
        before = jnp.where(first, starts[section], pltpu.roll(current, 1, 0))
        driven = current - zero * before
        driven = driven + jnp.where(first, powers[0] * starts[section + 1], 0.0)
        current = recur(driven, powers, down)
        states.append(current[length - 1 :])
    extended = jnp.concatenate([history, current], axis=0)
    reach = history.shape[0]
    filtered = taps[0] * current
    for lag in range(1, len(taps)):
        filtered = filtered + taps[lag] * pltpu.roll(extended, lag, 0)[reach:]
    for back in range(1, reach):
        states.append(current[length - 1 - back : length - back])
    return (filtered, states)


def backward_block(filtered, ends, poles, zeros, taps):
    length = filtered.shape[0]
    reach = len(taps) - 1
    border = jnp.zeros((reach, LANES), F32)
    padded = jnp.concatenate([border, filtered, border], axis=0)
    total = padded.shape[0]
    spread = taps[0] * padded
    for lag in range(1, reach + 1):
        spread = spread + taps[lag] * pltpu.roll(padded, total - lag, 0)
    history = spread[:reach]
    current = spread[reach : reach + length]
    sections = len(poles)
    rows = rows_of(current)
    if ends is not None:
        for back in range(reach):
            current = current + jnp.where(rows == length - 1 - back, ends[sections + back], 0.0)
    states = [None] * (sections + reach)
    from_later = None
    for section in reversed(range(sections)):
        value = recur(current, poles[section], up)
        current = value - zeros[section] * up(value, 1)
        if ends is not None:
            current = current + jnp.where(rows == length - 1, ends[section], 0.0)
        to_output = poles[section][0] * value[:1]
        states[section + 1] = to_output if from_later is None else to_output + from_later
        from_later = -zeros[section] * value[:1]
    states[0] = from_later
    states[sections] = states[sections] + history[reach - 1 :]
    for back in range(1, reach):
        states[sections + back] = history[reach - 1 - back : reach - back]
    return (current, states)


def pack(states):
    rows = lax.broadcasted_iota(jnp.int32, (SLOT, LANES), 0)
    packed = jnp.zeros((SLOT, LANES), F32)
    for at, state in enumerate(states):
        packed = jnp.where(rows == at, state, packed)
    return packed


def filter_kernel(sections, taps_count, parts, *refs):
    counts_ref, table_ref = refs[:2]
    gathered = refs[2 : 2 + parts]
    send_ref, keep_ref, spread_ref, steps_ref, energy_ref = refs[2 + parts :]
    length = keep_ref.shape[0]
    half = LANES // 2
    received = gathered[0][...]
    for other in gathered[1:]:
        received = received + other[...]
    energy_ref[...] = received[length:]
    received = received[:length]
    lane = lax.broadcasted_iota(jnp.int32, (1, LANES), 1)
    live = rows_of(received) < counts_ref[0]
    data = jnp.where(live & (lane < half), received, 0.0)

    table = table_ref[...]
    life = table[:sections]
    ratio = table[sections : 2 * sections]
    active = table[2 * sections : 3 * sections] > 0.5
    taps = [table[3 * sections + at :][:1] for at in range(taps_count)]
    pole_all = jnp.exp(-1.0 / life)
    pole_rate = jnp.where(active, pole_all, 0.0)
    zero_rate = jnp.where(active, 1.0 - ratio * (1.0 - pole_all), 0.0)
    poles, zeros = ([], [])
    for section in range(sections):
        power, powers, by = (pole_rate[section : section + 1], [], 1)
        while by < length:
            powers.append(power)
            power, by = (power * power, 2 * by)
        poles.append(powers)
        zeros.append(zero_rate[section : section + 1])

    reach = taps_count - 1
    kinds = sections + reach
    slot = jnp.where(lane >= half, lane % SLOT, SLOT)
    units = [jnp.where(slot == at, 1.0, 0.0) for at in range(kinds)]
    rows = lax.broadcasted_iota(jnp.int32, (reach, LANES), 0)
    history = jnp.where(slot == kinds - 1 - rows, 1.0, 0.0)
    filtered, ends = forward_block(data, units[: sections + 1], history, poles, zeros, taps)
    local, heads = backward_block(filtered, None, poles, zeros, taps)
    reply, replies = backward_block(jnp.zeros_like(filtered), units, poles, zeros, taps)
    ends, heads, replies = (pack(ends), pack(heads), pack(replies))

    low_half = lane < half
    send_ref[...] = jnp.where(low_half, ends, pltpu.roll(heads, half, 1))
    spread_ref[...] = jnp.where(low_half, pltpu.roll(local, half, 1), reply)
    full = received + pltpu.roll(received, half, 1)
    keep_ref[...] = jnp.where(low_half, local, full)
    stacked = jnp.concatenate([ends, heads, replies], axis=0)
    source = lax.broadcasted_iota(jnp.int32, (LANES, kinds * LANES), 0)
    target = lax.broadcasted_iota(jnp.int32, (LANES, kinds * LANES), 1)
    within = target % LANES
    wanted = half + within // SLOT * SLOT + target // LANES
    pick = jnp.where((within < half) & (source == wanted), 1.0, 0.0)
    steps_ref[...] = jnp.dot(stacked, pick, precision=HIGHEST, preferred_element_type=F32)


def blocks_of(value, width, padded):
    wide = value.shape[1]
    window = min(padded + LANES, wide)
    for block in range(wide // width):
        start = block * width
        base = min(start // LANES * LANES, wide - window)
        part = value[:, base : base + window]
        if start != base:
            part = pltpu.roll(part, window - (start - base), 1)
        yield part[:, :padded]


def normal_kernel(kinds, width, layout, *refs):
    place_ref, counts_ref, all_ref, keep_ref, spread_ref, steps_ref, design_ref = refs[:7]
    out_ref, entering_ref = refs[7:]
    blocks = all_ref.shape[0]
    mine = place_ref[0]
    half = LANES // 2

    def apply(which, state):
        total = None
        for at in range(kinds):
            column = steps_ref[which * SLOT : (which + 1) * SLOT, at * LANES : (at + 1) * LANES]
            term = column * state[at : at + 1]
            total = term if total is None else total + term
        return total

    def advance(block, state):
        entering_ref[block] = state
        return apply(0, state) + all_ref[block]

    def retreat(step, state):
        block = blocks - 1 - step
        later = apply(2, state) + (apply(1, entering_ref[block]) + pltpu.roll(all_ref[block], half, 1))
        return jnp.where(block > mine, later, state)

    empty = jnp.zeros((SLOT, LANES), F32)
    unroll = blocks if blocks <= 16 else 4
    lax.fori_loop(0, blocks, advance, empty, unroll=unroll)
    leaving = lax.fori_loop(0, blocks, retreat, empty, unroll=unroll)
    entering = entering_ref[mine]

    groups = half // SLOT
    row = lax.broadcasted_iota(jnp.int32, (half, LANES), 0)
    lane = lax.broadcasted_iota(jnp.int32, (half, LANES), 1)
    own = row // SLOT == lane // SLOT
    expanded = [
        jnp.where(own, jnp.concatenate([state] * groups, axis=0), 0.0)
        for state in (entering, leaving)
    ]
    correction = jnp.dot(
        spread_ref[...],
        jnp.concatenate(expanded, axis=0),
        precision=HIGHEST,
        preferred_element_type=F32,
    )
    kept = keep_ref[...]
    live = rows_of(kept) < counts_ref[0]
    weighted = jnp.where(live & (lane < half), kept + correction, 0.0)
    weighted = weighted.astype(BF16).astype(F32)
    product = weighted * pltpu.roll(kept, half, 1)
    turned = jnp.transpose(weighted)
    count = out_ref.shape[-2]
    low = jnp.concatenate(
        [turned[at * count : (at + 1) * count] for at in range(half // count)], axis=1
    ).astype(BF16)
    curve = lax.dot_general(
        product,
        jnp.ones((product.shape[0], LANES), F32),
        (((0,), (0,)), ((), ())),
        precision=HIGHEST,
        preferred_element_type=F32,
    )
    curvature = curve[:count]
    for at in range(1, half // count):
        curvature = curvature + curve[at * count : (at + 1) * count]
    normal = jnp.dot(low, design_ref[...], preferred_element_type=F32)
    padded = out_ref.shape[-1]
    column = lax.broadcasted_iota(jnp.int32, (count, padded), 1)
    curvature = jnp.broadcast_to(curvature[:, :1], (count, padded))
    for block, part in enumerate(blocks_of(normal, width, padded)):
        out_ref[layout(block)] = jnp.where(column < width, part, curvature)


def slices_kernel(width, first_bits, place_ref, *refs):
    count = len(refs) // 2
    mine = place_ref[0]
    low = mine % first_bits
    for source_ref, target_ref in zip(refs[:count], refs[count:]):
        wide = source_ref.shape[-1]
        padded = target_ref.shape[-1]
        window = min(padded + LANES, wide)
        for at in range(target_ref.shape[0]):
            block = at * first_bits + low if target_ref.shape[0] > 1 else mine
            start = block * width
            base = jnp.minimum(start // LANES * LANES, wide - window)
            part = source_ref[:, pl.ds(pl.multiple_of(base, LANES), window)]
            part = jnp.broadcast_to(part, (target_ref.shape[1], window))
            moved = pltpu.roll(part, (window - (start - base)) % window, 1)
            target_ref[at] = moved[:, :padded]


def update_kernel(width, first_bits, *refs):
    place_ref, held_ref, got_ref, energy_ref = refs[:4]
    remaining_ref, diagonal_ref, current_ref, search_ref = refs[4:8]
    next_ref, new_solution_ref, new_residual_ref, conditioned_ref, entering_ref = refs[8:]
    parts, count, padded = held_ref.shape
    column = lax.broadcasted_iota(jnp.int32, (count, padded), 1)
    at_curve = column == width
    normal = held_ref[0] + got_ref[0]
    curvature = jnp.sum(jnp.where(at_curve, normal, 0.0), axis=1, keepdims=True)
    step = energy_ref[:, :1] / curvature
    total = jnp.zeros((count, padded), F32)
    for at in range(parts):
        normal = held_ref[at] + got_ref[at]
        changed = remaining_ref[at] - step * normal
        scaled = diagonal_ref[at] * changed
        entering_ref[at] = changed
        total = total + jnp.where(column < width, changed * scaled, 0.0)
    share = jnp.sum(total, axis=1, keepdims=True)
    next_ref[...] = jnp.broadcast_to(share, next_ref.shape)
    own = place_ref[0] // first_bits
    changed = entering_ref[own]
    new_residual_ref[...] = changed
    conditioned_ref[...] = diagonal_ref[own] * changed
    new_solution_ref[...] = current_ref[0] + step * search_ref[0]


def exchange(value, axis, bit):
    size = lax.axis_size(axis)
    return lax.ppermute(value, axis, [(at, at ^ bit) for at in range(size)])


def over_order(value):
    if lax.axis_size("order") == 2:
        return [value, exchange(value, "order", 1)]
    return [lax.psum(value, "order")]


def shards(
    solution,
    residual,
    direction,
    precond,
    design,
    epoch_counts,
    segment_orders,
    pole_life,
    zero_ratio,
    fir_taps,
):
    count, _, wide = direction.shape
    components, length = design.shape[:2]
    sections = pole_life.shape[1] * pole_life.shape[2]
    taps_count = fir_taps.shape[1]
    kinds = sections + taps_count - 1
    blocks = lax.axis_size("tm")
    width = wide // blocks
    padded = (width // LANES + 1) * LANES
    bits = blocks.bit_length() - 1
    halved = bits // 2
    classes = 1 << halved
    parts = blocks // classes
    place = lax.axis_index("tm").astype(jnp.int32).reshape(1)
    design_rows = design.reshape(components * length, wide)
    search = direction[:, 0, :]
    remaining = residual[:, 0, :]

    predicted = call(
        predict_kernel, shape(length + count, LANES), search, remaining, precond, design_rows
    )
    arrived = over_order(predicted)

    active = jnp.arange(pole_life.shape[2])[None, None, :] < segment_orders[:, :, None]
    columns = jnp.concatenate(
        [
            pole_life.reshape(components, -1),
            zero_ratio.reshape(components, -1),
            active.astype(F32).reshape(components, -1),
            fir_taps,
        ],
        axis=1,
    )
    table = jnp.broadcast_to(
        columns.T[:, None, :, None], (columns.shape[1], 2, components, count)
    ).reshape(columns.shape[1], LANES)

    send, keep, spread, steps, energy = call(
        functools.partial(filter_kernel, sections, taps_count, len(arrived)),
        (
            shape(SLOT, LANES),
            shape(length, LANES),
            shape(length, LANES),
            shape(3 * SLOT, kinds * LANES),
            shape(count, LANES),
        ),
        epoch_counts,
        table,
        *arrived,
        specs=[smem()] + [vmem()] * (1 + len(arrived)),
    )
    everyone = lax.all_to_all(jnp.broadcast_to(send, (blocks, SLOT, LANES)), "tm", 0, 0)

    def layout(block):
        low = [block >> bit & 1 for bit in range(halved)]
        return (*low, block >> halved)

    buffer = call(
        functools.partial(normal_kernel, kinds, width, layout),
        shape(*(2,) * halved, parts, count, padded),
        place,
        epoch_counts,
        everyone,
        keep,
        spread,
        steps,
        design_rows,
        specs=[smem()] * 2 + [vmem()] * 5,
        scratch=[pltpu.VMEM((blocks, SLOT, LANES), F32)],
    )
    diagonal_parts, remaining_parts, search_own, current_own = call(
        functools.partial(slices_kernel, width, classes),
        (
            shape(parts, count, padded),
            shape(parts, count, padded),
            shape(1, count, padded),
            shape(1, count, padded),
        ),
        place,
        precond,
        remaining,
        search,
        solution[:, 0, :],
        specs=[smem()] + [vmem()] * 4,
    )
    for bit in range(halved):
        side = place[0] >> bit & 1
        mine = lax.dynamic_index_in_dim(buffer, side, 0, False)
        other = lax.dynamic_index_in_dim(buffer, 1 - side, 0, False)
        buffer = mine + exchange(other, "tm", 1 << bit)
    for bit in range(halved, bits - 1):
        buffer = buffer + exchange(buffer, "tm", 1 << bit)
    arriving = exchange(buffer, "tm", 1 << bits - 1)
    share, new_solution, new_residual, conditioned = call(
        functools.partial(update_kernel, width, classes),
        (
            shape(count, LANES),
            shape(count, padded),
            shape(count, padded),
            shape(count, padded),
        ),
        place,
        buffer,
        arriving,
        energy,
        remaining_parts,
        diagonal_parts,
        current_own,
        search_own,
        specs=[smem()] + [vmem()] * 7,
        scratch=[pltpu.VMEM((parts, count, padded), F32)],
    )
    for bit in range(halved):
        share = share + exchange(share, "tm", 1 << bit)
    energy_next = sum(over_order(share))
    new_direction = conditioned + (energy_next / energy)[:, :1] * search_own[0]
    return tuple(
        vector[:, None, :width] for vector in (new_solution, new_residual, new_direction)
    )


def solution(mesh):
    placed = (
        P(None, "order", None),
        P(None, "order", None),
        P(None, "order", None),
        P("order", None),
        P(None, "tm", "order", None),
        P("tm"),
        P(),
        P(),
        P(),
        P(),
    )
    return jax.shard_map(
        shards,
        mesh=mesh,
        in_specs=placed,
        out_specs=(P(None, "order", "tm"), P(None, "order", "tm"), P(None, "order", "tm")),
        check_vma=False,
    )
```

time: 368 us -> 64.8 us (0.18); the launches traced: 362 us -> 64.2 us
  blocking collectives: 134 us -> 0 us
  waiting for transfers between devices: 104 us -> 31.9 us
  matrix products: 42.8 us -> 0 us
  local copies, waits for them, and re-layouts: 51.3 us -> 13.1 us
  between operations: 15 us -> 1.48 us
  other arithmetic: 9.58 us -> 1.32 us
  starting transfers between devices: 5.12 us -> 12.5 us
  Pallas kernels: 0 us -> 3.92 us
    all_gather x3 -> x0, blocking collectives: 125 us -> none  [prefix(): pieces = jax.tree.map(lambda part: lax.all_gather(part, axis), value)]
    psum x1 -> x0, waiting for transfers between devices: 100 us -> none  [shards(): normal = lax.psum(partial_normal, 'tm')]
    dot_general x49 -> x0, matrix products: 42.8 us -> none  [the longest x30 26.3 us: compose(): jnp.einsum('ckm,cmb->ckb', second_map, first_end, precision=HIGHEST)]
    squeeze x30 -> x2, local copies, waits for them, and re-layouts: 21.3 us -> 0.03 us  [shards(): other = lax.dynamic_index_in_dim(buffer, 1 - side, 0, False)]
    ppermute x2 -> x8, waiting for transfers between devices: 3.16 us -> 23.8 us  [exchange(): return lax.ppermute(value, axis, [(at, at ^ bit) for at in range(size)])]
    slice x17 -> x0, local copies, waits for them, and re-layouts: 9.82 us -> none  [the longest x12 7.06 us: local_cascade(): ends.append(output[:, :, length - 1])]
    psum x3 -> x0, blocking collectives: 8.61 us -> none  [the longest x2 4.93 us: order_sums(): return lax.psum(values, 'order')]
    all_to_all x0 -> x1, waiting for transfers between devices: none -> 8.08 us  [shards(): lax.all_to_all(jnp.broadcast_to(send, (blocks, SLOT, LANES)), 'tm', 0, 0)]
  transfers between devices with their start and end apart: 3 -> 9, of which waited for: 3 -> 7; matrix products, arithmetic and copies ran while one was open for 2% -> 7% of each run, Pallas kernels for 0% -> 0%
where the time goes in v1:
time: 64.8 us; the launch traced here: 64.2 us
  waiting for transfers between devices  31.9 us (49%)
  local copies, waits for them, and re-layouts  13.1 us (20%)
  starting transfers between devices  12.5 us (19%)
  Pallas kernels  3.92 us (6%)
  between operations  1.48 us (2%)
  other arithmetic  1.32 us (2%)
    ppermute x8, waiting for transfers between devices, exchange(): return lax.ppermute(value, axis, [(at, at ^ bit) for at in range(size)])  23.8 us
    unnamed x31, local copies, waits for them, and re-layouts  10.2 us
    all_to_all x1, waiting for transfers between devices, shards(): lax.all_to_all(jnp.broadcast_to(send, (blocks, SLOT, LANES)), 'tm', 0, 0)  8.08 us
    all_to_all x1, starting transfers between devices, shards(): lax.all_to_all(jnp.broadcast_to(send, (blocks, SLOT, LANES)), 'tm', 0, 0)  7.87 us
    ppermute x8, starting transfers between devices, exchange(): return lax.ppermute(value, axis, [(at, at ^ bit) for at in range(size)])  4.62 us
    pallas_call x5, Pallas kernels, call(): pl.pallas_call(kernel, out_shape=outs, in_specs=specs or [vmem()] * len(a...  3.92 us
  transfers between devices with their start and end apart: 9, of which 7 were waited for; matrix products, arithmetic and copies ran while one was open for 7% of the time, Pallas kernels for 0%

profile of v1, /device:TPU:0, one launch (start us, length us, event | category | flops | bytes accessed | tf_op | source)
XLA Modules:
  0.0 64.2 jit_solution(9363283177930148866)
XLA Ops:
  0.7 1.2 %copy_bitcast_fusion.1 = (f32[16,5760]{1,0:T(8,128)S(1)}, f32[16,5760]{1,0:T(8,128)S(1)}) fusion(f32[16,1,5760]{2,1,0:T(1,128)} %param.11, f32[16,1,5760]{2,1,0:T(1,128)} %param.12), kind=kLoop, calls=%fused_computation.1 | loop fusion | bytes 1474560
  1.9 0.0 copy-start
  1.9 2.0 %copy-done = bf16[4,64,1,5760]{3,1,2,0:T(8,128)(2,1)S(1)} copy-done((bf16[4,64,1,5760]{3,1,2,0:T(8,128)(2,1)S(1)}, bf16[4,64,1,5760]{3,1,2,0:T(8,128)(2,1)}, u32[]{:S(2)}) %copy-start) | copy-done | bytes 2949144
  3.8 0.7 %copy-done.7 = f32[1,5760]{1,0:T(1,128)S(1)} copy-done((f32[1,5760]{1,0:T(1,128)S(1)}, f32[1,5760]{1,0:T(1,128)}, u32[]{:S(2)}) %copy-start.7) | copy-done | bytes 23064
  4.6 1.1 %shard_map.121.refs_2_ = f32[80,128]{1,0:T(8,128)S(1)} custom-call(f32[16,5760]{1,0:T(8,128)S(1)} %get-tuple-element.36.direction_ref.refs_2_, f32[16,5760]{1,0:T(8,128)S(1)} %get-tuple-element.35.residual_ref.refs_1_, f32[1,5760]{1,0:T(1,128)S(1)} %copy-done.7, bf16[256,5760]{1,0:T(8,128)(2,1)S(1)} %bitcast.29), custom_call_target="tpu_custom_call" | custom-call | tf_op jit(solution)/shard_map/pallas_call | solution.py:27
  5.6 0.5 collective-permute-start
  6.2 0.1 lt.35
  6.2 0.1 compare_convert_fusion
  6.3 0.1 copy.22
  6.4 0.1 copy.20
  6.5 0.1 copy.21
  6.6 0.1 maximum_bitcast_fusion
  7.3 0.1 copy.23
  7.4 0.7 %broadcast_in_dim.20 = f32[21,2,4,16]{3,2,1,0:T(4,128)} broadcast(f32[21,4]{1,0:T(8,128)S(1)} %copy.23), dimensions={0,2} | broadcast | bytes 11088 | tf_op jit(solution)/shard_map/broadcast_in_dim | solution.py:386
  8.2 1.0 %reshape.29.refs_1_ = f32[21,128]{1,0:T(8,128)S(1)} reshape(f32[21,2,4,16]{3,2,1,0:T(4,128)} %broadcast_in_dim.20) | data formatting | bytes 21504 | tf_op jit(solution)/shard_map/reshape | solution.py:388
  9.2 0.0 collective-permute-done.refs_3_
  9.2 1.0 %shard_map.122 = (f32[16,128]{1,0:T(8,128)S(1)}, f32[64,128]{1,0:T(8,128)S(1)}, f32[64,128]{1,0:T(8,128)S(1)}, f32[48,1536]{1,0:T(8,128)S(1)}, f32[16,128]{1,0:T(8,128)S(1)}) custom-call(s32[1]{0:T(128)S(6)} %copy.34.refs_0_.refs_1_, f32[21,128]{1,0:T(8,128)S(1)} %reshape.29.refs_1_, f32[80,128]{1,0:T(8,128)S(1)} %shard_map.121.refs_2_, ...), custom_call_target="tpu_custom_call" | custom-call | tf_op jit(solution)/shard_map/pallas_call | solution.py:27
  10.2 0.7 %copy-done.5 = f32[48,1536]{1,0:T(8,128)} copy-done((f32[48,1536]{1,0:T(8,128)}, f32[48,1536]{1,0:T(8,128)S(1)}, u32[]{:S(2)}) %copy-start.5) | copy-done | bytes 294936
  10.9 0.7 %broadcast_in_dim.21 = f32[16,16,128]{2,1,0:T(8,128)} broadcast(f32[16,128]{1,0:T(8,128)S(1)} %get-tuple-element.16), dimensions={1,2} | broadcast | bytes 139264 | tf_op jit(solution)/shard_map/broadcast_in_dim | solution.py:404
  11.5 7.9 %all-to-all-start = ((f32[16,16,128]{2,1,0:T(8,128)}), f32[16,16,128]{2,1,0:T(8,128)S(1)}, u32[]{:S(2)}, u32[]{:S(2)}) async-start(f32[16,16,128]{2,1,0:T(8,128)} %broadcast_in_dim.21), calls=%async_computation | async-start | bytes 262144 | tf_op jit(solution)/shard_map/all_to_all | solution.py:404
  19.4 8.1 %all-to-all-done.refs_2_ = f32[16,16,128]{2,1,0:T(8,128)S(1)} async-done(((f32[16,16,128]{2,1,0:T(8,128)}), f32[16,16,128]{2,1,0:T(8,128)S(1)}, u32[]{:S(2)}, u32[]{:S(2)}) %all-to-all-start) | async-done | bytes 131104 | tf_op jit(solution)/shard_map/all_to_all | solution.py:404
  27.5 1.0 %copy-done.6 = f32[48,1536]{1,0:T(8,128)S(1)} copy-done((f32[48,1536]{1,0:T(8,128)S(1)}, f32[48,1536]{1,0:T(8,128)}, u32[]{:S(2)}) %copy-start.6) | copy-done | bytes 294936
  28.5 1.5 %shard_map.123 = f32[2,2,4,16,384]{4,3,2,1,0:T(8,128)S(1)} custom-call(s32[1]{0:T(128)} %bitcast.refs_0_.place_ref, s32[1]{0:T(128)S(6)} %copy.34.refs_0_.refs_1_, f32[16,16,128]{2,1,0:T(8,128)S(1)} %all-to-all-done.refs_2_, f32[64,128]{1,0:T(8,128)S(1)} %get-tuple-element.17.refs_3_, f32[64,128]{1,0:T(8,128)S(1)} %get-tuple-element.18.refs_4_, ...), custom_call_target="tpu_custom_call" | custom-call | tf_op jit(solution)/shard_map/pallas_call | solution.py:27
  30.0 0.7 %copy-done.4 = f32[2,2,4,16,384]{4,3,2,1,0:T(8,128)} copy-done((f32[2,2,4,16,384]{4,3,2,1,0:T(8,128)}, f32[2,2,4,16,384]{4,3,2,1,0:T(8,128)S(1)}, u32[]{:S(2)}) %copy-start.4) | copy-done | bytes 393240
  30.7 1.2 %collective-permute-start.1 = (f32[2,4,16,384]{3,2,1,0:T(8,128)S(1)}, f32[2,4,16,384]{3,2,1,0:T(8,128)S(1)}, u32[]{:S(2)}, u32[]{:S(2)}) collective-permute-start(f32[2,4,16,384]{3,2,1,0:T(8,128)S(1)} %dynamic-slice_bitcast_fusion), channel_id=1, source_target_pairs={{0,2},{2,0},{4,6},{6,4},{8,10},{10,8},{12,14},{14,12},{16,18},{18,... | collective-permute-start | bytes 589832 | tf_op jit(solution)/shard_map/ppermute | solution.py:333
  31.9 4.6 %collective-permute-done.1 = f32[2,4,16,384]{3,2,1,0:T(8,128)S(1)} collective-permute-done((f32[2,4,16,384]{3,2,1,0:T(8,128)S(1)}, f32[2,4,16,384]{3,2,1,0:T(8,128)S(1)}, u32[]{:S(2)}, u32[]{:S(2)}) %collective-permute-start.1) | collective-permute-done | bytes 196640 | tf_op jit(solution)/shard_map/ppermute | solution.py:333
  36.5 0.9 %bitcast_add_fusion = f32[2,4,16,384]{3,2,1,0:T(8,128)S(1)} fusion(f32[2,4,16,384]{3,2,1,0:T(8,128)S(1)} %collective-permute-done.1, f32[2,2,4,16,384]{4,3,2,1,0:T(8,128)} %copy-done.4, s32[]{:T(128)S(6)} %select_n.14), kind=kLoop, calls=%fused_computation.3 | loop fusion | flops 49152 | bytes 589828 | tf_op jit(solution)/shard_map/add | solution.py:442
  37.4 0.8 %collective-permute-start.2 = (f32[4,16,384]{2,1,0:T(8,128)S(1)}, f32[4,16,384]{2,1,0:T(8,128)S(1)}, u32[]{:S(2)}, u32[]{:S(2)}) collective-permute-start(f32[4,16,384]{2,1,0:T(8,128)S(1)} %dynamic-slice_bitcast_fusion.1), channel_id=1, source_target_pairs={{0,4},{2,6},{4,0},{6,2},{8,12},{10,14},{12,8},{14,10},{16,20},{18,... | collective-permute-start | bytes 294920 | tf_op jit(solution)/shard_map/ppermute | solution.py:333
  38.2 3.9 %collective-permute-done.2 = f32[4,16,384]{2,1,0:T(8,128)S(1)} collective-permute-done((f32[4,16,384]{2,1,0:T(8,128)S(1)}, f32[4,16,384]{2,1,0:T(8,128)S(1)}, u32[]{:S(2)}, u32[]{:S(2)}) %collective-permute-start.2) | collective-permute-done | bytes 98336 | tf_op jit(solution)/shard_map/ppermute | solution.py:333
  42.1 0.8 %collective-permute-start.3 = (f32[4,16,384]{2,1,0:T(8,128)S(1)}, f32[4,16,384]{2,1,0:T(8,128)S(1)}, u32[]{:S(2)}, u32[]{:S(2)}) collective-permute-start(f32[4,16,384]{2,1,0:T(8,128)S(1)} %bitcast_add_fusion.1), channel_id=1, source_target_pairs={{0,8},{2,10},{4,12},{6,14},{8,0},{10,2},{12,4},{14,6},{16,24},{18,... | collective-permute-start | bytes 294920 | tf_op jit(solution)/shard_map/ppermute | solution.py:333
  42.9 4.9 %collective-permute-done.3 = f32[4,16,384]{2,1,0:T(8,128)S(1)} collective-permute-done((f32[4,16,384]{2,1,0:T(8,128)S(1)}, f32[4,16,384]{2,1,0:T(8,128)S(1)}, u32[]{:S(2)}, u32[]{:S(2)}) %collective-permute-start.3) | collective-permute-done | bytes 98336 | tf_op jit(solution)/shard_map/ppermute | solution.py:333
  47.9 1.0 %collective-permute-start.4 = (f32[4,16,384]{2,1,0:T(8,128)S(1)}, f32[4,16,384]{2,1,0:T(8,128)S(1)}, u32[]{:S(2)}, u32[]{:S(2)}) collective-permute-start(f32[4,16,384]{2,1,0:T(8,128)S(1)} %add.43.refs_1_), channel_id=1, source_target_pairs={{0,16},{2,18},{4,20},{6,22},{8,24},{10,26},{12,28},{14,30},{16,0},... | collective-permute-start | bytes 294920 | tf_op jit(solution)/shard_map/ppermute | solution.py:333
  48.8 1.0 %copy.33 = f32[16,1,5760]{2,0,1:T(8,128)S(1)} copy(f32[16,1,5760]{2,1,0:T(1,128)} %param.10) | data formatting | bytes 737280
  49.9 1.0 %copy-done.3 = f32[16,5760]{1,0:T(8,128)S(1)} copy-done((f32[16,5760]{1,0:T(8,128)S(1)}, f32[16,5760]{1,0:T(8,128)}, u32[]{:S(2)}) %copy-start.3) | copy-done | bytes 368664
  50.9 0.1 shard_map.124
  51.0 3.5 %collective-permute-done.4.refs_2_ = f32[4,16,384]{2,1,0:T(8,128)S(1)} collective-permute-done((f32[4,16,384]{2,1,0:T(8,128)S(1)}, f32[4,16,384]{2,1,0:T(8,128)S(1)}, u32[]{:S(2)}, u32[]{:S(2)}) %collective-permute-start.4) | collective-permute-done | bytes 98336 | tf_op jit(solution)/shard_map/ppermute | solution.py:333
  54.5 0.3 shard_map.125
  54.8 0.0 collective-permute-start.5
  54.8 3.6 %collective-permute-done.5 = f32[16,128]{1,0:T(8,128)S(1)} collective-permute-done((f32[16,128]{1,0:T(8,128)S(1)}, f32[16,128]{1,0:T(8,128)S(1)}, u32[]{:S(2)}, u32[]{:S(2)}) %collective-permute-start.5) | collective-permute-done | bytes 8224 | tf_op jit(solution)/shard_map/ppermute | solution.py:333
  58.4 0.4 collective-permute-start.6
  58.8 3.3 %collective-permute-done.6 = f32[16,128]{1,0:T(8,128)S(1)} collective-permute-done((f32[16,128]{1,0:T(8,128)S(1)}, f32[16,128]{1,0:T(8,128)S(1)}, u32[]{:S(2)}, u32[]{:S(2)}) %collective-permute-start.6) | collective-permute-done | bytes 8224 | tf_op jit(solution)/shard_map/ppermute | solution.py:333
  62.1 0.0 collective-permute-start.7
  62.1 0.6 copy.24
  62.7 0.6 copy.25
  63.4 0.0 collective-permute-done.7
  63.4 0.1 fusion.1
  63.5 0.1 fusion
  63.6 0.6 %copy.26 = f32[16,1,360]{2,1,0:T(1,128)} copy(f32[16,1,360]{2,0,1:T(8,128)S(1)} %fusion) | data formatting | bytes 46080
  (29 shorter events, 0.1 us)
Async XLA Ops:
  0.6 5.6 %copy-start.12 = (s32[4,2]{0,1:T(2,128)S(1)}, s32[4,2]{0,1:T(2,128)}, u32[]{:S(2)}) copy-start(s32[4,2]{0,1:T(2,128)} %param.16) | copy-start | bytes 100
  0.6 5.8 %copy-start.10 = (f32[4,2,2]{0,2,1:T(2,128)S(1)}, f32[4,2,2]{0,2,1:T(2,128)}, u32[]{:S(2)}) copy-start(f32[4,2,2]{0,2,1:T(2,128)} %param.17) | copy-start | bytes 196
  0.7 5.9 %copy-start.11 = (f32[4,2,2]{0,2,1:T(2,128)S(1)}, f32[4,2,2]{0,2,1:T(2,128)}, u32[]{:S(2)}) copy-start(f32[4,2,2]{0,2,1:T(2,128)} %param.18) | copy-start | bytes 196
  0.7 5.9 %copy-start.9 = (f32[4,9]{1,0:T(4,128)S(1)}, f32[4,9]{1,0:T(4,128)}, u32[]{:S(2)}) copy-start(f32[4,9]{1,0:T(4,128)} %param.19) | copy-start | bytes 436
  1.8 3.8 %copy-start.2 = (f32[16,5760]{1,0:T(8,128)}, f32[16,5760]{1,0:T(8,128)S(1)}, u32[]{:S(2)}) copy-start(f32[16,5760]{1,0:T(8,128)S(1)} %get-tuple-element.36.direction_ref.refs_2_) | copy-start | bytes 1105924
  1.9 2.0 %copy-start = (bf16[4,64,1,5760]{3,1,2,0:T(8,128)(2,1)S(1)}, bf16[4,64,1,5760]{3,1,2,0:T(8,128)(2,1)}, u32[]{:S(2)}) copy-start(bf16[4,64,1,5760]{3,1,2,0:T(8,128)(2,1)} %param.14) | copy-start | bytes 8847364
  3.8 0.7 %copy-start.7 = (f32[1,5760]{1,0:T(1,128)S(1)}, f32[1,5760]{1,0:T(1,128)}, u32[]{:S(2)}) copy-start(f32[1,5760]{1,0:T(1,128)} %refs_0_.2) | copy-start | bytes 69124
  4.6 22.9 %copy-start.1 = (bf16[4,64,1,5760]{3,1,2,0:T(8,128)(2,1)S(1)}, bf16[4,64,1,5760]{3,1,2,0:T(8,128)(2,1)}, u32[]{:S(2)}) copy-start(bf16[4,64,1,5760]{3,1,2,0:T(8,128)(2,1)} %param.14) | copy-start | bytes 8847364
  5.6 3.5 %collective-permute-start = (f32[80,128]{1,0:T(8,128)S(1)}, f32[80,128]{1,0:T(8,128)S(1)}, u32[]{:S(2)}, u32[]{:S(2)}) collective-permute-start(f32[80,128]{1,0:T(8,128)S(1)} %shard_map.121.refs_2_), channel_id=1, source_target_pairs={{0,1},{1,0},{2,3},{3,2},{4,5},{5,4},{6,7},{7,6},{8,9},{9,8},{10,11... | collective-permute-start | bytes 122888 | tf_op jit(solution)/shard_map/ppermute | solution.py:333
  10.1 0.7 %copy-start.5 = (f32[48,1536]{1,0:T(8,128)}, f32[48,1536]{1,0:T(8,128)S(1)}, u32[]{:S(2)}) copy-start(f32[48,1536]{1,0:T(8,128)S(1)} %get-tuple-element.19.refs_5_) | copy-start | bytes 884740
  11.5 16.0 %all-to-all-start = ((f32[16,16,128]{2,1,0:T(8,128)}), f32[16,16,128]{2,1,0:T(8,128)S(1)}, u32[]{:S(2)}, u32[]{:S(2)}) async-start(f32[16,16,128]{2,1,0:T(8,128)} %broadcast_in_dim.21), calls=%async_computation | async-start | bytes 262144 | tf_op jit(solution)/shard_map/all_to_all | solution.py:404
  27.5 1.0 %copy-start.6 = (f32[48,1536]{1,0:T(8,128)S(1)}, f32[48,1536]{1,0:T(8,128)}, u32[]{:S(2)}) copy-start(f32[48,1536]{1,0:T(8,128)} %copy-done.5) | copy-start | bytes 884740
  28.4 21.4 %copy-start.8 = (f32[1,5760]{1,0:T(1,128)S(1)}, f32[1,5760]{1,0:T(1,128)}, u32[]{:S(2)}) copy-start(f32[1,5760]{1,0:T(1,128)} %refs_0_.2) | copy-start | bytes 69124
  29.9 0.8 %copy-start.4 = (f32[2,2,4,16,384]{4,3,2,1,0:T(8,128)}, f32[2,2,4,16,384]{4,3,2,1,0:T(8,128)S(1)}, u32[]{:S(2)}) copy-start(f32[2,2,4,16,384]{4,3,2,1,0:T(8,128)S(1)} %shard_map.123) | copy-start | bytes 1179652
  30.7 5.7 %collective-permute-start.1 = (f32[2,4,16,384]{3,2,1,0:T(8,128)S(1)}, f32[2,4,16,384]{3,2,1,0:T(8,128)S(1)}, u32[]{:S(2)}, u32[]{:S(2)}) collective-permute-start(f32[2,4,16,384]{3,2,1,0:T(8,128)S(1)} %dynamic-slice_bitcast_fusion), channel_id=1, source_target_pairs={{0,2},{2,0},{4,6},{6,4},{8,10},{10,8},{12,14},{14,12},{16,18},{18,... | collective-permute-start | bytes 589832 | tf_op jit(solution)/shard_map/ppermute | solution.py:333
  37.4 4.7 %collective-permute-start.2 = (f32[4,16,384]{2,1,0:T(8,128)S(1)}, f32[4,16,384]{2,1,0:T(8,128)S(1)}, u32[]{:S(2)}, u32[]{:S(2)}) collective-permute-start(f32[4,16,384]{2,1,0:T(8,128)S(1)} %dynamic-slice_bitcast_fusion.1), channel_id=1, source_target_pairs={{0,4},{2,6},{4,0},{6,2},{8,12},{10,14},{12,8},{14,10},{16,20},{18,... | collective-permute-start | bytes 294920 | tf_op jit(solution)/shard_map/ppermute | solution.py:333
  42.1 5.7 %collective-permute-start.3 = (f32[4,16,384]{2,1,0:T(8,128)S(1)}, f32[4,16,384]{2,1,0:T(8,128)S(1)}, u32[]{:S(2)}, u32[]{:S(2)}) collective-permute-start(f32[4,16,384]{2,1,0:T(8,128)S(1)} %bitcast_add_fusion.1), channel_id=1, source_target_pairs={{0,8},{2,10},{4,12},{6,14},{8,0},{10,2},{12,4},{14,6},{16,24},{18,... | collective-permute-start | bytes 294920 | tf_op jit(solution)/shard_map/ppermute | solution.py:333
  47.9 6.6 %collective-permute-start.4 = (f32[4,16,384]{2,1,0:T(8,128)S(1)}, f32[4,16,384]{2,1,0:T(8,128)S(1)}, u32[]{:S(2)}, u32[]{:S(2)}) collective-permute-start(f32[4,16,384]{2,1,0:T(8,128)S(1)} %add.43.refs_1_), channel_id=1, source_target_pairs={{0,16},{2,18},{4,20},{6,22},{8,24},{10,26},{12,28},{14,30},{16,0},... | collective-permute-start | bytes 294920 | tf_op jit(solution)/shard_map/ppermute | solution.py:333
  49.9 1.0 %copy-start.3 = (f32[16,5760]{1,0:T(8,128)S(1)}, f32[16,5760]{1,0:T(8,128)}, u32[]{:S(2)}) copy-start(f32[16,5760]{1,0:T(8,128)} %copy-done.2) | copy-start | bytes 1105924
  54.8 3.7 %collective-permute-start.5 = (f32[16,128]{1,0:T(8,128)S(1)}, f32[16,128]{1,0:T(8,128)S(1)}, u32[]{:S(2)}, u32[]{:S(2)}) collective-permute-start(f32[16,128]{1,0:T(8,128)S(1)} %get-tuple-element.28), channel_id=1, source_target_pairs={{0,2},{2,0},{4,6},{6,4},{8,10},{10,8},{12,14},{14,12},{16,18},{18,... | collective-permute-start | bytes 24584 | tf_op jit(solution)/shard_map/ppermute | solution.py:333
  58.4 3.7 %collective-permute-start.6 = (f32[16,128]{1,0:T(8,128)S(1)}, f32[16,128]{1,0:T(8,128)S(1)}, u32[]{:S(2)}, u32[]{:S(2)}) collective-permute-start(f32[16,128]{1,0:T(8,128)S(1)} %add.44), channel_id=1, source_target_pairs={{0,4},{2,6},{4,0},{6,2},{8,12},{10,14},{12,8},{14,10},{16,20},{18,... | collective-permute-start | bytes 24584 | tf_op jit(solution)/shard_map/ppermute | solution.py:333
  62.1 1.3 %collective-permute-start.7 = (f32[16,128]{1,0:T(8,128)S(1)}, f32[16,128]{1,0:T(8,128)S(1)}, u32[]{:S(2)}, u32[]{:S(2)}) collective-permute-start(f32[16,128]{1,0:T(8,128)S(1)} %add.45), channel_id=1, source_target_pairs={{0,1},{1,0},{2,3},{3,2},{4,5},{5,4},{6,7},{7,6},{8,9},{9,8},{10,11... | collective-permute-start | bytes 24584 | tf_op jit(solution)/shard_map/ppermute | solution.py:333

commit v2 on v1

--- a/solution.py
+++ b/solution.py
@@ -12,7 +12,7 @@
 BF16 = jnp.bfloat16
 LANES = 128
 SLOT = 16
-VMEM_LIMIT = 48 * 1024 * 1024
+VMEM_LIMIT = 16 * 1024 * 1024
 
 
 def vmem():
@@ -38,25 +38,17 @@
     return jax.ShapeDtypeStruct(dims, F32)
 
 
-def predict_kernel(direction_ref, residual_ref, precond_ref, design_ref, out_ref):
-    search = direction_ref[...]
-    high = search.astype(BF16)
-    rest = search - high.astype(F32)
-    middle = rest.astype(BF16)
-    low = (rest - middle.astype(F32)).astype(BF16)
-    stacked = jnp.concatenate([high, middle, low], axis=0)
-    count = search.shape[0]
+def predict_kernel(stacked_ref, energy_ref, design_ref, out_ref):
+    count = stacked_ref.shape[0] // 3
     sums = lax.dot_general(
-        design_ref[...], stacked, (((1,), (1,)), ((), ())), preferred_element_type=F32
+        design_ref[...], stacked_ref[...], (((1,), (1,)), ((), ())), preferred_element_type=F32
     )
     length = sums.shape[0] * count // (LANES // 2)
     pieces = [sums[start : start + length] for start in range(0, sums.shape[0], length)]
     coarse = [piece[:, :count] for piece in pieces]
     fine = [piece[:, count : 2 * count] + piece[:, 2 * count :] for piece in pieces]
     out_ref[:length, :] = jnp.concatenate(coarse + fine, axis=1)
-    remaining = residual_ref[...]
-    energy = jnp.sum(remaining * precond_ref[...] * remaining, axis=1, keepdims=True)
-    out_ref[length:, :] = jnp.broadcast_to(energy, (count, LANES))
+    out_ref[length:, :] = energy_ref[...]
 
 
 def rows_of(value):
@@ -87,13 +79,16 @@
     first = rows_of(series) == 0
     current, states = (series, [series[length - 1 :]])
     for section, (powers, zero) in enumerate(zip(poles, zeros)):
-        before = jnp.where(first, starts[section], pltpu.roll(current, 1, 0))
-        driven = current - zero * before
-        driven = driven + jnp.where(first, powers[0] * starts[section + 1], 0.0)
+        if starts is None:
+            driven = current - zero * down(current, 1)
+        else:
+            before = jnp.where(first, starts[section], pltpu.roll(current, 1, 0))
+            driven = current - zero * before
+            driven = driven + jnp.where(first, powers[0] * starts[section + 1], 0.0)
         current = recur(driven, powers, down)
         states.append(current[length - 1 :])
+    reach = history.shape[0]
     extended = jnp.concatenate([history, current], axis=0)
-    reach = history.shape[0]
     filtered = taps[0] * current
     for lag in range(1, len(taps)):
         filtered = filtered + taps[lag] * pltpu.roll(extended, lag, 0)[reach:]
@@ -143,10 +138,128 @@
     return packed
 
 
+def rates_of(table, sections, taps_count, levels):
+    rows = [table[at : at + 1] for at in range(sections * (levels + 1) + taps_count)]
+    poles = [rows[at * levels : (at + 1) * levels] for at in range(sections)]
+    zeros = rows[sections * levels : sections * (levels + 1)]
+    return (poles, zeros, rows[sections * (levels + 1) :])
+
+
+def prepare_kernel(width, first_bits, length, *refs):
+    place_ref, orders_hbm, lives_hbm, ratios_hbm, taps_hbm, counts_hbm = refs[:6]
+    vectors_hbm, diagonal_hbm = (refs[6:9], refs[9])
+    outs, scratch = (refs[10:20], refs[20:])
+    stacked_ref, energy_ref, live_ref, rates_ref, spread_ref, steps_ref = outs[:6]
+    slices = outs[6:]
+    orders_ref, lives_ref, ratios_ref, taps_ref, counts_ref = scratch[:5]
+    current_ref, remaining_ref, search_ref, diagonal_ref, sems = scratch[5:]
+    copies = [
+        pltpu.make_async_copy(source, target, sems.at[at])
+        for at, (source, target) in enumerate(
+            [
+                (orders_hbm, orders_ref),
+                (lives_hbm, lives_ref),
+                (ratios_hbm, ratios_ref),
+                (taps_hbm, taps_ref),
+                (counts_hbm, counts_ref),
+                (vectors_hbm[2].at[:, 0, :], search_ref),
+                (vectors_hbm[1].at[:, 0, :], remaining_ref),
+                (diagonal_hbm, diagonal_ref),
+                (vectors_hbm[0].at[:, 0, :], current_ref),
+            ]
+        )
+    ]
+    for copy in copies:
+        copy.start()
+    half = LANES // 2
+    segments, sections_each, components = lives_ref.shape
+    sections = segments * sections_each
+    taps_count = taps_ref.shape[1]
+    reach = taps_count - 1
+    kinds = sections + reach
+    for copy in copies[:5]:
+        copy.wait()
+    lane = lax.broadcasted_iota(jnp.int32, (components, LANES), 1)
+    component = lax.broadcasted_iota(jnp.int32, (components, LANES), 0)
+    count = half // components
+    spreader = jnp.where(lane % half // count == component, 1.0, 0.0)
+
+    def over_lanes(rows):
+        return jnp.dot(rows, spreader, precision=HIGHEST, preferred_element_type=F32)
+
+    def flat(ref):
+        return jnp.concatenate([ref[at] for at in range(segments)], axis=0)
+
+    life = over_lanes(flat(lives_ref))
+    ratio = over_lanes(flat(ratios_ref))
+    orders = over_lanes(orders_ref[...].astype(F32))
+    tap_rows = lax.dot_general(
+        taps_ref[...], spreader, (((0,), (0,)), ((), ())), precision=HIGHEST,
+        preferred_element_type=F32,
+    )
+    spare = jnp.concatenate(
+        [orders[at : at + 1] - (each + 0.5) for at in range(segments) for each in range(sections_each)],
+        axis=0,
+    )
+    active = spare > 0.0
+    pole_all = jnp.exp(-1.0 / life)
+    pole_rate = jnp.where(active, pole_all, 0.0)
+    zero_rate = jnp.where(active, 1.0 - ratio * (1.0 - pole_all), 0.0)
+    levels = length.bit_length() - 1
+    table = []
+    for section in range(sections):
+        power = pole_rate[section : section + 1]
+        for _ in range(levels):
+            table.append(power)
+            power = power * power
+    table = table + [zero_rate[section : section + 1] for section in range(sections)]
+    table = table + [tap_rows[tap : tap + 1] for tap in range(taps_count)]
+    for at, row in enumerate(table):
+        rates_ref[at : at + 1, :] = row
+    poles = [table[at * levels : (at + 1) * levels] for at in range(sections)]
+    zeros = table[sections * levels : sections * (levels + 1)]
+    taps = table[sections * (levels + 1) :]
+
+    lane = lax.broadcasted_iota(jnp.int32, (1, LANES), 1)
+    slot = jnp.where(lane >= half, lane % SLOT, SLOT)
+    units = [jnp.where(slot == at, 1.0, 0.0) for at in range(kinds)]
+    rows = lax.broadcasted_iota(jnp.int32, (reach, LANES), 0)
+    history = jnp.where(slot == kinds - 1 - rows, 1.0, 0.0)
+    nothing = jnp.zeros((length, LANES), F32)
+    filtered, ends = forward_block(nothing, units[: sections + 1], history, poles, zeros, taps)
+    local, heads = backward_block(filtered, None, poles, zeros, taps)
+    reply, replies = backward_block(nothing, units, poles, zeros, taps)
+    spread_ref[...] = jnp.where(lane < half, pltpu.roll(local, half, 1), reply)
+    stacked = jnp.concatenate([pack(ends), pack(heads), pack(replies)], axis=0)
+    source = lax.broadcasted_iota(jnp.int32, (LANES, kinds * LANES), 0)
+    target = lax.broadcasted_iota(jnp.int32, (LANES, kinds * LANES), 1)
+    within = target % LANES
+    wanted = half + within // SLOT * SLOT + target // LANES
+    pick = jnp.where((within < half) & (source == wanted), 1.0, 0.0)
+    steps_ref[...] = jnp.dot(stacked, pick, precision=HIGHEST, preferred_element_type=F32)
+    live_ref[...] = jnp.where(rows_of(nothing) < counts_ref[0], 1.0, 0.0)
+
+    copies[5].wait()
+    search = search_ref[...]
+    high = search.astype(BF16)
+    rest = search - high.astype(F32)
+    middle = rest.astype(BF16)
+    stacked_ref[...] = jnp.concatenate(
+        [high, middle, (rest - middle.astype(F32)).astype(BF16)], axis=0
+    )
+    copies[6].wait()
+    copies[7].wait()
+    remaining = remaining_ref[...]
+    energy = jnp.sum(remaining * diagonal_ref[...] * remaining, axis=1, keepdims=True)
+    energy_ref[...] = jnp.broadcast_to(energy, energy_ref.shape)
+    copies[8].wait()
+    cut_slices(width, first_bits, place_ref[0], [diagonal_ref, remaining_ref, search_ref, current_ref], slices)
+
+
 def filter_kernel(sections, taps_count, parts, *refs):
-    counts_ref, table_ref = refs[:2]
+    rates_ref, live_ref = refs[:2]
     gathered = refs[2 : 2 + parts]
-    send_ref, keep_ref, spread_ref, steps_ref, energy_ref = refs[2 + parts :]
+    send_ref, keep_ref, energy_ref = refs[2 + parts :]
     length = keep_ref.shape[0]
     half = LANES // 2
     received = gathered[0][...]
@@ -154,50 +267,16 @@
         received = received + other[...]
     energy_ref[...] = received[length:]
     received = received[:length]
-    lane = lax.broadcasted_iota(jnp.int32, (1, LANES), 1)
-    live = rows_of(received) < counts_ref[0]
-    data = jnp.where(live & (lane < half), received, 0.0)
-
-    table = table_ref[...]
-    life = table[:sections]
-    ratio = table[sections : 2 * sections]
-    active = table[2 * sections : 3 * sections] > 0.5
-    taps = [table[3 * sections + at :][:1] for at in range(taps_count)]
-    pole_all = jnp.exp(-1.0 / life)
-    pole_rate = jnp.where(active, pole_all, 0.0)
-    zero_rate = jnp.where(active, 1.0 - ratio * (1.0 - pole_all), 0.0)
-    poles, zeros = ([], [])
-    for section in range(sections):
-        power, powers, by = (pole_rate[section : section + 1], [], 1)
-        while by < length:
-            powers.append(power)
-            power, by = (power * power, 2 * by)
-        poles.append(powers)
-        zeros.append(zero_rate[section : section + 1])
-
-    reach = taps_count - 1
-    kinds = sections + reach
-    slot = jnp.where(lane >= half, lane % SLOT, SLOT)
-    units = [jnp.where(slot == at, 1.0, 0.0) for at in range(kinds)]
-    rows = lax.broadcasted_iota(jnp.int32, (reach, LANES), 0)
-    history = jnp.where(slot == kinds - 1 - rows, 1.0, 0.0)
-    filtered, ends = forward_block(data, units[: sections + 1], history, poles, zeros, taps)
+    low_half = lax.broadcasted_iota(jnp.int32, (1, LANES), 1) < half
+    data = jnp.where(low_half, received * live_ref[...], 0.0)
+    poles, zeros, taps = rates_of(rates_ref, sections, taps_count, length.bit_length() - 1)
+    history = jnp.zeros((taps_count - 1, LANES), F32)
+    filtered, ends = forward_block(data, None, history, poles, zeros, taps)
     local, heads = backward_block(filtered, None, poles, zeros, taps)
-    reply, replies = backward_block(jnp.zeros_like(filtered), units, poles, zeros, taps)
-    ends, heads, replies = (pack(ends), pack(heads), pack(replies))
-
-    low_half = lane < half
-    send_ref[...] = jnp.where(low_half, ends, pltpu.roll(heads, half, 1))
-    spread_ref[...] = jnp.where(low_half, pltpu.roll(local, half, 1), reply)
-    full = received + pltpu.roll(received, half, 1)
-    keep_ref[...] = jnp.where(low_half, local, full)
-    stacked = jnp.concatenate([ends, heads, replies], axis=0)
-    source = lax.broadcasted_iota(jnp.int32, (LANES, kinds * LANES), 0)
-    target = lax.broadcasted_iota(jnp.int32, (LANES, kinds * LANES), 1)
-    within = target % LANES
-    wanted = half + within // SLOT * SLOT + target // LANES
-    pick = jnp.where((within < half) & (source == wanted), 1.0, 0.0)
-    steps_ref[...] = jnp.dot(stacked, pick, precision=HIGHEST, preferred_element_type=F32)
+    sent = jnp.where(low_half, pack(ends), pltpu.roll(pack(heads), half, 1))
+    for block in range(send_ref.shape[0]):
+        send_ref[block] = sent
+    keep_ref[...] = jnp.where(low_half, local, received + pltpu.roll(received, half, 1))
 
 
 def blocks_of(value, width, padded):
@@ -212,9 +291,9 @@
         yield part[:, :padded]
 
 
-def normal_kernel(kinds, width, layout, *refs):
-    place_ref, counts_ref, all_ref, keep_ref, spread_ref, steps_ref, design_ref = refs[:7]
-    out_ref, entering_ref = refs[7:]
+def normal_kernel(kinds, width, first_bits, *refs):
+    place_ref, live_ref, all_ref, keep_ref, spread_ref, steps_ref, design_ref = refs[:7]
+    out_refs, entering_ref = (refs[7:-1], refs[-1])
     blocks = all_ref.shape[0]
     mine = place_ref[0]
     half = LANES // 2
@@ -257,12 +336,11 @@
         preferred_element_type=F32,
     )
     kept = keep_ref[...]
-    live = rows_of(kept) < counts_ref[0]
-    weighted = jnp.where(live & (lane < half), kept + correction, 0.0)
+    weighted = jnp.where(lane < half, (kept + correction) * live_ref[...], 0.0)
     weighted = weighted.astype(BF16).astype(F32)
     product = weighted * pltpu.roll(kept, half, 1)
     turned = jnp.transpose(weighted)
-    count = out_ref.shape[-2]
+    count = out_refs[0].shape[-2]
     low = jnp.concatenate(
         [turned[at * count : (at + 1) * count] for at in range(half // count)], axis=1
     ).astype(BF16)
@@ -277,18 +355,22 @@
     for at in range(1, half // count):
         curvature = curvature + curve[at * count : (at + 1) * count]
     normal = jnp.dot(low, design_ref[...], preferred_element_type=F32)
-    padded = out_ref.shape[-1]
+    padded = out_refs[0].shape[-1]
     column = lax.broadcasted_iota(jnp.int32, (count, padded), 1)
     curvature = jnp.broadcast_to(curvature[:, :1], (count, padded))
+    low_bits = mine % first_bits
     for block, part in enumerate(blocks_of(normal, width, padded)):
-        out_ref[layout(block)] = jnp.where(column < width, part, curvature)
-
-
-def slices_kernel(width, first_bits, place_ref, *refs):
-    count = len(refs) // 2
-    mine = place_ref[0]
+        part = jnp.where(column < width, part, curvature)
+        for apart, out_ref in enumerate(out_refs):
+
+            @pl.when((low_bits ^ apart) == block % first_bits)
+            def _(out_ref=out_ref, part=part, block=block):
+                out_ref[block // first_bits] = part
+
+
+def cut_slices(width, first_bits, mine, sources, targets):
     low = mine % first_bits
-    for source_ref, target_ref in zip(refs[:count], refs[count:]):
+    for source_ref, target_ref in zip(sources, targets):
         wide = source_ref.shape[-1]
         padded = target_ref.shape[-1]
         window = min(padded + LANES, wide)
@@ -365,81 +447,69 @@
     parts = blocks // classes
     place = lax.axis_index("tm").astype(jnp.int32).reshape(1)
     design_rows = design.reshape(components * length, wide)
-    search = direction[:, 0, :]
-    remaining = residual[:, 0, :]
-
-    predicted = call(
-        predict_kernel, shape(length + count, LANES), search, remaining, precond, design_rows
-    )
-    arrived = over_order(predicted)
-
-    active = jnp.arange(pole_life.shape[2])[None, None, :] < segment_orders[:, :, None]
-    columns = jnp.concatenate(
-        [
-            pole_life.reshape(components, -1),
-            zero_ratio.reshape(components, -1),
-            active.astype(F32).reshape(components, -1),
-            fir_taps,
-        ],
-        axis=1,
-    )
-    table = jnp.broadcast_to(
-        columns.T[:, None, :, None], (columns.shape[1], 2, components, count)
-    ).reshape(columns.shape[1], LANES)
-
-    send, keep, spread, steps, energy = call(
-        functools.partial(filter_kernel, sections, taps_count, len(arrived)),
+    levels = length.bit_length() - 1
+    anywhere = pl.BlockSpec(memory_space=pl.ANY)
+    small = [
+        segment_orders.T,
+        jnp.transpose(pole_life, (1, 2, 0)),
+        jnp.transpose(zero_ratio, (1, 2, 0)),
+        fir_taps,
+    ]
+
+    (stacked, energy_own, live, rates, spread, steps, diagonal_parts, remaining_parts, search_own, current_own) = call(
+        functools.partial(prepare_kernel, width, classes, length),
         (
-            shape(SLOT, LANES),
+            jax.ShapeDtypeStruct((3 * count, wide), BF16),
+            shape(count, LANES),
             shape(length, LANES),
+            shape(sections * (levels + 1) + taps_count, LANES),
             shape(length, LANES),
             shape(3 * SLOT, kinds * LANES),
-            shape(count, LANES),
-        ),
-        epoch_counts,
-        table,
-        *arrived,
-        specs=[smem()] + [vmem()] * (1 + len(arrived)),
-    )
-    everyone = lax.all_to_all(jnp.broadcast_to(send, (blocks, SLOT, LANES)), "tm", 0, 0)
-
-    def layout(block):
-        low = [block >> bit & 1 for bit in range(halved)]
-        return (*low, block >> halved)
-
-    buffer = call(
-        functools.partial(normal_kernel, kinds, width, layout),
-        shape(*(2,) * halved, parts, count, padded),
-        place,
-        epoch_counts,
-        everyone,
-        keep,
-        spread,
-        steps,
-        design_rows,
-        specs=[smem()] * 2 + [vmem()] * 5,
-        scratch=[pltpu.VMEM((blocks, SLOT, LANES), F32)],
-    )
-    diagonal_parts, remaining_parts, search_own, current_own = call(
-        functools.partial(slices_kernel, width, classes),
-        (
             shape(parts, count, padded),
             shape(parts, count, padded),
             shape(1, count, padded),
             shape(1, count, padded),
         ),
         place,
+        *small,
+        epoch_counts,
+        solution,
+        residual,
+        direction,
         precond,
-        remaining,
-        search,
-        solution[:, 0, :],
-        specs=[smem()] + [vmem()] * 4,
-    )
-    for bit in range(halved):
-        side = place[0] >> bit & 1
-        mine = lax.dynamic_index_in_dim(buffer, side, 0, False)
-        other = lax.dynamic_index_in_dim(buffer, 1 - side, 0, False)
-        buffer = mine + exchange(other, "tm", 1 << bit)
+        specs=[smem()] + [anywhere] * 9,
+        scratch=[pltpu.VMEM(each.shape, each.dtype) for each in small]
+        + [pltpu.SMEM((1,), jnp.int32)]
+        + [pltpu.VMEM((count, wide), F32)] * 3
+        + [pltpu.VMEM((1, wide), F32), pltpu.SemaphoreType.DMA((9,))],
+    )
+    predicted = call(
+        predict_kernel, shape(length + count, LANES), stacked, energy_own, design_rows
+    )
+    arrived = over_order(predicted)
+    send, keep, energy = call(
+        functools.partial(filter_kernel, sections, taps_count, len(arrived)),
+        (shape(blocks, SLOT, LANES), shape(length, LANES), shape(count, LANES)),
+        rates,
+        live,
+        *arrived,
+    )
+    everyone = lax.all_to_all(send, "tm", 0, 0)
+    pieces = call(
+        functools.partial(normal_kernel, kinds, width, classes),
+        [shape(parts, count, padded)] * classes,
+        place,
+        live,
+        everyone,
+        keep,
+        spread,
+        steps,
+        design_rows,
+        specs=[smem()] + [vmem()] * 6,
+        scratch=[pltpu.VMEM((blocks, SLOT, LANES), F32)],
+    )
+    arriving = [exchange(pieces[apart], "tm", apart) for apart in range(1, classes)]
+    buffer = pieces[0] + sum(arriving[1:], arriving[0])
     for bit in range(halved, bits - 1):
         buffer = buffer + exchange(buffer, "tm", 1 << bit)
     arriving = exchange(buffer, "tm", 1 << bits - 1)

time: 64.8 us -> 61.7 us (0.952)
  blocking collectives: 0 us -> 15.8 us
  waiting for transfers between devices: 31.9 us -> 18.6 us
  starting transfers between devices: 12.5 us -> 8.43 us
  local copies, waits for them, and re-layouts: 13.1 us -> 10.2 us
  Pallas kernels: 3.92 us -> 6.59 us
  other arithmetic: 1.32 us -> 0.24 us
    all_to_all x0 -> x1, blocking collectives: none -> 15.8 us  [shards(): everyone = lax.all_to_all(send, 'tm', 0, 0)]
    all_to_all x1 -> x0, waiting for transfers between devices: 8.08 us -> none  [shards(): lax.all_to_all(jnp.broadcast_to(send, (blocks, SLOT, LANES)), 'tm', 0, 0)]
    all_to_all x1 -> x0, starting transfers between devices: 7.87 us -> none  [shards(): lax.all_to_all(jnp.broadcast_to(send, (blocks, SLOT, LANES)), 'tm', 0, 0)]
    ppermute x8 -> x9, waiting for transfers between devices: 23.8 us -> 18.6 us  [exchange(): return lax.ppermute(value, axis, [(at, at ^ bit) for at in range(size)])]
    ppermute x8 -> x9, starting transfers between devices: 4.62 us -> 8.43 us  [exchange(): return lax.ppermute(value, axis, [(at, at ^ bit) for at in range(size)])]
    pallas_call x5, Pallas kernels: 3.92 us -> 6.59 us  [call(): pl.pallas_call(kernel, out_shape=outs, in_specs=specs or [vmem()] * len(a...]
    broadcast_in_dim x2 -> x0, local copies, waits for them, and re-layouts: 1.38 us -> none  [the longest x1 0.72 us: shards(): jnp.broadcast_to(columns.T[:, None, :, None], (columns.shape[1], 2, compo...]
    reshape x3 -> x0, local copies, waits for them, and re-layouts: 1.18 us -> none  [the longest x1 0.99 us: shards(): table = jnp.broadcast_to(columns.T[:, None, :, None], (columns.shape[1],...]
  transfers between devices with their start and end apart: 9 -> 9, of which waited for: 7 -> 7; matrix products, arithmetic and copies ran while one was open for 7% -> 2% of each run, Pallas kernels for 0% -> 0%
where the time goes in v2:
time: 61.7 us; the launch traced here: 61.2 us
  waiting for transfers between devices  18.6 us (30%)
  blocking collectives  15.8 us (26%)
  local copies, waits for them, and re-layouts  10.2 us (17%)
  starting transfers between devices  8.43 us (14%)
  Pallas kernels  6.59 us (11%)
  between operations  1.34 us (2%)
    ppermute x9, waiting for transfers between devices, exchange(): return lax.ppermute(value, axis, [(at, at ^ bit) for at in range(size)])  18.6 us
    all_to_all x1, blocking collectives, shards(): everyone = lax.all_to_all(send, 'tm', 0, 0)  15.8 us
    unnamed x23, local copies, waits for them, and re-layouts  10.2 us
    ppermute x9, starting transfers between devices, exchange(): return lax.ppermute(value, axis, [(at, at ^ bit) for at in range(size)])  8.43 us
    pallas_call x5, Pallas kernels, call(): pl.pallas_call(kernel, out_shape=outs, in_specs=specs or [vmem()] * len(a...  6.59 us
  transfers between devices with their start and end apart: 9, of which 7 were waited for; matrix products, arithmetic and copies ran while one was open for 2% of the time, Pallas kernels for 0%

profile of v2, /device:TPU:0, one launch (start us, length us, event | category | flops | bytes accessed | tf_op | source)
XLA Modules:
  0.0 61.2 jit_solution(5254591258247183176)
XLA Ops:
  1.3 0.0 copy-start.2
  1.3 1.0 %copy-done.2 = f32[16,1,5760]{2,1,0:T(1,128)S(1)} copy-done((f32[16,1,5760]{2,1,0:T(1,128)S(1)}, f32[16,1,5760]{2,1,0:T(1,128)}, u32[]{:S(2)}) %copy-start.2) | copy-done | bytes 368664
  2.3 0.0 copy-start.3
  2.3 1.0 %copy-done.3 = f32[16,1,5760]{2,1,0:T(1,128)S(1)} copy-done((f32[16,1,5760]{2,1,0:T(1,128)S(1)}, f32[16,1,5760]{2,1,0:T(1,128)}, u32[]{:S(2)}) %copy-start.3) | copy-done | bytes 368664
  3.3 0.0 copy-start.4
  3.3 1.0 %copy-done.4 = f32[16,1,5760]{2,1,0:T(1,128)S(1)} copy-done((f32[16,1,5760]{2,1,0:T(1,128)S(1)}, f32[16,1,5760]{2,1,0:T(1,128)}, u32[]{:S(2)}) %copy-start.4) | copy-done | bytes 368664
  4.2 0.0 copy-start.5
  4.2 0.7 %copy-done.5 = f32[1,5760]{1,0:T(1,128)S(1)} copy-done((f32[1,5760]{1,0:T(1,128)S(1)}, f32[1,5760]{1,0:T(1,128)}, u32[]{:S(2)}) %copy-start.5) | copy-done | bytes 23064
  5.0 0.0 copy-start.6
  5.0 0.7 %copy-done.6 = f32[4,2,2]{0,2,1:T(2,128)S(1)} copy-done((f32[4,2,2]{0,2,1:T(2,128)S(1)}, f32[4,2,2]{0,2,1:T(2,128)}, u32[]{:S(2)}) %copy-start.6) | copy-done | bytes 88
  5.7 0.0 copy-start.7
  5.7 0.7 %copy-done.7 = f32[4,2,2]{0,2,1:T(2,128)S(1)} copy-done((f32[4,2,2]{0,2,1:T(2,128)S(1)}, f32[4,2,2]{0,2,1:T(2,128)}, u32[]{:S(2)}) %copy-start.7) | copy-done | bytes 88
  6.3 0.0 copy-start.8
  6.3 0.7 %copy-done.8 = f32[4,9]{1,0:T(4,128)S(1)} copy-done((f32[4,9]{1,0:T(4,128)S(1)}, f32[4,9]{1,0:T(4,128)}, u32[]{:S(2)}) %copy-start.8) | copy-done | bytes 168
  7.0 0.0 copy-start.9
  7.0 0.7 %copy-done.9 = s32[4,2]{0,1:T(2,128)S(1)} copy-done((s32[4,2]{0,1:T(2,128)S(1)}, s32[4,2]{0,1:T(2,128)}, u32[]{:S(2)}) %copy-start.9) | copy-done | bytes 56
  7.7 2.4 %shard_map.121 = (bf16[48,5760]{1,0:T(8,128)(2,1)S(1)}, f32[16,128]{1,0:T(8,128)S(1)}, f32[64,128]{1,0:T(8,128)S(1)}, f32[37,128]{1,0:T(8,128)S(1)}, f32[64,128]...) custom-call(s32[1]{0:T(128)} %bitcast.refs_0_, ...), custom_call_target="tpu_custom_call" | custom-call | tf_op jit(solution)/shard_map/pallas_call | solution.py:27
  10.1 0.0 copy-start
  10.1 1.8 %copy-done = bf16[4,64,1,5760]{3,1,2,0:T(8,128)(2,1)S(1)} copy-done((bf16[4,64,1,5760]{3,1,2,0:T(8,128)(2,1)S(1)}, bf16[4,64,1,5760]{3,1,2,0:T(8,128)(2,1)}, u32[]{:S(2)}) %copy-start) | copy-done | bytes 2949144
  11.9 1.1 %shard_map.122.refs_2_ = f32[80,128]{1,0:T(8,128)S(1)} custom-call(bf16[48,5760]{1,0:T(8,128)(2,1)S(1)} %get-tuple-element.26.stacked_ref, f32[16,128]{1,0:T(8,128)S(1)} %get-tuple-element.27.energy_ref, bf16[256,5760]{1,0:T(8,128)(2,1)S(1)} %bitcast.12), custom_call_target="tpu_custom_call" | custom-call | tf_op jit(solution)/shard_map/pallas_call | solution.py:27
  13.0 0.5 collective-permute-start
  13.5 0.9 %collective-permute-done.refs_3_ = f32[80,128]{1,0:T(8,128)S(1)} collective-permute-done((f32[80,128]{1,0:T(8,128)S(1)}, f32[80,128]{1,0:T(8,128)S(1)}, u32[]{:S(2)}, u32[]{:S(2)}) %collective-permute-start) | collective-permute-done | bytes 40992 | tf_op jit(solution)/shard_map/ppermute | solution.py:415
  14.4 0.4 shard_map.123
  14.7 15.8 %all_to_all.5.refs_2_ = f32[16,16,128]{2,1,0:T(8,128)S(1)} all-to-all(f32[16,16,128]{2,1,0:T(8,128)S(1)} %get-tuple-element.28), channel_id=1, replica_groups=mesh['tm'=16,'order'=2] {'tm'}, dimensions={0} | all-to-all | bytes 262144 | tf_op jit(solution)/shard_map/all_to_all | solution.py:497
  30.5 0.0 copy-done.1
  30.5 2.6 %shard_map.124 = (f32[4,16,384]{2,1,0:T(8,128)S(1)}, f32[4,16,384]{2,1,0:T(8,128)S(1)}, f32[4,16,384]{2,1,0:T(8,128)S(1)}, f32[4,16,384]{2,1,0:T(8,128)S(1)}) custom-call(s32[1]{0:T(128)} %bitcast.refs_0_, f32[64,128]{1,0:T(8,128)S(1)} %get-tuple-element.24.refs_1_, f32[16,16,128]{2,1,0:T(8,128)S(1)} %all_to_all.5.refs_2_, ...), custom_call_target="tpu_custom_call" | custom-call | tf_op jit(solution)/shard_map/pallas_call | solution.py:27
  33.1 1.1 %collective-permute-start.1 = (f32[4,16,384]{2,1,0:T(8,128)S(1)}, f32[4,16,384]{2,1,0:T(8,128)S(1)}, u32[]{:S(2)}, u32[]{:S(2)}) collective-permute-start(f32[4,16,384]{2,1,0:T(8,128)S(1)} %get-tuple-element.33), channel_id=1, source_target_pairs={{0,2},{2,0},{4,6},{6,4},{8,10},{10,8},{12,14},{14,12},{16,18},{18,... | collective-permute-start | bytes 294920 | tf_op jit(solution)/shard_map/ppermute | solution.py:415
  34.2 0.2 collective-permute-start.2
  34.4 2.2 %collective-permute-start.3 = (f32[4,16,384]{2,1,0:T(8,128)S(1)}, f32[4,16,384]{2,1,0:T(8,128)S(1)}, u32[]{:S(2)}, u32[]{:S(2)}) collective-permute-start(f32[4,16,384]{2,1,0:T(8,128)S(1)} %get-tuple-element.35), channel_id=1, source_target_pairs={{0,6},{2,4},{4,2},{6,0},{8,14},{10,12},{12,10},{14,8},{16,22},{18,... | collective-permute-start | bytes 294920 | tf_op jit(solution)/shard_map/ppermute | solution.py:415
  36.6 2.1 %collective-permute-done.1 = f32[4,16,384]{2,1,0:T(8,128)S(1)} collective-permute-done((f32[4,16,384]{2,1,0:T(8,128)S(1)}, f32[4,16,384]{2,1,0:T(8,128)S(1)}, u32[]{:S(2)}, u32[]{:S(2)}) %collective-permute-start.1) | collective-permute-done | bytes 98336 | tf_op jit(solution)/shard_map/ppermute | solution.py:415
  38.7 1.4 %collective-permute-done.2 = f32[4,16,384]{2,1,0:T(8,128)S(1)} collective-permute-done((f32[4,16,384]{2,1,0:T(8,128)S(1)}, f32[4,16,384]{2,1,0:T(8,128)S(1)}, u32[]{:S(2)}, u32[]{:S(2)}) %collective-permute-start.2) | collective-permute-done | bytes 98336 | tf_op jit(solution)/shard_map/ppermute | solution.py:415
  40.1 0.0 collective-permute-done.3
  40.1 0.8 %collective-permute-start.4 = (f32[4,16,384]{2,1,0:T(8,128)S(1)}, f32[4,16,384]{2,1,0:T(8,128)S(1)}, u32[]{:S(2)}, u32[]{:S(2)}) collective-permute-start(f32[4,16,384]{2,1,0:T(8,128)S(1)} %add_add_fusion), channel_id=1, source_target_pairs={{0,8},{2,10},{4,12},{6,14},{8,0},{10,2},{12,4},{14,6},{16,24},{18,... | collective-permute-start | bytes 294920 | tf_op jit(solution)/shard_map/ppermute | solution.py:415
  40.9 3.9 %collective-permute-done.4 = f32[4,16,384]{2,1,0:T(8,128)S(1)} collective-permute-done((f32[4,16,384]{2,1,0:T(8,128)S(1)}, f32[4,16,384]{2,1,0:T(8,128)S(1)}, u32[]{:S(2)}, u32[]{:S(2)}) %collective-permute-start.4) | collective-permute-done | bytes 98336 | tf_op jit(solution)/shard_map/ppermute | solution.py:415
  44.8 0.9 %collective-permute-start.5 = (f32[4,16,384]{2,1,0:T(8,128)S(1)}, f32[4,16,384]{2,1,0:T(8,128)S(1)}, u32[]{:S(2)}, u32[]{:S(2)}) collective-permute-start(f32[4,16,384]{2,1,0:T(8,128)S(1)} %add.27.refs_1_), channel_id=1, source_target_pairs={{0,16},{2,18},{4,20},{6,22},{8,24},{10,26},{12,28},{14,30},{16,0},... | collective-permute-start | bytes 294920 | tf_op jit(solution)/shard_map/ppermute | solution.py:415
  45.7 5.7 %collective-permute-done.5.refs_2_ = f32[4,16,384]{2,1,0:T(8,128)S(1)} collective-permute-done((f32[4,16,384]{2,1,0:T(8,128)S(1)}, f32[4,16,384]{2,1,0:T(8,128)S(1)}, u32[]{:S(2)}, u32[]{:S(2)}) %collective-permute-start.5) | collective-permute-done | bytes 98336 | tf_op jit(solution)/shard_map/ppermute | solution.py:415
  51.5 0.3 shard_map.125
  51.7 1.3 %collective-permute-start.6 = (f32[16,128]{1,0:T(8,128)S(1)}, f32[16,128]{1,0:T(8,128)S(1)}, u32[]{:S(2)}, u32[]{:S(2)}) collective-permute-start(f32[16,128]{1,0:T(8,128)S(1)} %get-tuple-element.44), channel_id=1, source_target_pairs={{0,2},{2,0},{4,6},{6,4},{8,10},{10,8},{12,14},{14,12},{16,18},{18,... | collective-permute-start | bytes 24584 | tf_op jit(solution)/shard_map/ppermute | solution.py:415
  53.0 2.4 %collective-permute-done.6 = f32[16,128]{1,0:T(8,128)S(1)} collective-permute-done((f32[16,128]{1,0:T(8,128)S(1)}, f32[16,128]{1,0:T(8,128)S(1)}, u32[]{:S(2)}, u32[]{:S(2)}) %collective-permute-start.6) | collective-permute-done | bytes 8224 | tf_op jit(solution)/shard_map/ppermute | solution.py:415
  55.4 1.4 %collective-permute-start.7 = (f32[16,128]{1,0:T(8,128)S(1)}, f32[16,128]{1,0:T(8,128)S(1)}, u32[]{:S(2)}, u32[]{:S(2)}) collective-permute-start(f32[16,128]{1,0:T(8,128)S(1)} %add.28), channel_id=1, source_target_pairs={{0,4},{2,6},{4,0},{6,2},{8,12},{10,14},{12,8},{14,10},{16,20},{18,... | collective-permute-start | bytes 24584 | tf_op jit(solution)/shard_map/ppermute | solution.py:415
  56.8 2.2 %collective-permute-done.7 = f32[16,128]{1,0:T(8,128)S(1)} collective-permute-done((f32[16,128]{1,0:T(8,128)S(1)}, f32[16,128]{1,0:T(8,128)S(1)}, u32[]{:S(2)}, u32[]{:S(2)}) %collective-permute-start.7) | collective-permute-done | bytes 8224 | tf_op jit(solution)/shard_map/ppermute | solution.py:415
  59.0 0.0 collective-permute-start.8
  59.1 0.6 %copy.17 = f32[16,1,360]{2,1,0:T(1,128)} copy(f32[16,1,360]{2,0,1:T(8,128)S(1)} %get-tuple-element.51) | data formatting | bytes 46080
  59.7 0.6 %copy.16 = f32[16,1,360]{2,1,0:T(1,128)} copy(f32[16,1,360]{2,0,1:T(8,128)S(1)} %get-tuple-element.52) | data formatting | bytes 46080
  60.3 0.0 collective-permute-done.8
  60.3 0.1 fusion.1
  60.4 0.1 fusion
  60.5 0.6 %copy.18 = f32[16,1,360]{2,1,0:T(1,128)} copy(f32[16,1,360]{2,0,1:T(8,128)S(1)} %fusion) | data formatting | bytes 46080
  (6 shorter events, 0.1 us)
Async XLA Ops:
  1.3 1.0 %copy-start.2 = (f32[16,1,5760]{2,1,0:T(1,128)S(1)}, f32[16,1,5760]{2,1,0:T(1,128)}, u32[]{:S(2)}) copy-start(f32[16,1,5760]{2,1,0:T(1,128)} %refs_6_.1) | copy-start | bytes 1105924
  2.3 1.0 %copy-start.3 = (f32[16,1,5760]{2,1,0:T(1,128)S(1)}, f32[16,1,5760]{2,1,0:T(1,128)}, u32[]{:S(2)}) copy-start(f32[16,1,5760]{2,1,0:T(1,128)} %refs_7_.1) | copy-start | bytes 1105924
  3.3 1.0 %copy-start.4 = (f32[16,1,5760]{2,1,0:T(1,128)S(1)}, f32[16,1,5760]{2,1,0:T(1,128)}, u32[]{:S(2)}) copy-start(f32[16,1,5760]{2,1,0:T(1,128)} %refs_8_.1) | copy-start | bytes 1105924
  4.2 0.7 %copy-start.5 = (f32[1,5760]{1,0:T(1,128)S(1)}, f32[1,5760]{1,0:T(1,128)}, u32[]{:S(2)}) copy-start(f32[1,5760]{1,0:T(1,128)} %refs_9_.1) | copy-start | bytes 69124
  5.0 0.7 %copy-start.6 = (f32[4,2,2]{0,2,1:T(2,128)S(1)}, f32[4,2,2]{0,2,1:T(2,128)}, u32[]{:S(2)}) copy-start(f32[4,2,2]{0,2,1:T(2,128)} %param.17) | copy-start | bytes 196
  5.7 0.7 %copy-start.7 = (f32[4,2,2]{0,2,1:T(2,128)S(1)}, f32[4,2,2]{0,2,1:T(2,128)}, u32[]{:S(2)}) copy-start(f32[4,2,2]{0,2,1:T(2,128)} %param.18) | copy-start | bytes 196
  6.3 0.7 %copy-start.8 = (f32[4,9]{1,0:T(4,128)S(1)}, f32[4,9]{1,0:T(4,128)}, u32[]{:S(2)}) copy-start(f32[4,9]{1,0:T(4,128)} %refs_4_.1) | copy-start | bytes 436
  7.0 0.7 %copy-start.9 = (s32[4,2]{0,1:T(2,128)S(1)}, s32[4,2]{0,1:T(2,128)}, u32[]{:S(2)}) copy-start(s32[4,2]{0,1:T(2,128)} %param.16) | copy-start | bytes 100
  10.1 1.8 %copy-start = (bf16[4,64,1,5760]{3,1,2,0:T(8,128)(2,1)S(1)}, bf16[4,64,1,5760]{3,1,2,0:T(8,128)(2,1)}, u32[]{:S(2)}) copy-start(bf16[4,64,1,5760]{3,1,2,0:T(8,128)(2,1)} %param.14) | copy-start | bytes 8847364
  11.9 18.6 %copy-start.1 = (bf16[4,64,1,5760]{3,1,2,0:T(8,128)(2,1)S(1)}, bf16[4,64,1,5760]{3,1,2,0:T(8,128)(2,1)}, u32[]{:S(2)}) copy-start(bf16[4,64,1,5760]{3,1,2,0:T(8,128)(2,1)} %param.14) | copy-start | bytes 8847364
  13.0 1.4 %collective-permute-start = (f32[80,128]{1,0:T(8,128)S(1)}, f32[80,128]{1,0:T(8,128)S(1)}, u32[]{:S(2)}, u32[]{:S(2)}) collective-permute-start(f32[80,128]{1,0:T(8,128)S(1)} %shard_map.122.refs_2_), channel_id=1, source_target_pairs={{0,1},{1,0},{2,3},{3,2},{4,5},{5,4},{6,7},{7,6},{8,9},{9,8},{10,11... | collective-permute-start | bytes 122888 | tf_op jit(solution)/shard_map/ppermute | solution.py:415
  33.1 5.7 %collective-permute-start.1 = (f32[4,16,384]{2,1,0:T(8,128)S(1)}, f32[4,16,384]{2,1,0:T(8,128)S(1)}, u32[]{:S(2)}, u32[]{:S(2)}) collective-permute-start(f32[4,16,384]{2,1,0:T(8,128)S(1)} %get-tuple-element.33), channel_id=1, source_target_pairs={{0,2},{2,0},{4,6},{6,4},{8,10},{10,8},{12,14},{14,12},{16,18},{18,... | collective-permute-start | bytes 294920 | tf_op jit(solution)/shard_map/ppermute | solution.py:415
  34.2 5.9 %collective-permute-start.2 = (f32[4,16,384]{2,1,0:T(8,128)S(1)}, f32[4,16,384]{2,1,0:T(8,128)S(1)}, u32[]{:S(2)}, u32[]{:S(2)}) collective-permute-start(f32[4,16,384]{2,1,0:T(8,128)S(1)} %get-tuple-element.34), channel_id=1, source_target_pairs={{0,4},{2,6},{4,0},{6,2},{8,12},{10,14},{12,8},{14,10},{16,20},{18,... | collective-permute-start | bytes 294920 | tf_op jit(solution)/shard_map/ppermute | solution.py:415
  34.4 5.7 %collective-permute-start.3 = (f32[4,16,384]{2,1,0:T(8,128)S(1)}, f32[4,16,384]{2,1,0:T(8,128)S(1)}, u32[]{:S(2)}, u32[]{:S(2)}) collective-permute-start(f32[4,16,384]{2,1,0:T(8,128)S(1)} %get-tuple-element.35), channel_id=1, source_target_pairs={{0,6},{2,4},{4,2},{6,0},{8,14},{10,12},{12,10},{14,8},{16,22},{18,... | collective-permute-start | bytes 294920 | tf_op jit(solution)/shard_map/ppermute | solution.py:415
  40.1 4.7 %collective-permute-start.4 = (f32[4,16,384]{2,1,0:T(8,128)S(1)}, f32[4,16,384]{2,1,0:T(8,128)S(1)}, u32[]{:S(2)}, u32[]{:S(2)}) collective-permute-start(f32[4,16,384]{2,1,0:T(8,128)S(1)} %add_add_fusion), channel_id=1, source_target_pairs={{0,8},{2,10},{4,12},{6,14},{8,0},{10,2},{12,4},{14,6},{16,24},{18,... | collective-permute-start | bytes 294920 | tf_op jit(solution)/shard_map/ppermute | solution.py:415
  44.8 6.6 %collective-permute-start.5 = (f32[4,16,384]{2,1,0:T(8,128)S(1)}, f32[4,16,384]{2,1,0:T(8,128)S(1)}, u32[]{:S(2)}, u32[]{:S(2)}) collective-permute-start(f32[4,16,384]{2,1,0:T(8,128)S(1)} %add.27.refs_1_), channel_id=1, source_target_pairs={{0,16},{2,18},{4,20},{6,22},{8,24},{10,26},{12,28},{14,30},{16,0},... | collective-permute-start | bytes 294920 | tf_op jit(solution)/shard_map/ppermute | solution.py:415
  51.7 3.7 %collective-permute-start.6 = (f32[16,128]{1,0:T(8,128)S(1)}, f32[16,128]{1,0:T(8,128)S(1)}, u32[]{:S(2)}, u32[]{:S(2)}) collective-permute-start(f32[16,128]{1,0:T(8,128)S(1)} %get-tuple-element.44), channel_id=1, source_target_pairs={{0,2},{2,0},{4,6},{6,4},{8,10},{10,8},{12,14},{14,12},{16,18},{18,... | collective-permute-start | bytes 24584 | tf_op jit(solution)/shard_map/ppermute | solution.py:415
  55.4 3.7 %collective-permute-start.7 = (f32[16,128]{1,0:T(8,128)S(1)}, f32[16,128]{1,0:T(8,128)S(1)}, u32[]{:S(2)}, u32[]{:S(2)}) collective-permute-start(f32[16,128]{1,0:T(8,128)S(1)} %add.28), channel_id=1, source_target_pairs={{0,4},{2,6},{4,0},{6,2},{8,12},{10,14},{12,8},{14,10},{16,20},{18,... | collective-permute-start | bytes 24584 | tf_op jit(solution)/shard_map/ppermute | solution.py:415
  59.0 1.3 %collective-permute-start.8 = (f32[16,128]{1,0:T(8,128)S(1)}, f32[16,128]{1,0:T(8,128)S(1)}, u32[]{:S(2)}, u32[]{:S(2)}) collective-permute-start(f32[16,128]{1,0:T(8,128)S(1)} %add.29), channel_id=1, source_target_pairs={{0,1},{1,0},{2,3},{3,2},{4,5},{5,4},{6,7},{7,6},{8,9},{9,8},{10,11... | collective-permute-start | bytes 24584 | tf_op jit(solution)/shard_map/ppermute | solution.py:415

commit v3 on v2

--- a/solution.py
+++ b/solution.py
@@ -24,6 +24,12 @@
 
 
 def call(kernel, outs, *args, specs=None, scratch=()):
+    args = [
+        pltpu.with_memory_space_constraint(arg, pltpu.HBM)
+        if specs and specs[at].memory_space == pltpu.HBM
+        else arg
+        for at, arg in enumerate(args)
+    ]
     return pl.pallas_call(
         kernel,
         out_shape=outs,
@@ -36,19 +42,6 @@
 
 def shape(*dims):
     return jax.ShapeDtypeStruct(dims, F32)
-
-
-def predict_kernel(stacked_ref, energy_ref, design_ref, out_ref):
-    count = stacked_ref.shape[0] // 3
-    sums = lax.dot_general(
-        design_ref[...], stacked_ref[...], (((1,), (1,)), ((), ())), preferred_element_type=F32
-    )
-    length = sums.shape[0] * count // (LANES // 2)
-    pieces = [sums[start : start + length] for start in range(0, sums.shape[0], length)]
-    coarse = [piece[:, :count] for piece in pieces]
-    fine = [piece[:, count : 2 * count] + piece[:, 2 * count :] for piece in pieces]
-    out_ref[:length, :] = jnp.concatenate(coarse + fine, axis=1)
-    out_ref[length:, :] = energy_ref[...]
 
 
 def rows_of(value):
@@ -146,13 +139,14 @@
 
 
 def prepare_kernel(width, first_bits, length, *refs):
-    place_ref, orders_hbm, lives_hbm, ratios_hbm, taps_hbm, counts_hbm = refs[:6]
-    vectors_hbm, diagonal_hbm = (refs[6:9], refs[9])
-    outs, scratch = (refs[10:20], refs[20:])
-    stacked_ref, energy_ref, live_ref, rates_ref, spread_ref, steps_ref = outs[:6]
-    slices = outs[6:]
-    orders_ref, lives_ref, ratios_ref, taps_ref, counts_ref = scratch[:5]
-    current_ref, remaining_ref, search_ref, diagonal_ref, sems = scratch[5:]
+    place_ref, orders_hbm, lives_hbm, ratios_hbm, taps_hbm = refs[:5]
+    vectors_hbm, diagonal_hbm, design_hbm = (refs[5:8], refs[8], refs[9])
+    outs, scratch = (refs[10:18], refs[18:])
+    predicted_ref, rates_ref, spread_ref, steps_ref = outs[:4]
+    slices = outs[4:]
+    orders_ref, lives_ref, ratios_ref, taps_ref = scratch[:4]
+    current_ref, remaining_ref, search_ref, diagonal_ref, design_ref, sems = scratch[4:]
+    components = design_ref.shape[0]
     copies = [
         pltpu.make_async_copy(source, target, sems.at[at])
         for at, (source, target) in enumerate(
@@ -161,8 +155,8 @@
                 (lives_hbm, lives_ref),
                 (ratios_hbm, ratios_ref),
                 (taps_hbm, taps_ref),
-                (counts_hbm, counts_ref),
                 (vectors_hbm[2].at[:, 0, :], search_ref),
+                *[(design_hbm.at[at], design_ref.at[at]) for at in range(components)],
                 (vectors_hbm[1].at[:, 0, :], remaining_ref),
                 (diagonal_hbm, diagonal_ref),
                 (vectors_hbm[0].at[:, 0, :], current_ref),
@@ -172,12 +166,12 @@
     for copy in copies:
         copy.start()
     half = LANES // 2
-    segments, sections_each, components = lives_ref.shape
+    segments, sections_each, _ = lives_ref.shape
     sections = segments * sections_each
     taps_count = taps_ref.shape[1]
     reach = taps_count - 1
     kinds = sections + reach
-    for copy in copies[:5]:
+    for copy in copies[:4]:
         copy.wait()
     lane = lax.broadcasted_iota(jnp.int32, (components, LANES), 1)
     component = lax.broadcasted_iota(jnp.int32, (components, LANES), 0)
@@ -237,27 +231,34 @@
     wanted = half + within // SLOT * SLOT + target // LANES
     pick = jnp.where((within < half) & (source == wanted), 1.0, 0.0)
     steps_ref[...] = jnp.dot(stacked, pick, precision=HIGHEST, preferred_element_type=F32)
-    live_ref[...] = jnp.where(rows_of(nothing) < counts_ref[0], 1.0, 0.0)
-
-    copies[5].wait()
+
+    copies[4].wait()
     search = search_ref[...]
     high = search.astype(BF16)
     rest = search - high.astype(F32)
     middle = rest.astype(BF16)
-    stacked_ref[...] = jnp.concatenate(
-        [high, middle, (rest - middle.astype(F32)).astype(BF16)], axis=0
-    )
-    copies[6].wait()
-    copies[7].wait()
+    low = (rest - middle.astype(F32)).astype(BF16)
+    split = jnp.concatenate([high, middle, low], axis=0)
+    coarse, fine = ([], [])
+    for at in range(components):
+        copies[5 + at].wait()
+        sums = lax.dot_general(
+            design_ref[at], split, (((1,), (1,)), ((), ())), preferred_element_type=F32
+        )
+        coarse.append(sums[:, :count])
+        fine.append(sums[:, count : 2 * count] + sums[:, 2 * count :])
+    predicted_ref[:length, :] = jnp.concatenate(coarse + fine, axis=1)
+    for copy in copies[5 + components :]:
+        copy.wait()
     remaining = remaining_ref[...]
     energy = jnp.sum(remaining * diagonal_ref[...] * remaining, axis=1, keepdims=True)
-    energy_ref[...] = jnp.broadcast_to(energy, energy_ref.shape)
-    copies[8].wait()
-    cut_slices(width, first_bits, place_ref[0], [diagonal_ref, remaining_ref, search_ref, current_ref], slices)
+    predicted_ref[length:, :] = jnp.broadcast_to(energy, (count, LANES))
+    sources = [diagonal_ref, remaining_ref, search_ref, current_ref]
+    cut_slices(width, first_bits, place_ref[0], sources, slices)
 
 
 def filter_kernel(sections, taps_count, parts, *refs):
-    rates_ref, live_ref = refs[:2]
+    counts_ref, rates_ref = refs[:2]
     gathered = refs[2 : 2 + parts]
     send_ref, keep_ref, energy_ref = refs[2 + parts :]
     length = keep_ref.shape[0]
@@ -268,7 +269,7 @@
     energy_ref[...] = received[length:]
     received = received[:length]
     low_half = lax.broadcasted_iota(jnp.int32, (1, LANES), 1) < half
-    data = jnp.where(low_half, received * live_ref[...], 0.0)
+    data = jnp.where(low_half & (rows_of(received) < counts_ref[0]), received, 0.0)
     poles, zeros, taps = rates_of(rates_ref, sections, taps_count, length.bit_length() - 1)
     history = jnp.zeros((taps_count - 1, LANES), F32)
     filtered, ends = forward_block(data, None, history, poles, zeros, taps)
@@ -292,8 +293,10 @@
 
 
 def normal_kernel(kinds, width, first_bits, *refs):
-    place_ref, live_ref, all_ref, keep_ref, spread_ref, steps_ref, design_ref = refs[:7]
-    out_refs, entering_ref = (refs[7:-1], refs[-1])
+    place_ref, counts_ref, all_ref, keep_ref, spread_ref, steps_ref, design_hbm = refs[:7]
+    out_refs, (entering_ref, design_ref, sem) = (refs[7:-3], refs[-3:])
+    fetch = pltpu.make_async_copy(design_hbm, design_ref, sem)
+    fetch.start()
     blocks = all_ref.shape[0]
     mine = place_ref[0]
     half = LANES // 2
@@ -336,7 +339,8 @@
         preferred_element_type=F32,
     )
     kept = keep_ref[...]
-    weighted = jnp.where(lane < half, (kept + correction) * live_ref[...], 0.0)
+    live = (row < counts_ref[0]) & (lane < half)
+    weighted = jnp.where(live, kept + correction, 0.0)
     weighted = weighted.astype(BF16).astype(F32)
     product = weighted * pltpu.roll(kept, half, 1)
     turned = jnp.transpose(weighted)
@@ -354,6 +358,7 @@
     curvature = curve[:count]
     for at in range(1, half // count):
         curvature = curvature + curve[at * count : (at + 1) * count]
+    fetch.wait()
     normal = jnp.dot(low, design_ref[...], preferred_element_type=F32)
     padded = out_refs[0].shape[-1]
     column = lax.broadcasted_iota(jnp.int32, (count, padded), 1)
@@ -446,9 +451,8 @@
     classes = 1 << halved
     parts = blocks // classes
     place = lax.axis_index("tm").astype(jnp.int32).reshape(1)
-    design_rows = design.reshape(components * length, wide)
     levels = length.bit_length() - 1
-    anywhere = pl.BlockSpec(memory_space=pl.ANY)
+    hbm = pl.BlockSpec(memory_space=pltpu.HBM)
     small = [
         segment_orders.T,
         jnp.transpose(pole_life, (1, 2, 0)),
@@ -456,12 +460,10 @@
         fir_taps,
     ]
 
-    (stacked, energy_own, live, rates, spread, steps, diagonal_parts, remaining_parts, search_own, current_own) = call(
+    (predicted, rates, spread, steps, diagonal_parts, remaining_parts, search_own, current_own) = call(
         functools.partial(prepare_kernel, width, classes, length),
         (
-            jax.ShapeDtypeStruct((3 * count, wide), BF16),
-            shape(count, LANES),
-            shape(length, LANES),
+            shape(length + count, LANES),
             shape(sections * (levels + 1) + taps_count, LANES),
             shape(length, LANES),
             shape(3 * SLOT, kinds * LANES),
@@ -472,41 +474,43 @@
         ),
         place,
         *small,
-        epoch_counts,
         solution,
         residual,
         direction,
         precond,
-        specs=[smem()] + [anywhere] * 9,
+        design[:, :, 0, :],
+        specs=[smem()] + [hbm] * 9,
         scratch=[pltpu.VMEM(each.shape, each.dtype) for each in small]
-        + [pltpu.SMEM((1,), jnp.int32)]
         + [pltpu.VMEM((count, wide), F32)] * 3
-        + [pltpu.VMEM((1, wide), F32), pltpu.SemaphoreType.DMA((9,))],
-    )
-    predicted = call(
-        predict_kernel, shape(length + count, LANES), stacked, energy_own, design_rows
+        + [pltpu.VMEM((1, wide), F32), pltpu.VMEM((components, length, wide), BF16)]
+        + [pltpu.SemaphoreType.DMA((8 + components,))],
     )
     arrived = over_order(predicted)
     send, keep, energy = call(
         functools.partial(filter_kernel, sections, taps_count, len(arrived)),
         (shape(blocks, SLOT, LANES), shape(length, LANES), shape(count, LANES)),
+        epoch_counts,
         rates,
-        live,
         *arrived,
+        specs=[smem()] + [vmem()] * (1 + len(arrived)),
     )
     everyone = lax.all_to_all(send, "tm", 0, 0)
     pieces = call(
         functools.partial(normal_kernel, kinds, width, classes),
         [shape(parts, count, padded)] * classes,
         place,
-        live,
+        epoch_counts,
         everyone,
         keep,
         spread,
         steps,
-        design_rows,
-        specs=[smem()] + [vmem()] * 6,
-        scratch=[pltpu.VMEM((blocks, SLOT, LANES), F32)],
+        design.reshape(components * length, wide),
+        specs=[smem()] * 2 + [vmem()] * 4 + [hbm],
+        scratch=[
+            pltpu.VMEM((blocks, SLOT, LANES), F32),
+            pltpu.VMEM((components * length, wide), BF16),
+            pltpu.SemaphoreType.DMA,
+        ],
     )
     arriving = [exchange(pieces[apart], "tm", apart) for apart in range(1, classes)]
     buffer = pieces[0] + sum(arriving[1:], arriving[0])

time: 61.7 us -> 55.2 us (0.89)
  local copies, waits for them, and re-layouts: 10.2 us -> 1.91 us
  Pallas kernels: 6.59 us -> 9.27 us
    unnamed x23 -> x3, local copies, waits for them, and re-layouts: 10.2 us -> 1.91 us
    pallas_call x5 -> x4, Pallas kernels: 6.59 us -> 9.27 us  [call(): pl.pallas_call(kernel, out_shape=outs, in_specs=specs or [vmem()] * len(a...]
    ppermute x9, waiting for transfers between devices: 18.6 us -> 18 us  [exchange(): return lax.ppermute(value, axis, [(at, at ^ bit) for at in range(size)])]
where the time goes in v3:
time: 55.2 us; the launch traced here: 55 us
  waiting for transfers between devices  18 us (33%)
  blocking collectives  15.8 us (29%)
  Pallas kernels  9.27 us (17%)
  starting transfers between devices  8.44 us (15%)
  local copies, waits for them, and re-layouts  1.91 us (3%)
  between operations  1.33 us (2%)
    ppermute x9, waiting for transfers between devices, exchange(): return lax.ppermute(value, axis, [(at, at ^ bit) for at in range(size)])  18 us
    all_to_all x1, blocking collectives, shards(): everyone = lax.all_to_all(send, 'tm', 0, 0)  15.8 us
    pallas_call x4, Pallas kernels, call(): pl.pallas_call(kernel, out_shape=outs, in_specs=specs or [vmem()] * len(a...  9.27 us
    ppermute x9, starting transfers between devices, exchange(): return lax.ppermute(value, axis, [(at, at ^ bit) for at in range(size)])  8.44 us
    unnamed x3, local copies, waits for them, and re-layouts  1.91 us
  transfers between devices with their start and end apart: 9, of which 7 were waited for; matrix products, arithmetic and copies ran while one was open for 2% of the time, Pallas kernels for 0%

profile of v3, /device:TPU:0, one launch (start us, length us, event | category | flops | bytes accessed | tf_op | source)
XLA Modules:
  0.0 55.0 jit_solution(8265775992345227964)
XLA Ops:
  0.6 4.6 %shard_map.121 = (f32[80,128]{1,0:T(8,128)S(1)}, f32[37,128]{1,0:T(8,128)S(1)}, f32[64,128]{1,0:T(8,128)S(1)}, f32[48,1536]{1,0:T(8,128)S(1)}, f32[4,16,384]{2,1...) custom-call(s32[1]{0:T(128)} %bitcast.refs_0_, s32[2,4]{1,0:T(2,128)} %bitcast.18, ...), custom_call_target="tpu_custom_call" | custom-call | tf_op jit(solution)/shard_map/pallas_call | solution.py:33
  5.2 0.5 collective-permute-start
  6.4 0.2 collective-permute-done.refs_3_
  6.6 0.4 shard_map.122
  7.0 15.8 %all_to_all.5.refs_2_ = f32[16,16,128]{2,1,0:T(8,128)S(1)} all-to-all(f32[16,16,128]{2,1,0:T(8,128)S(1)} %get-tuple-element.24), channel_id=1, replica_groups=mesh['tm'=16,'order'=2] {'tm'}, dimensions={0} | all-to-all | bytes 262144 | tf_op jit(solution)/shard_map/all_to_all | solution.py:497
  22.8 4.1 %shard_map.123 = (f32[4,16,384]{2,1,0:T(8,128)S(1)}, f32[4,16,384]{2,1,0:T(8,128)S(1)}, f32[4,16,384]{2,1,0:T(8,128)S(1)}, f32[4,16,384]{2,1,0:T(8,128)S(1)}) custom-call(s32[1]{0:T(128)} %bitcast.refs_0_, s32[1]{0:T(128)S(6)} %copy.19.refs_0_.refs_1_, f32[16,16,128]{2,1,0:T(8,128)S(1)} %all_to_all.5.refs_2_, f32[64,128]{1,0:T(8,128)S(1)} %get-tuple-element.25.refs_3_, ...), custom_call_target="tpu_custom_call" | custom-call | tf_op jit(solution)/shard_map/pallas_call | solution.py:33
  26.8 1.2 %collective-permute-start.1 = (f32[4,16,384]{2,1,0:T(8,128)S(1)}, f32[4,16,384]{2,1,0:T(8,128)S(1)}, u32[]{:S(2)}, u32[]{:S(2)}) collective-permute-start(f32[4,16,384]{2,1,0:T(8,128)S(1)} %get-tuple-element.29), channel_id=1, source_target_pairs={{0,2},{2,0},{4,6},{6,4},{8,10},{10,8},{12,14},{14,12},{16,18},{18,... | collective-permute-start | bytes 294920 | tf_op jit(solution)/shard_map/ppermute | solution.py:420
  28.0 0.2 collective-permute-start.2
  28.2 2.2 %collective-permute-start.3 = (f32[4,16,384]{2,1,0:T(8,128)S(1)}, f32[4,16,384]{2,1,0:T(8,128)S(1)}, u32[]{:S(2)}, u32[]{:S(2)}) collective-permute-start(f32[4,16,384]{2,1,0:T(8,128)S(1)} %get-tuple-element.31), channel_id=1, source_target_pairs={{0,6},{2,4},{4,2},{6,0},{8,14},{10,12},{12,10},{14,8},{16,22},{18,... | collective-permute-start | bytes 294920 | tf_op jit(solution)/shard_map/ppermute | solution.py:420
  30.4 2.1 %collective-permute-done.1 = f32[4,16,384]{2,1,0:T(8,128)S(1)} collective-permute-done((f32[4,16,384]{2,1,0:T(8,128)S(1)}, f32[4,16,384]{2,1,0:T(8,128)S(1)}, u32[]{:S(2)}, u32[]{:S(2)}) %collective-permute-start.1) | collective-permute-done | bytes 98336 | tf_op jit(solution)/shard_map/ppermute | solution.py:420
  32.5 1.4 %collective-permute-done.2 = f32[4,16,384]{2,1,0:T(8,128)S(1)} collective-permute-done((f32[4,16,384]{2,1,0:T(8,128)S(1)}, f32[4,16,384]{2,1,0:T(8,128)S(1)}, u32[]{:S(2)}, u32[]{:S(2)}) %collective-permute-start.2) | collective-permute-done | bytes 98336 | tf_op jit(solution)/shard_map/ppermute | solution.py:420
  33.9 0.0 collective-permute-done.3
  33.9 0.8 %collective-permute-start.4 = (f32[4,16,384]{2,1,0:T(8,128)S(1)}, f32[4,16,384]{2,1,0:T(8,128)S(1)}, u32[]{:S(2)}, u32[]{:S(2)}) collective-permute-start(f32[4,16,384]{2,1,0:T(8,128)S(1)} %add_add_fusion), channel_id=1, source_target_pairs={{0,8},{2,10},{4,12},{6,14},{8,0},{10,2},{12,4},{14,6},{16,24},{18,... | collective-permute-start | bytes 294920 | tf_op jit(solution)/shard_map/ppermute | solution.py:420
  34.7 3.9 %collective-permute-done.4 = f32[4,16,384]{2,1,0:T(8,128)S(1)} collective-permute-done((f32[4,16,384]{2,1,0:T(8,128)S(1)}, f32[4,16,384]{2,1,0:T(8,128)S(1)}, u32[]{:S(2)}, u32[]{:S(2)}) %collective-permute-start.4) | collective-permute-done | bytes 98336 | tf_op jit(solution)/shard_map/ppermute | solution.py:420
  38.6 0.9 %collective-permute-start.5 = (f32[4,16,384]{2,1,0:T(8,128)S(1)}, f32[4,16,384]{2,1,0:T(8,128)S(1)}, u32[]{:S(2)}, u32[]{:S(2)}) collective-permute-start(f32[4,16,384]{2,1,0:T(8,128)S(1)} %add.27.refs_1_), channel_id=1, source_target_pairs={{0,16},{2,18},{4,20},{6,22},{8,24},{10,26},{12,28},{14,30},{16,0},... | collective-permute-start | bytes 294920 | tf_op jit(solution)/shard_map/ppermute | solution.py:420
  39.5 5.7 %collective-permute-done.5.refs_2_ = f32[4,16,384]{2,1,0:T(8,128)S(1)} collective-permute-done((f32[4,16,384]{2,1,0:T(8,128)S(1)}, f32[4,16,384]{2,1,0:T(8,128)S(1)}, u32[]{:S(2)}, u32[]{:S(2)}) %collective-permute-start.5) | collective-permute-done | bytes 98336 | tf_op jit(solution)/shard_map/ppermute | solution.py:420
  45.3 0.3 shard_map.124
  45.5 1.3 %collective-permute-start.6 = (f32[16,128]{1,0:T(8,128)S(1)}, f32[16,128]{1,0:T(8,128)S(1)}, u32[]{:S(2)}, u32[]{:S(2)}) collective-permute-start(f32[16,128]{1,0:T(8,128)S(1)} %get-tuple-element.40), channel_id=1, source_target_pairs={{0,2},{2,0},{4,6},{6,4},{8,10},{10,8},{12,14},{14,12},{16,18},{18,... | collective-permute-start | bytes 24584 | tf_op jit(solution)/shard_map/ppermute | solution.py:420
  46.8 2.4 %collective-permute-done.6 = f32[16,128]{1,0:T(8,128)S(1)} collective-permute-done((f32[16,128]{1,0:T(8,128)S(1)}, f32[16,128]{1,0:T(8,128)S(1)}, u32[]{:S(2)}, u32[]{:S(2)}) %collective-permute-start.6) | collective-permute-done | bytes 8224 | tf_op jit(solution)/shard_map/ppermute | solution.py:420
  49.2 1.4 %collective-permute-start.7 = (f32[16,128]{1,0:T(8,128)S(1)}, f32[16,128]{1,0:T(8,128)S(1)}, u32[]{:S(2)}, u32[]{:S(2)}) collective-permute-start(f32[16,128]{1,0:T(8,128)S(1)} %add.28), channel_id=1, source_target_pairs={{0,4},{2,6},{4,0},{6,2},{8,12},{10,14},{12,8},{14,10},{16,20},{18,... | collective-permute-start | bytes 24584 | tf_op jit(solution)/shard_map/ppermute | solution.py:420
  50.6 2.2 %collective-permute-done.7 = f32[16,128]{1,0:T(8,128)S(1)} collective-permute-done((f32[16,128]{1,0:T(8,128)S(1)}, f32[16,128]{1,0:T(8,128)S(1)}, u32[]{:S(2)}, u32[]{:S(2)}) %collective-permute-start.7) | collective-permute-done | bytes 8224 | tf_op jit(solution)/shard_map/ppermute | solution.py:420
  52.8 0.0 collective-permute-start.8
  52.9 0.6 %copy.17 = f32[16,1,360]{2,1,0:T(1,128)} copy(f32[16,1,360]{2,0,1:T(8,128)S(1)} %get-tuple-element.47) | data formatting | bytes 46080
  53.5 0.6 %copy.16 = f32[16,1,360]{2,1,0:T(1,128)} copy(f32[16,1,360]{2,0,1:T(8,128)S(1)} %get-tuple-element.48) | data formatting | bytes 46080
  54.1 0.0 collective-permute-done.8
  54.1 0.1 fusion.1
  54.2 0.1 fusion
  54.3 0.6 %copy.18 = f32[16,1,360]{2,1,0:T(1,128)} copy(f32[16,1,360]{2,0,1:T(8,128)S(1)} %fusion) | data formatting | bytes 46080
  (5 shorter events, 0.0 us)
Async XLA Ops:
  5.2 1.4 %collective-permute-start = (f32[80,128]{1,0:T(8,128)S(1)}, f32[80,128]{1,0:T(8,128)S(1)}, u32[]{:S(2)}, u32[]{:S(2)}) collective-permute-start(f32[80,128]{1,0:T(8,128)S(1)} %get-tuple-element.23.refs_2_), channel_id=1, source_target_pairs={{0,1},{1,0},{2,3},{3,2},{4,5},{5,4},{6,7},{7,6},{8,9},{9,8},{10,11... | collective-permute-start | bytes 122888 | tf_op jit(solution)/shard_map/ppermute | solution.py:420
  26.8 5.7 %collective-permute-start.1 = (f32[4,16,384]{2,1,0:T(8,128)S(1)}, f32[4,16,384]{2,1,0:T(8,128)S(1)}, u32[]{:S(2)}, u32[]{:S(2)}) collective-permute-start(f32[4,16,384]{2,1,0:T(8,128)S(1)} %get-tuple-element.29), channel_id=1, source_target_pairs={{0,2},{2,0},{4,6},{6,4},{8,10},{10,8},{12,14},{14,12},{16,18},{18,... | collective-permute-start | bytes 294920 | tf_op jit(solution)/shard_map/ppermute | solution.py:420
  28.0 5.9 %collective-permute-start.2 = (f32[4,16,384]{2,1,0:T(8,128)S(1)}, f32[4,16,384]{2,1,0:T(8,128)S(1)}, u32[]{:S(2)}, u32[]{:S(2)}) collective-permute-start(f32[4,16,384]{2,1,0:T(8,128)S(1)} %get-tuple-element.30), channel_id=1, source_target_pairs={{0,4},{2,6},{4,0},{6,2},{8,12},{10,14},{12,8},{14,10},{16,20},{18,... | collective-permute-start | bytes 294920 | tf_op jit(solution)/shard_map/ppermute | solution.py:420
  28.2 5.7 %collective-permute-start.3 = (f32[4,16,384]{2,1,0:T(8,128)S(1)}, f32[4,16,384]{2,1,0:T(8,128)S(1)}, u32[]{:S(2)}, u32[]{:S(2)}) collective-permute-start(f32[4,16,384]{2,1,0:T(8,128)S(1)} %get-tuple-element.31), channel_id=1, source_target_pairs={{0,6},{2,4},{4,2},{6,0},{8,14},{10,12},{12,10},{14,8},{16,22},{18,... | collective-permute-start | bytes 294920 | tf_op jit(solution)/shard_map/ppermute | solution.py:420
  33.9 4.7 %collective-permute-start.4 = (f32[4,16,384]{2,1,0:T(8,128)S(1)}, f32[4,16,384]{2,1,0:T(8,128)S(1)}, u32[]{:S(2)}, u32[]{:S(2)}) collective-permute-start(f32[4,16,384]{2,1,0:T(8,128)S(1)} %add_add_fusion), channel_id=1, source_target_pairs={{0,8},{2,10},{4,12},{6,14},{8,0},{10,2},{12,4},{14,6},{16,24},{18,... | collective-permute-start | bytes 294920 | tf_op jit(solution)/shard_map/ppermute | solution.py:420
  38.6 6.6 %collective-permute-start.5 = (f32[4,16,384]{2,1,0:T(8,128)S(1)}, f32[4,16,384]{2,1,0:T(8,128)S(1)}, u32[]{:S(2)}, u32[]{:S(2)}) collective-permute-start(f32[4,16,384]{2,1,0:T(8,128)S(1)} %add.27.refs_1_), channel_id=1, source_target_pairs={{0,16},{2,18},{4,20},{6,22},{8,24},{10,26},{12,28},{14,30},{16,0},... | collective-permute-start | bytes 294920 | tf_op jit(solution)/shard_map/ppermute | solution.py:420
  45.5 3.7 %collective-permute-start.6 = (f32[16,128]{1,0:T(8,128)S(1)}, f32[16,128]{1,0:T(8,128)S(1)}, u32[]{:S(2)}, u32[]{:S(2)}) collective-permute-start(f32[16,128]{1,0:T(8,128)S(1)} %get-tuple-element.40), channel_id=1, source_target_pairs={{0,2},{2,0},{4,6},{6,4},{8,10},{10,8},{12,14},{14,12},{16,18},{18,... | collective-permute-start | bytes 24584 | tf_op jit(solution)/shard_map/ppermute | solution.py:420
  49.2 3.7 %collective-permute-start.7 = (f32[16,128]{1,0:T(8,128)S(1)}, f32[16,128]{1,0:T(8,128)S(1)}, u32[]{:S(2)}, u32[]{:S(2)}) collective-permute-start(f32[16,128]{1,0:T(8,128)S(1)} %add.28), channel_id=1, source_target_pairs={{0,4},{2,6},{4,0},{6,2},{8,12},{10,14},{12,8},{14,10},{16,20},{18,... | collective-permute-start | bytes 24584 | tf_op jit(solution)/shard_map/ppermute | solution.py:420
  52.8 1.3 %collective-permute-start.8 = (f32[16,128]{1,0:T(8,128)S(1)}, f32[16,128]{1,0:T(8,128)S(1)}, u32[]{:S(2)}, u32[]{:S(2)}) collective-permute-start(f32[16,128]{1,0:T(8,128)S(1)} %add.29), channel_id=1, source_target_pairs={{0,1},{1,0},{2,3},{3,2},{4,5},{5,4},{6,7},{7,6},{8,9},{9,8},{10,11... | collective-permute-start | bytes 24584 | tf_op jit(solution)/shard_map/ppermute | solution.py:420

commit v4 on v3

--- a/solution.py
+++ b/solution.py
@@ -34,7 +34,9 @@
         kernel,
         out_shape=outs,
         in_specs=specs or [vmem()] * len(args),
-        out_specs=jax.tree.map(lambda _: vmem(), outs),
+        out_specs=jax.tree.map(
+            lambda out: pl.BlockSpec(memory_space=getattr(out, "memory_space", pltpu.VMEM)), outs
+        ),
         scratch_shapes=scratch,
         compiler_params=pltpu.CompilerParams(vmem_limit_bytes=VMEM_LIMIT),
     )(*args)
@@ -42,6 +44,15 @@
 
 def shape(*dims):
     return jax.ShapeDtypeStruct(dims, F32)
+
+
+def column_block(source_ref, block, width, padded):
+    wide = source_ref.shape[-1]
+    window = min(padded + LANES, wide)
+    start = block * width
+    base = jnp.minimum(start // LANES * LANES, wide - window)
+    part = source_ref[:, pl.ds(pl.multiple_of(base, LANES), window)]
+    return pltpu.roll(part, (window - (start - base)) % window, 1)[:, :padded]
 
 
 def rows_of(value):
@@ -138,28 +149,24 @@
     return (poles, zeros, rows[sections * (levels + 1) :])
 
 
-def prepare_kernel(width, first_bits, length, *refs):
-    place_ref, orders_hbm, lives_hbm, ratios_hbm, taps_hbm = refs[:5]
-    vectors_hbm, diagonal_hbm, design_hbm = (refs[5:8], refs[8], refs[9])
-    outs, scratch = (refs[10:18], refs[18:])
-    predicted_ref, rates_ref, spread_ref, steps_ref = outs[:4]
-    slices = outs[4:]
-    orders_ref, lives_ref, ratios_ref, taps_ref = scratch[:4]
-    current_ref, remaining_ref, search_ref, diagonal_ref, design_ref, sems = scratch[4:]
-    components = design_ref.shape[0]
+def predict_kernel(*refs):
+    orders_hbm, lives_hbm, ratios_hbm, taps_hbm = refs[:4]
+    residual_hbm, direction_hbm, diagonal_hbm, design_hbm = refs[4:8]
+    predicted_ref, rates_ref, design_ref = refs[8:11]
+    orders_ref, lives_ref, ratios_ref, taps_ref, remaining_ref, search_ref, diagonal_ref, sems = refs[11:]
+    components, length, _ = design_ref.shape
     copies = [
         pltpu.make_async_copy(source, target, sems.at[at])
         for at, (source, target) in enumerate(
             [
+                (direction_hbm.at[:, 0, :], search_ref),
                 (orders_hbm, orders_ref),
                 (lives_hbm, lives_ref),
                 (ratios_hbm, ratios_ref),
                 (taps_hbm, taps_ref),
-                (vectors_hbm[2].at[:, 0, :], search_ref),
                 *[(design_hbm.at[at], design_ref.at[at]) for at in range(components)],
-                (vectors_hbm[1].at[:, 0, :], remaining_ref),
+                (residual_hbm.at[:, 0, :], remaining_ref),
                 (diagonal_hbm, diagonal_ref),
-                (vectors_hbm[0].at[:, 0, :], current_ref),
             ]
         )
     ]
@@ -169,9 +176,7 @@
     segments, sections_each, _ = lives_ref.shape
     sections = segments * sections_each
     taps_count = taps_ref.shape[1]
-    reach = taps_count - 1
-    kinds = sections + reach
-    for copy in copies[:4]:
+    for copy in copies[1:5]:
         copy.wait()
     lane = lax.broadcasted_iota(jnp.int32, (components, LANES), 1)
     component = lax.broadcasted_iota(jnp.int32, (components, LANES), 0)
@@ -200,39 +205,16 @@
     pole_rate = jnp.where(active, pole_all, 0.0)
     zero_rate = jnp.where(active, 1.0 - ratio * (1.0 - pole_all), 0.0)
     levels = length.bit_length() - 1
-    table = []
-    for section in range(sections):
-        power = pole_rate[section : section + 1]
-        for _ in range(levels):
-            table.append(power)
-            power = power * power
-    table = table + [zero_rate[section : section + 1] for section in range(sections)]
-    table = table + [tap_rows[tap : tap + 1] for tap in range(taps_count)]
-    for at, row in enumerate(table):
-        rates_ref[at : at + 1, :] = row
-    poles = [table[at * levels : (at + 1) * levels] for at in range(sections)]
-    zeros = table[sections * levels : sections * (levels + 1)]
-    taps = table[sections * (levels + 1) :]
-
-    lane = lax.broadcasted_iota(jnp.int32, (1, LANES), 1)
-    slot = jnp.where(lane >= half, lane % SLOT, SLOT)
-    units = [jnp.where(slot == at, 1.0, 0.0) for at in range(kinds)]
-    rows = lax.broadcasted_iota(jnp.int32, (reach, LANES), 0)
-    history = jnp.where(slot == kinds - 1 - rows, 1.0, 0.0)
-    nothing = jnp.zeros((length, LANES), F32)
-    filtered, ends = forward_block(nothing, units[: sections + 1], history, poles, zeros, taps)
-    local, heads = backward_block(filtered, None, poles, zeros, taps)
-    reply, replies = backward_block(nothing, units, poles, zeros, taps)
-    spread_ref[...] = jnp.where(lane < half, pltpu.roll(local, half, 1), reply)
-    stacked = jnp.concatenate([pack(ends), pack(heads), pack(replies)], axis=0)
-    source = lax.broadcasted_iota(jnp.int32, (LANES, kinds * LANES), 0)
-    target = lax.broadcasted_iota(jnp.int32, (LANES, kinds * LANES), 1)
-    within = target % LANES
-    wanted = half + within // SLOT * SLOT + target // LANES
-    pick = jnp.where((within < half) & (source == wanted), 1.0, 0.0)
-    steps_ref[...] = jnp.dot(stacked, pick, precision=HIGHEST, preferred_element_type=F32)
-
-    copies[4].wait()
+    power = pole_rate
+    for level in range(levels):
+        for section in range(sections):
+            at = section * levels + level
+            rates_ref[at : at + 1, :] = power[section : section + 1]
+        power = power * power
+    rates_ref[sections * levels : sections * (levels + 1), :] = zero_rate
+    rates_ref[sections * (levels + 1) : sections * (levels + 1) + taps_count, :] = tap_rows
+
+    copies[0].wait()
     search = search_ref[...]
     high = search.astype(BF16)
     rest = search - high.astype(F32)
@@ -253,20 +235,65 @@
     remaining = remaining_ref[...]
     energy = jnp.sum(remaining * diagonal_ref[...] * remaining, axis=1, keepdims=True)
     predicted_ref[length:, :] = jnp.broadcast_to(energy, (count, LANES))
-    sources = [diagonal_ref, remaining_ref, search_ref, current_ref]
-    cut_slices(width, first_bits, place_ref[0], sources, slices)
-
-
-def filter_kernel(sections, taps_count, parts, *refs):
+
+
+def tables_kernel(width, first_bits, sections, taps_count, length, *refs):
+    place_ref, rates_ref, keep_hbm = refs[:3]
+    vectors_hbm, diagonal_hbm = (refs[3:6], refs[6])
+    spread_ref, steps_ref, energy_ref = refs[7:10]
+    slices = refs[10:14]
+    current_ref, remaining_ref, search_ref, diagonal_ref, sems = refs[14:]
+    sources = [current_ref, remaining_ref, search_ref]
+    copies = [
+        pltpu.make_async_copy(vector.at[:, 0, :], target, sems.at[at])
+        for at, (vector, target) in enumerate(zip(vectors_hbm, sources))
+    ]
+    copies.append(pltpu.make_async_copy(diagonal_hbm, diagonal_ref, sems.at[len(sources)]))
+    tail = keep_hbm.at[pl.ds(length, energy_ref.shape[0]), :]
+    copies.append(pltpu.make_async_copy(tail, energy_ref, sems.at[len(sources) + 1]))
+    for copy in copies:
+        copy.start()
+    half = LANES // 2
+    reach = taps_count - 1
+    kinds = sections + reach
+    poles, zeros, taps = rates_of(rates_ref, sections, taps_count, length.bit_length() - 1)
+    lane = lax.broadcasted_iota(jnp.int32, (1, LANES), 1)
+    slot = jnp.where(lane >= half, lane % SLOT, SLOT)
+    units = [jnp.where(slot == at, 1.0, 0.0) for at in range(kinds)]
+    rows = lax.broadcasted_iota(jnp.int32, (reach, LANES), 0)
+    history = jnp.where(slot == kinds - 1 - rows, 1.0, 0.0)
+    nothing = jnp.zeros((length, LANES), F32)
+    filtered, ends = forward_block(nothing, units[: sections + 1], history, poles, zeros, taps)
+    local, heads = backward_block(filtered, None, poles, zeros, taps)
+    reply, replies = backward_block(nothing, units, poles, zeros, taps)
+    spread_ref[...] = jnp.where(lane < half, pltpu.roll(local, half, 1), reply)
+    stacked = jnp.concatenate([pack(ends), pack(heads), pack(replies)], axis=0)
+    source = lax.broadcasted_iota(jnp.int32, (LANES, kinds * LANES), 0)
+    target = lax.broadcasted_iota(jnp.int32, (LANES, kinds * LANES), 1)
+    within = target % LANES
+    wanted = half + within // SLOT * SLOT + target // LANES
+    pick = jnp.where((within < half) & (source == wanted), 1.0, 0.0)
+    steps_ref[...] = jnp.dot(stacked, pick, precision=HIGHEST, preferred_element_type=F32)
+    for copy in copies:
+        copy.wait()
+    mine = place_ref[0]
+    vectors = [diagonal_ref, remaining_ref, search_ref, current_ref]
+    for source_ref, target_ref in zip(vectors, slices):
+        for at in range(target_ref.shape[0]):
+            block = mine if target_ref.shape[0] == 1 else at * first_bits + mine % first_bits
+            part = column_block(source_ref, block, width, target_ref.shape[2])
+            target_ref[at] = jnp.broadcast_to(part, target_ref.shape[1:])
+
+
+def filter_kernel(sections, taps_count, length, parts, *refs):
     counts_ref, rates_ref = refs[:2]
     gathered = refs[2 : 2 + parts]
-    send_ref, keep_ref, energy_ref = refs[2 + parts :]
-    length = keep_ref.shape[0]
+    send_ref, keep_hbm, keep_ref, sem = refs[2 + parts :]
     half = LANES // 2
     received = gathered[0][...]
     for other in gathered[1:]:
         received = received + other[...]
-    energy_ref[...] = received[length:]
+    keep_ref[length:, :] = received[length:]
     received = received[:length]
     low_half = lax.broadcasted_iota(jnp.int32, (1, LANES), 1) < half
     data = jnp.where(low_half & (rows_of(received) < counts_ref[0]), received, 0.0)
@@ -277,25 +304,16 @@
     sent = jnp.where(low_half, pack(ends), pltpu.roll(pack(heads), half, 1))
     for block in range(send_ref.shape[0]):
         send_ref[block] = sent
-    keep_ref[...] = jnp.where(low_half, local, received + pltpu.roll(received, half, 1))
-
-
-def blocks_of(value, width, padded):
-    wide = value.shape[1]
-    window = min(padded + LANES, wide)
-    for block in range(wide // width):
-        start = block * width
-        base = min(start // LANES * LANES, wide - window)
-        part = value[:, base : base + window]
-        if start != base:
-            part = pltpu.roll(part, window - (start - base), 1)
-        yield part[:, :padded]
+    keep_ref[:length, :] = jnp.where(low_half, local, received + pltpu.roll(received, half, 1))
+    copy = pltpu.make_async_copy(keep_ref, keep_hbm, sem)
+    copy.start()
+    copy.wait()
 
 
 def normal_kernel(kinds, width, first_bits, *refs):
-    place_ref, counts_ref, all_ref, keep_ref, spread_ref, steps_ref, design_hbm = refs[:7]
-    out_refs, (entering_ref, design_ref, sem) = (refs[7:-3], refs[-3:])
-    fetch = pltpu.make_async_copy(design_hbm, design_ref, sem)
+    place_ref, counts_ref, all_ref, keep_hbm, spread_ref, steps_ref, design_ref = refs[:7]
+    out_refs, (entering_ref, normal_ref, keep_ref, sem) = (refs[7:-4], refs[-4:])
+    fetch = pltpu.make_async_copy(keep_hbm.at[pl.ds(0, keep_ref.shape[0]), :], keep_ref, sem)
     fetch.start()
     blocks = all_ref.shape[0]
     mine = place_ref[0]
@@ -338,6 +356,7 @@
         precision=HIGHEST,
         preferred_element_type=F32,
     )
+    fetch.wait()
     kept = keep_ref[...]
     live = (row < counts_ref[0]) & (lane < half)
     weighted = jnp.where(live, kept + correction, 0.0)
@@ -358,35 +377,17 @@
     curvature = curve[:count]
     for at in range(1, half // count):
         curvature = curvature + curve[at * count : (at + 1) * count]
-    fetch.wait()
-    normal = jnp.dot(low, design_ref[...], preferred_element_type=F32)
+    rows = jnp.concatenate([design_ref[at] for at in range(design_ref.shape[0])], axis=0)
+    normal_ref[...] = jnp.dot(low, rows, preferred_element_type=F32)
     padded = out_refs[0].shape[-1]
     column = lax.broadcasted_iota(jnp.int32, (count, padded), 1)
     curvature = jnp.broadcast_to(curvature[:, :1], (count, padded))
     low_bits = mine % first_bits
-    for block, part in enumerate(blocks_of(normal, width, padded)):
-        part = jnp.where(column < width, part, curvature)
-        for apart, out_ref in enumerate(out_refs):
-
-            @pl.when((low_bits ^ apart) == block % first_bits)
-            def _(out_ref=out_ref, part=part, block=block):
-                out_ref[block // first_bits] = part
-
-
-def cut_slices(width, first_bits, mine, sources, targets):
-    low = mine % first_bits
-    for source_ref, target_ref in zip(sources, targets):
-        wide = source_ref.shape[-1]
-        padded = target_ref.shape[-1]
-        window = min(padded + LANES, wide)
-        for at in range(target_ref.shape[0]):
-            block = at * first_bits + low if target_ref.shape[0] > 1 else mine
-            start = block * width
-            base = jnp.minimum(start // LANES * LANES, wide - window)
-            part = source_ref[:, pl.ds(pl.multiple_of(base, LANES), window)]
-            part = jnp.broadcast_to(part, (target_ref.shape[1], window))
-            moved = pltpu.roll(part, (window - (start - base)) % window, 1)
-            target_ref[at] = moved[:, :padded]
+    for apart, out_ref in enumerate(out_refs):
+        for at in range(out_ref.shape[0]):
+            block = at * first_bits + (low_bits ^ apart)
+            part = column_block(normal_ref, block, width, padded)
+            out_ref[at] = jnp.where(column < width, part, curvature)
 
 
 def update_kernel(width, first_bits, *refs):
@@ -460,41 +461,56 @@
         fir_taps,
     ]
 
-    (predicted, rates, spread, steps, diagonal_parts, remaining_parts, search_own, current_own) = call(
-        functools.partial(prepare_kernel, width, classes, length),
+    predicted, rates, design_kept = call(
+        predict_kernel,
         (
             shape(length + count, LANES),
             shape(sections * (levels + 1) + taps_count, LANES),
+            jax.ShapeDtypeStruct((components, length, wide), BF16),
+        ),
+        *small,
+        residual,
+        direction,
+        precond,
+        design[:, :, 0, :],
+        specs=[hbm] * 8,
+        scratch=[pltpu.VMEM(each.shape, each.dtype) for each in small]
+        + [pltpu.VMEM((count, wide), F32)] * 2
+        + [pltpu.VMEM((1, wide), F32), pltpu.SemaphoreType.DMA((7 + components,))],
+    )
+    arrived = over_order(predicted)
+    send, keep = call(
+        functools.partial(filter_kernel, sections, taps_count, length, len(arrived)),
+        (shape(blocks, SLOT, LANES), pltpu.HBM((length + count, LANES), F32)),
+        epoch_counts,
+        rates,
+        *arrived,
+        specs=[smem()] + [vmem()] * (1 + len(arrived)),
+        scratch=[pltpu.VMEM((length + count, LANES), F32), pltpu.SemaphoreType.DMA],
+    )
+    everyone = lax.all_to_all(send, "tm", 0, 0)
+    spread, steps, energy, diagonal_parts, remaining_parts, search_own, current_own = call(
+        functools.partial(tables_kernel, width, classes, sections, taps_count, length),
+        (
             shape(length, LANES),
             shape(3 * SLOT, kinds * LANES),
+            shape(count, LANES),
             shape(parts, count, padded),
             shape(parts, count, padded),
             shape(1, count, padded),
             shape(1, count, padded),
         ),
         place,
-        *small,
+        rates,
+        keep,
         solution,
         residual,
         direction,
         precond,
-        design[:, :, 0, :],
-        specs=[smem()] + [hbm] * 9,
-        scratch=[pltpu.VMEM(each.shape, each.dtype) for each in small]
-        + [pltpu.VMEM((count, wide), F32)] * 3
-        + [pltpu.VMEM((1, wide), F32), pltpu.VMEM((components, length, wide), BF16)]
-        + [pltpu.SemaphoreType.DMA((8 + components,))],
-    )
-    arrived = over_order(predicted)
-    send, keep, energy = call(
-        functools.partial(filter_kernel, sections, taps_count, len(arrived)),
-        (shape(blocks, SLOT, LANES), shape(length, LANES), shape(count, LANES)),
-        epoch_counts,
-        rates,
-        *arrived,
-        specs=[smem()] + [vmem()] * (1 + len(arrived)),
-    )
-    everyone = lax.all_to_all(send, "tm", 0, 0)
+        specs=[smem(), vmem()] + [hbm] * 5,
+        scratch=[pltpu.VMEM((count, wide), F32)] * 3
+        + [pltpu.VMEM((1, wide), F32), pltpu.SemaphoreType.DMA((5,))],
+    )
     pieces = call(
         functools.partial(normal_kernel, kinds, width, classes),
         [shape(parts, count, padded)] * classes,
@@ -504,19 +520,20 @@
         keep,
         spread,
         steps,
-        design.reshape(components * length, wide),
-        specs=[smem()] * 2 + [vmem()] * 4 + [hbm],
+        design_kept,
+        specs=[smem()] * 2 + [vmem(), hbm] + [vmem()] * 3,
         scratch=[
             pltpu.VMEM((blocks, SLOT, LANES), F32),
-            pltpu.VMEM((components * length, wide), BF16),
+            pltpu.VMEM((count, wide), F32),
+            pltpu.VMEM((length, LANES), F32),
             pltpu.SemaphoreType.DMA,
         ],
     )
     arriving = [exchange(pieces[apart], "tm", apart) for apart in range(1, classes)]
     buffer = pieces[0] + sum(arriving[1:], arriving[0])
     for bit in range(halved, bits - 1):
-        buffer = buffer + exchange(buffer, "tm", 1 << bit)
-    arriving = exchange(buffer, "tm", 1 << bits - 1)
+        buffer = buffer + exchange(buffer, "tm", (2 << bit) - classes)
+    arriving = exchange(buffer, "tm", blocks - classes)
     share, new_solution, new_residual, conditioned = call(
         functools.partial(update_kernel, width, classes),
         (

time: 55.2 us -> 54.1 us (0.980)
  blocking collectives: 15.8 us -> 0 us
  starting transfers between devices: 8.44 us -> 17.6 us
  waiting for transfers between devices: 18 us -> 21.4 us
  local copies, waits for them, and re-layouts: 1.91 us -> 3.77 us
    all_to_all x1 -> x0, blocking collectives: 15.8 us -> none  [shards(): everyone = lax.all_to_all(send, 'tm', 0, 0)]
    all_to_all x0 -> x1, starting transfers between devices: none -> 8.22 us  [shards(): everyone = lax.all_to_all(send, 'tm', 0, 0)]
    all_to_all x0 -> x1, waiting for transfers between devices: none -> 4.52 us  [shards(): everyone = lax.all_to_all(send, 'tm', 0, 0)]
    unnamed x3 -> x15, local copies, waits for them, and re-layouts: 1.91 us -> 3.77 us
    ppermute x9, waiting for transfers between devices: 18 us -> 16.9 us  [exchange(): return lax.ppermute(value, axis, [(at, at ^ bit) for at in range(size)])]
    ppermute x9, starting transfers between devices: 8.44 us -> 9.35 us  [exchange(): return lax.ppermute(value, axis, [(at, at ^ bit) for at in range(size)])]
    pallas_call x4 -> x5, Pallas kernels: 9.27 us -> 9.36 us  [call(): pl.pallas_call(kernel, out_shape=outs, in_specs=specs or [vmem()] * len(a...]
  transfers between devices with their start and end apart: 9 -> 10, of which waited for: 7 -> 8; matrix products, arithmetic and copies ran while one was open for 2% -> 2% of each run, Pallas kernels for 0% -> 3%
where the time goes in v4:
time: 54.1 us; the launch traced here: 53.8 us
  waiting for transfers between devices  21.4 us (40%)
  starting transfers between devices  17.6 us (33%)
  Pallas kernels  9.36 us (17%)
  local copies, waits for them, and re-layouts  3.77 us (7%)
  between operations  1.37 us (3%)
    ppermute x9, waiting for transfers between devices, exchange(): return lax.ppermute(value, axis, [(at, at ^ bit) for at in range(size)])  16.9 us
    pallas_call x5, Pallas kernels, call(): pl.pallas_call(kernel, out_shape=outs, in_specs=specs or [vmem()] * len(a...  9.36 us
    ppermute x9, starting transfers between devices, exchange(): return lax.ppermute(value, axis, [(at, at ^ bit) for at in range(size)])  9.35 us
    all_to_all x1, starting transfers between devices, shards(): everyone = lax.all_to_all(send, 'tm', 0, 0)  8.22 us
    all_to_all x1, waiting for transfers between devices, shards(): everyone = lax.all_to_all(send, 'tm', 0, 0)  4.52 us
    unnamed x15, local copies, waits for them, and re-layouts  3.77 us
  transfers between devices with their start and end apart: 10, of which 8 were waited for; matrix products, arithmetic and copies ran while one was open for 2% of the time, Pallas kernels for 3%

profile of v4, /device:TPU:0, one launch (start us, length us, event | category | flops | bytes accessed | tf_op | source)
XLA Modules:
  0.0 53.8 jit_solution(4719765990262146781)
XLA Ops:
  0.6 3.9 %shard_map.121 = (f32[80,128]{1,0:T(8,128)S(1)}, f32[37,128]{1,0:T(8,128)S(1)}, bf16[4,64,5760]{2,1,0:T(8,128)(2,1)S(1)}) custom-call(s32[2,4]{1,0:T(2,128)} %bitcast.16, f32[2,2,4]{2,1,0:T(2,128)} %bitcast.14, f32[2,2,4]{2,1,0:T(2,128)} %bitcast.15, f32[4,9]{1,0:T(4,128)} %refs_3_.2, f32[16,1,5760]{2,1,0:T(1,128)} %refs_4_.3, f32[16,1,5760]{2,1,0:T(1,128)} %refs_5_.3, ...), custom_call_target="tpu_custom_call" | custom-call | tf_op jit(solution)/shard_map/pallas_call | solution.py:33
  4.5 0.5 collective-permute-start
  5.7 0.2 collective-permute-done.refs_3_
  5.9 1.6 %shard_map.122 = (f32[16,16,128]{2,1,0:T(8,128)}, f32[80,128]{1,0:T(8,128)}) custom-call(s32[1]{0:T(128)S(6)} %copy.19.refs_0_.refs_1_, f32[37,128]{1,0:T(8,128)S(1)} %get-tuple-element.23.refs_1_, f32[80,128]{1,0:T(8,128)S(1)} %get-tuple-element.24.refs_2_, f32[80,128]{1,0:T(8,128)S(1)} %collective-permute-done.refs_3_), custom_call_target="tpu_custom_call" | custom-call | tf_op jit(solution)/shard_map/pallas_call | solution.py:33
  7.5 8.2 %all-to-all-start = ((f32[16,16,128]{2,1,0:T(8,128)}), f32[16,16,128]{2,1,0:T(8,128)S(1)}, u32[]{:S(2)}, u32[]{:S(2)}) async-start(f32[16,16,128]{2,1,0:T(8,128)} %get-tuple-element.25), calls=%async_computation | async-start | bytes 262144 | tf_op jit(solution)/shard_map/all_to_all | solution.py:491
  15.7 1.4 %shard_map.123 = (f32[64,128]{1,0:T(8,128)S(1)}, f32[48,1536]{1,0:T(8,128)S(1)}, f32[16,128]{1,0:T(8,128)S(1)}, f32[4,16,384]{2,1,0:T(8,128)S(1)}, f32[4,16,384]...) custom-call(s32[1]{0:T(128)} %bitcast.refs_0_, f32[37,128]{1,0:T(8,128)S(1)} %get-tuple-element.23.refs_1_, ...), custom_call_target="tpu_custom_call" | custom-call | tf_op jit(solution)/shard_map/pallas_call | solution.py:33
  17.1 0.0 copy-start
  17.1 0.6 %copy-done = f32[4,16,384]{2,1,0:T(8,128)} copy-done((f32[4,16,384]{2,1,0:T(8,128)}, f32[4,16,384]{2,1,0:T(8,128)S(1)}, u32[]{:S(2)}) %copy-start) | copy-done | bytes 98328
  17.8 0.0 copy-start.2
  17.8 0.6 %copy-done.2 = f32[16,128]{1,0:T(8,128)} copy-done((f32[16,128]{1,0:T(8,128)}, f32[16,128]{1,0:T(8,128)S(1)}, u32[]{:S(2)}) %copy-start.2) | copy-done | bytes 8216
  18.4 0.0 copy-start.4
  18.4 0.6 %copy-done.4 = f32[1,16,384]{2,1,0:T(8,128)} copy-done((f32[1,16,384]{2,1,0:T(8,128)}, f32[1,16,384]{2,1,0:T(8,128)S(1)}, u32[]{:S(2)}) %copy-start.4) | copy-done | bytes 24600
  19.0 4.5 %all-to-all-done.refs_2_ = f32[16,16,128]{2,1,0:T(8,128)S(1)} async-done(((f32[16,16,128]{2,1,0:T(8,128)}), f32[16,16,128]{2,1,0:T(8,128)S(1)}, u32[]{:S(2)}, u32[]{:S(2)}) %all-to-all-start) | async-done | bytes 131104 | tf_op jit(solution)/shard_map/all_to_all | solution.py:491
  23.5 0.0 copy-start.1
  23.5 0.0 copy-start.3
  23.5 0.0 copy-start.5
  23.5 2.3 %shard_map.124 = (f32[4,16,384]{2,1,0:T(8,128)S(1)}, f32[4,16,384]{2,1,0:T(8,128)S(1)}, f32[4,16,384]{2,1,0:T(8,128)S(1)}, f32[4,16,384]{2,1,0:T(8,128)S(1)}) custom-call(s32[1]{0:T(128)} %bitcast.refs_0_, s32[1]{0:T(128)S(6)} %copy.19.refs_0_.refs_1_, f32[16,16,128]{2,1,0:T(8,128)S(1)} %all-to-all-done.refs_2_, ...), custom_call_target="tpu_custom_call" | custom-call | tf_op jit(solution)/shard_map/pallas_call | solution.py:33
  25.8 1.2 %collective-permute-start.1 = (f32[4,16,384]{2,1,0:T(8,128)S(1)}, f32[4,16,384]{2,1,0:T(8,128)S(1)}, u32[]{:S(2)}, u32[]{:S(2)}) collective-permute-start(f32[4,16,384]{2,1,0:T(8,128)S(1)} %get-tuple-element.31), channel_id=1, source_target_pairs={{0,2},{2,0},{4,6},{6,4},{8,10},{10,8},{12,14},{14,12},{16,18},{18,... | collective-permute-start | bytes 294920 | tf_op jit(solution)/shard_map/ppermute | solution.py:421
  26.9 0.2 collective-permute-start.2
  27.1 2.2 %collective-permute-start.3 = (f32[4,16,384]{2,1,0:T(8,128)S(1)}, f32[4,16,384]{2,1,0:T(8,128)S(1)}, u32[]{:S(2)}, u32[]{:S(2)}) collective-permute-start(f32[4,16,384]{2,1,0:T(8,128)S(1)} %get-tuple-element.33), channel_id=1, source_target_pairs={{0,6},{2,4},{4,2},{6,0},{8,14},{10,12},{12,10},{14,8},{16,22},{18,... | collective-permute-start | bytes 294920 | tf_op jit(solution)/shard_map/ppermute | solution.py:421
  29.3 2.1 %collective-permute-done.1 = f32[4,16,384]{2,1,0:T(8,128)S(1)} collective-permute-done((f32[4,16,384]{2,1,0:T(8,128)S(1)}, f32[4,16,384]{2,1,0:T(8,128)S(1)}, u32[]{:S(2)}, u32[]{:S(2)}) %collective-permute-start.1) | collective-permute-done | bytes 98336 | tf_op jit(solution)/shard_map/ppermute | solution.py:421
  31.4 1.4 %collective-permute-done.2 = f32[4,16,384]{2,1,0:T(8,128)S(1)} collective-permute-done((f32[4,16,384]{2,1,0:T(8,128)S(1)}, f32[4,16,384]{2,1,0:T(8,128)S(1)}, u32[]{:S(2)}, u32[]{:S(2)}) %collective-permute-start.2) | collective-permute-done | bytes 98336 | tf_op jit(solution)/shard_map/ppermute | solution.py:421
  32.8 0.0 collective-permute-done.3
  32.9 0.8 %collective-permute-start.4 = (f32[4,16,384]{2,1,0:T(8,128)S(1)}, f32[4,16,384]{2,1,0:T(8,128)S(1)}, u32[]{:S(2)}, u32[]{:S(2)}) collective-permute-start(f32[4,16,384]{2,1,0:T(8,128)S(1)} %add_add_fusion), channel_id=1, source_target_pairs={{0,8},{2,10},{4,12},{6,14},{8,0},{10,2},{12,4},{14,6},{16,24},{18,... | collective-permute-start | bytes 294920 | tf_op jit(solution)/shard_map/ppermute | solution.py:421
  33.6 3.9 %collective-permute-done.4 = f32[4,16,384]{2,1,0:T(8,128)S(1)} collective-permute-done((f32[4,16,384]{2,1,0:T(8,128)S(1)}, f32[4,16,384]{2,1,0:T(8,128)S(1)}, u32[]{:S(2)}, u32[]{:S(2)}) %collective-permute-start.4) | collective-permute-done | bytes 98336 | tf_op jit(solution)/shard_map/ppermute | solution.py:421
  37.6 1.6 %collective-permute-start.5 = (f32[4,16,384]{2,1,0:T(8,128)S(1)}, f32[4,16,384]{2,1,0:T(8,128)S(1)}, u32[]{:S(2)}, u32[]{:S(2)}) collective-permute-start(f32[4,16,384]{2,1,0:T(8,128)S(1)} %add.27.refs_1_), channel_id=1, source_target_pairs={{0,24},{2,26},{4,28},{6,30},{8,16},{10,18},{12,20},{14,22},{16,8},... | collective-permute-start | bytes 294920 | tf_op jit(solution)/shard_map/ppermute | solution.py:421
  39.2 4.9 %collective-permute-done.5.refs_2_ = f32[4,16,384]{2,1,0:T(8,128)S(1)} collective-permute-done((f32[4,16,384]{2,1,0:T(8,128)S(1)}, f32[4,16,384]{2,1,0:T(8,128)S(1)}, u32[]{:S(2)}, u32[]{:S(2)}) %collective-permute-start.5) | collective-permute-done | bytes 98336 | tf_op jit(solution)/shard_map/ppermute | solution.py:421
  44.0 0.0 copy-done.1
  44.0 0.0 copy-done.3
  44.0 0.0 copy-done.5
  44.1 0.3 shard_map.125
  44.3 1.3 %collective-permute-start.6 = (f32[16,128]{1,0:T(8,128)S(1)}, f32[16,128]{1,0:T(8,128)S(1)}, u32[]{:S(2)}, u32[]{:S(2)}) collective-permute-start(f32[16,128]{1,0:T(8,128)S(1)} %get-tuple-element.42), channel_id=1, source_target_pairs={{0,2},{2,0},{4,6},{6,4},{8,10},{10,8},{12,14},{14,12},{16,18},{18,... | collective-permute-start | bytes 24584 | tf_op jit(solution)/shard_map/ppermute | solution.py:421
  45.6 2.4 %collective-permute-done.6 = f32[16,128]{1,0:T(8,128)S(1)} collective-permute-done((f32[16,128]{1,0:T(8,128)S(1)}, f32[16,128]{1,0:T(8,128)S(1)}, u32[]{:S(2)}, u32[]{:S(2)}) %collective-permute-start.6) | collective-permute-done | bytes 8224 | tf_op jit(solution)/shard_map/ppermute | solution.py:421
  48.0 1.6 %collective-permute-start.7 = (f32[16,128]{1,0:T(8,128)S(1)}, f32[16,128]{1,0:T(8,128)S(1)}, u32[]{:S(2)}, u32[]{:S(2)}) collective-permute-start(f32[16,128]{1,0:T(8,128)S(1)} %add.28), channel_id=1, source_target_pairs={{0,4},{2,6},{4,0},{6,2},{8,12},{10,14},{12,8},{14,10},{16,20},{18,... | collective-permute-start | bytes 24584 | tf_op jit(solution)/shard_map/ppermute | solution.py:421
  49.6 2.0 %collective-permute-done.7 = f32[16,128]{1,0:T(8,128)S(1)} collective-permute-done((f32[16,128]{1,0:T(8,128)S(1)}, f32[16,128]{1,0:T(8,128)S(1)}, u32[]{:S(2)}, u32[]{:S(2)}) %collective-permute-start.7) | collective-permute-done | bytes 8224 | tf_op jit(solution)/shard_map/ppermute | solution.py:421
  51.6 0.0 collective-permute-start.8
  51.6 0.6 %copy.17 = f32[16,1,360]{2,1,0:T(1,128)} copy(f32[16,1,360]{2,0,1:T(8,128)S(1)} %get-tuple-element.49) | data formatting | bytes 46080
  52.3 0.6 %copy.16 = f32[16,1,360]{2,1,0:T(1,128)} copy(f32[16,1,360]{2,0,1:T(8,128)S(1)} %get-tuple-element.50) | data formatting | bytes 46080
  52.9 0.0 collective-permute-done.8
  52.9 0.1 fusion.1
  53.0 0.1 fusion
  53.1 0.6 %copy.18 = f32[16,1,360]{2,1,0:T(1,128)} copy(f32[16,1,360]{2,0,1:T(8,128)S(1)} %fusion) | data formatting | bytes 46080
  (5 shorter events, 0.1 us)
Async XLA Ops:
  4.5 1.4 %collective-permute-start = (f32[80,128]{1,0:T(8,128)S(1)}, f32[80,128]{1,0:T(8,128)S(1)}, u32[]{:S(2)}, u32[]{:S(2)}) collective-permute-start(f32[80,128]{1,0:T(8,128)S(1)} %get-tuple-element.24.refs_2_), channel_id=1, source_target_pairs={{0,1},{1,0},{2,3},{3,2},{4,5},{5,4},{6,7},{7,6},{8,9},{9,8},{10,11... | collective-permute-start | bytes 122888 | tf_op jit(solution)/shard_map/ppermute | solution.py:421
  7.5 16.0 %all-to-all-start = ((f32[16,16,128]{2,1,0:T(8,128)}), f32[16,16,128]{2,1,0:T(8,128)S(1)}, u32[]{:S(2)}, u32[]{:S(2)}) async-start(f32[16,16,128]{2,1,0:T(8,128)} %get-tuple-element.25), calls=%async_computation | async-start | bytes 262144 | tf_op jit(solution)/shard_map/all_to_all | solution.py:491
  17.1 0.6 %copy-start = (f32[4,16,384]{2,1,0:T(8,128)}, f32[4,16,384]{2,1,0:T(8,128)S(1)}, u32[]{:S(2)}) copy-start(f32[4,16,384]{2,1,0:T(8,128)S(1)} %get-tuple-element.35.refs_4_) | copy-start | bytes 294916
  17.8 0.6 %copy-start.2 = (f32[16,128]{1,0:T(8,128)}, f32[16,128]{1,0:T(8,128)S(1)}, u32[]{:S(2)}) copy-start(f32[16,128]{1,0:T(8,128)S(1)} %get-tuple-element.34.refs_3_) | copy-start | bytes 24580
  18.4 0.6 %copy-start.4 = (f32[1,16,384]{2,1,0:T(8,128)}, f32[1,16,384]{2,1,0:T(8,128)S(1)}, u32[]{:S(2)}) copy-start(f32[1,16,384]{2,1,0:T(8,128)S(1)} %get-tuple-element.37.refs_6_) | copy-start | bytes 73732
  23.5 20.5 %copy-start.1 = (f32[4,16,384]{2,1,0:T(8,128)S(1)}, f32[4,16,384]{2,1,0:T(8,128)}, u32[]{:S(2)}) copy-start(f32[4,16,384]{2,1,0:T(8,128)} %copy-done) | copy-start | bytes 294916
  23.5 20.5 %copy-start.3 = (f32[16,128]{1,0:T(8,128)S(1)}, f32[16,128]{1,0:T(8,128)}, u32[]{:S(2)}) copy-start(f32[16,128]{1,0:T(8,128)} %copy-done.2) | copy-start | bytes 24580
  23.5 20.5 %copy-start.5 = (f32[1,16,384]{2,1,0:T(8,128)S(1)}, f32[1,16,384]{2,1,0:T(8,128)}, u32[]{:S(2)}) copy-start(f32[1,16,384]{2,1,0:T(8,128)} %copy-done.4) | copy-start | bytes 73732
  25.8 5.7 %collective-permute-start.1 = (f32[4,16,384]{2,1,0:T(8,128)S(1)}, f32[4,16,384]{2,1,0:T(8,128)S(1)}, u32[]{:S(2)}, u32[]{:S(2)}) collective-permute-start(f32[4,16,384]{2,1,0:T(8,128)S(1)} %get-tuple-element.31), channel_id=1, source_target_pairs={{0,2},{2,0},{4,6},{6,4},{8,10},{10,8},{12,14},{14,12},{16,18},{18,... | collective-permute-start | bytes 294920 | tf_op jit(solution)/shard_map/ppermute | solution.py:421
  26.9 5.9 %collective-permute-start.2 = (f32[4,16,384]{2,1,0:T(8,128)S(1)}, f32[4,16,384]{2,1,0:T(8,128)S(1)}, u32[]{:S(2)}, u32[]{:S(2)}) collective-permute-start(f32[4,16,384]{2,1,0:T(8,128)S(1)} %get-tuple-element.32), channel_id=1, source_target_pairs={{0,4},{2,6},{4,0},{6,2},{8,12},{10,14},{12,8},{14,10},{16,20},{18,... | collective-permute-start | bytes 294920 | tf_op jit(solution)/shard_map/ppermute | solution.py:421
  27.1 5.7 %collective-permute-start.3 = (f32[4,16,384]{2,1,0:T(8,128)S(1)}, f32[4,16,384]{2,1,0:T(8,128)S(1)}, u32[]{:S(2)}, u32[]{:S(2)}) collective-permute-start(f32[4,16,384]{2,1,0:T(8,128)S(1)} %get-tuple-element.33), channel_id=1, source_target_pairs={{0,6},{2,4},{4,2},{6,0},{8,14},{10,12},{12,10},{14,8},{16,22},{18,... | collective-permute-start | bytes 294920 | tf_op jit(solution)/shard_map/ppermute | solution.py:421
  32.9 4.7 %collective-permute-start.4 = (f32[4,16,384]{2,1,0:T(8,128)S(1)}, f32[4,16,384]{2,1,0:T(8,128)S(1)}, u32[]{:S(2)}, u32[]{:S(2)}) collective-permute-start(f32[4,16,384]{2,1,0:T(8,128)S(1)} %add_add_fusion), channel_id=1, source_target_pairs={{0,8},{2,10},{4,12},{6,14},{8,0},{10,2},{12,4},{14,6},{16,24},{18,... | collective-permute-start | bytes 294920 | tf_op jit(solution)/shard_map/ppermute | solution.py:421
  37.6 6.5 %collective-permute-start.5 = (f32[4,16,384]{2,1,0:T(8,128)S(1)}, f32[4,16,384]{2,1,0:T(8,128)S(1)}, u32[]{:S(2)}, u32[]{:S(2)}) collective-permute-start(f32[4,16,384]{2,1,0:T(8,128)S(1)} %add.27.refs_1_), channel_id=1, source_target_pairs={{0,24},{2,26},{4,28},{6,30},{8,16},{10,18},{12,20},{14,22},{16,8},... | collective-permute-start | bytes 294920 | tf_op jit(solution)/shard_map/ppermute | solution.py:421
  44.3 3.7 %collective-permute-start.6 = (f32[16,128]{1,0:T(8,128)S(1)}, f32[16,128]{1,0:T(8,128)S(1)}, u32[]{:S(2)}, u32[]{:S(2)}) collective-permute-start(f32[16,128]{1,0:T(8,128)S(1)} %get-tuple-element.42), channel_id=1, source_target_pairs={{0,2},{2,0},{4,6},{6,4},{8,10},{10,8},{12,14},{14,12},{16,18},{18,... | collective-permute-start | bytes 24584 | tf_op jit(solution)/shard_map/ppermute | solution.py:421
  48.0 3.7 %collective-permute-start.7 = (f32[16,128]{1,0:T(8,128)S(1)}, f32[16,128]{1,0:T(8,128)S(1)}, u32[]{:S(2)}, u32[]{:S(2)}) collective-permute-start(f32[16,128]{1,0:T(8,128)S(1)} %add.28), channel_id=1, source_target_pairs={{0,4},{2,6},{4,0},{6,2},{8,12},{10,14},{12,8},{14,10},{16,20},{18,... | collective-permute-start | bytes 24584 | tf_op jit(solution)/shard_map/ppermute | solution.py:421
  51.6 1.3 %collective-permute-start.8 = (f32[16,128]{1,0:T(8,128)S(1)}, f32[16,128]{1,0:T(8,128)S(1)}, u32[]{:S(2)}, u32[]{:S(2)}) collective-permute-start(f32[16,128]{1,0:T(8,128)S(1)} %add.29), channel_id=1, source_target_pairs={{0,1},{1,0},{2,3},{3,2},{4,5},{5,4},{6,7},{7,6},{8,9},{9,8},{10,11... | collective-permute-start | bytes 24584 | tf_op jit(solution)/shard_map/ppermute | solution.py:421

commit v5 on v4

--- a/solution.py
+++ b/solution.py
@@ -152,9 +152,10 @@
 def predict_kernel(*refs):
     orders_hbm, lives_hbm, ratios_hbm, taps_hbm = refs[:4]
     residual_hbm, direction_hbm, diagonal_hbm, design_hbm = refs[4:8]
-    predicted_ref, rates_ref, design_ref = refs[8:11]
-    orders_ref, lives_ref, ratios_ref, taps_ref, remaining_ref, search_ref, diagonal_ref, sems = refs[11:]
-    components, length, _ = design_ref.shape
+    predicted_ref, rates_ref, spread_ref, steps_ref, design_ref = refs[8:13]
+    orders_ref, lives_ref, ratios_ref, taps_ref, remaining_ref, search_ref, diagonal_ref, sems = refs[13:]
+    components = taps_ref.shape[0]
+    length = design_ref.shape[0] // components
     copies = [
         pltpu.make_async_copy(source, target, sems.at[at])
         for at, (source, target) in enumerate(
@@ -164,7 +165,7 @@
                 (lives_hbm, lives_ref),
                 (ratios_hbm, ratios_ref),
                 (taps_hbm, taps_ref),
-                *[(design_hbm.at[at], design_ref.at[at]) for at in range(components)],
+                (design_hbm, design_ref),
                 (residual_hbm.at[:, 0, :], remaining_ref),
                 (diagonal_hbm, diagonal_ref),
             ]
@@ -214,46 +215,6 @@
     rates_ref[sections * levels : sections * (levels + 1), :] = zero_rate
     rates_ref[sections * (levels + 1) : sections * (levels + 1) + taps_count, :] = tap_rows
 
-    copies[0].wait()
-    search = search_ref[...]
-    high = search.astype(BF16)
-    rest = search - high.astype(F32)
-    middle = rest.astype(BF16)
-    low = (rest - middle.astype(F32)).astype(BF16)
-    split = jnp.concatenate([high, middle, low], axis=0)
-    coarse, fine = ([], [])
-    for at in range(components):
-        copies[5 + at].wait()
-        sums = lax.dot_general(
-            design_ref[at], split, (((1,), (1,)), ((), ())), preferred_element_type=F32
-        )
-        coarse.append(sums[:, :count])
-        fine.append(sums[:, count : 2 * count] + sums[:, 2 * count :])
-    predicted_ref[:length, :] = jnp.concatenate(coarse + fine, axis=1)
-    for copy in copies[5 + components :]:
-        copy.wait()
-    remaining = remaining_ref[...]
-    energy = jnp.sum(remaining * diagonal_ref[...] * remaining, axis=1, keepdims=True)
-    predicted_ref[length:, :] = jnp.broadcast_to(energy, (count, LANES))
-
-
-def tables_kernel(width, first_bits, sections, taps_count, length, *refs):
-    place_ref, rates_ref, keep_hbm = refs[:3]
-    vectors_hbm, diagonal_hbm = (refs[3:6], refs[6])
-    spread_ref, steps_ref, energy_ref = refs[7:10]
-    slices = refs[10:14]
-    current_ref, remaining_ref, search_ref, diagonal_ref, sems = refs[14:]
-    sources = [current_ref, remaining_ref, search_ref]
-    copies = [
-        pltpu.make_async_copy(vector.at[:, 0, :], target, sems.at[at])
-        for at, (vector, target) in enumerate(zip(vectors_hbm, sources))
-    ]
-    copies.append(pltpu.make_async_copy(diagonal_hbm, diagonal_ref, sems.at[len(sources)]))
-    tail = keep_hbm.at[pl.ds(length, energy_ref.shape[0]), :]
-    copies.append(pltpu.make_async_copy(tail, energy_ref, sems.at[len(sources) + 1]))
-    for copy in copies:
-        copy.start()
-    half = LANES // 2
     reach = taps_count - 1
     kinds = sections + reach
     poles, zeros, taps = rates_of(rates_ref, sections, taps_count, length.bit_length() - 1)
@@ -274,6 +235,41 @@
     wanted = half + within // SLOT * SLOT + target // LANES
     pick = jnp.where((within < half) & (source == wanted), 1.0, 0.0)
     steps_ref[...] = jnp.dot(stacked, pick, precision=HIGHEST, preferred_element_type=F32)
+
+    copies[0].wait()
+    search = search_ref[...]
+    high = search.astype(BF16)
+    rest = search - high.astype(F32)
+    middle = rest.astype(BF16)
+    low = (rest - middle.astype(F32)).astype(BF16)
+    split = jnp.concatenate([high, middle, low], axis=0)
+    copies[5].wait()
+    sums = lax.dot_general(
+        design_ref[...], split, (((1,), (1,)), ((), ())), preferred_element_type=F32
+    )
+    pieces = [sums[at * length : (at + 1) * length] for at in range(components)]
+    coarse = [piece[:, :count] for piece in pieces]
+    fine = [piece[:, count : 2 * count] + piece[:, 2 * count :] for piece in pieces]
+    predicted_ref[:length, :] = jnp.concatenate(coarse + fine, axis=1)
+    for copy in copies[6:]:
+        copy.wait()
+    remaining = remaining_ref[...]
+    energy = jnp.sum(remaining * diagonal_ref[...] * remaining, axis=1, keepdims=True)
+    predicted_ref[length:, :] = jnp.broadcast_to(energy, (count, LANES))
+
+
+def slices_kernel(width, first_bits, *refs):
+    place_ref, vectors_hbm, diagonal_hbm = (refs[0], refs[1:4], refs[4])
+    slices = refs[5:9]
+    current_ref, remaining_ref, search_ref, diagonal_ref, sems = refs[9:]
+    sources = [current_ref, remaining_ref, search_ref]
+    copies = [
+        pltpu.make_async_copy(vector.at[:, 0, :], target, sems.at[at])
+        for at, (vector, target) in enumerate(zip(vectors_hbm, sources))
+    ]
+    copies.append(pltpu.make_async_copy(diagonal_hbm, diagonal_ref, sems.at[len(sources)]))
+    for copy in copies:
+        copy.start()
     for copy in copies:
         copy.wait()
     mine = place_ref[0]
@@ -288,12 +284,12 @@
 def filter_kernel(sections, taps_count, length, parts, *refs):
     counts_ref, rates_ref = refs[:2]
     gathered = refs[2 : 2 + parts]
-    send_ref, keep_hbm, keep_ref, sem = refs[2 + parts :]
+    send_ref, keep_ref, energy_ref = refs[2 + parts :]
     half = LANES // 2
     received = gathered[0][...]
     for other in gathered[1:]:
         received = received + other[...]
-    keep_ref[length:, :] = received[length:]
+    energy_ref[...] = received[length:]
     received = received[:length]
     low_half = lax.broadcasted_iota(jnp.int32, (1, LANES), 1) < half
     data = jnp.where(low_half & (rows_of(received) < counts_ref[0]), received, 0.0)
@@ -304,17 +300,12 @@
     sent = jnp.where(low_half, pack(ends), pltpu.roll(pack(heads), half, 1))
     for block in range(send_ref.shape[0]):
         send_ref[block] = sent
-    keep_ref[:length, :] = jnp.where(low_half, local, received + pltpu.roll(received, half, 1))
-    copy = pltpu.make_async_copy(keep_ref, keep_hbm, sem)
-    copy.start()
-    copy.wait()
+    keep_ref[...] = jnp.where(low_half, local, received + pltpu.roll(received, half, 1))
 
 
 def normal_kernel(kinds, width, first_bits, *refs):
-    place_ref, counts_ref, all_ref, keep_hbm, spread_ref, steps_ref, design_ref = refs[:7]
-    out_refs, (entering_ref, normal_ref, keep_ref, sem) = (refs[7:-4], refs[-4:])
-    fetch = pltpu.make_async_copy(keep_hbm.at[pl.ds(0, keep_ref.shape[0]), :], keep_ref, sem)
-    fetch.start()
+    place_ref, counts_ref, all_ref, keep_ref, spread_ref, steps_ref, design_ref = refs[:7]
+    out_refs, (entering_ref, normal_ref) = (refs[7:-2], refs[-2:])
     blocks = all_ref.shape[0]
     mine = place_ref[0]
     half = LANES // 2
@@ -356,7 +347,6 @@
         precision=HIGHEST,
         preferred_element_type=F32,
     )
-    fetch.wait()
     kept = keep_ref[...]
     live = (row < counts_ref[0]) & (lane < half)
     weighted = jnp.where(live, kept + correction, 0.0)
@@ -377,8 +367,7 @@
     curvature = curve[:count]
     for at in range(1, half // count):
         curvature = curvature + curve[at * count : (at + 1) * count]
-    rows = jnp.concatenate([design_ref[at] for at in range(design_ref.shape[0])], axis=0)
-    normal_ref[...] = jnp.dot(low, rows, preferred_element_type=F32)
+    normal_ref[...] = jnp.dot(low, design_ref[...], preferred_element_type=F32)
     padded = out_refs[0].shape[-1]
     column = lax.broadcasted_iota(jnp.int32, (count, padded), 1)
     curvature = jnp.broadcast_to(curvature[:, :1], (count, padded))
@@ -461,56 +450,35 @@
         fir_taps,
     ]
 
-    predicted, rates, design_kept = call(
+    predicted, rates, spread, steps, design_kept = call(
         predict_kernel,
         (
             shape(length + count, LANES),
             shape(sections * (levels + 1) + taps_count, LANES),
-            jax.ShapeDtypeStruct((components, length, wide), BF16),
+            shape(length, LANES),
+            shape(3 * SLOT, kinds * LANES),
+            jax.ShapeDtypeStruct((components * length, wide), BF16),
         ),
         *small,
         residual,
         direction,
         precond,
-        design[:, :, 0, :],
+        design.reshape(components * length, wide),
         specs=[hbm] * 8,
         scratch=[pltpu.VMEM(each.shape, each.dtype) for each in small]
         + [pltpu.VMEM((count, wide), F32)] * 2
-        + [pltpu.VMEM((1, wide), F32), pltpu.SemaphoreType.DMA((7 + components,))],
+        + [pltpu.VMEM((1, wide), F32), pltpu.SemaphoreType.DMA((8,))],
     )
     arrived = over_order(predicted)
-    send, keep = call(
+    send, keep, energy = call(
         functools.partial(filter_kernel, sections, taps_count, length, len(arrived)),
-        (shape(blocks, SLOT, LANES), pltpu.HBM((length + count, LANES), F32)),
+        (shape(blocks, SLOT, LANES), shape(length, LANES), shape(count, LANES)),
         epoch_counts,
         rates,
         *arrived,
         specs=[smem()] + [vmem()] * (1 + len(arrived)),
-        scratch=[pltpu.VMEM((length + count, LANES), F32), pltpu.SemaphoreType.DMA],
     )
     everyone = lax.all_to_all(send, "tm", 0, 0)
-    spread, steps, energy, diagonal_parts, remaining_parts, search_own, current_own = call(
-        functools.partial(tables_kernel, width, classes, sections, taps_count, length),
-        (
-            shape(length, LANES),
-            shape(3 * SLOT, kinds * LANES),
-            shape(count, LANES),
-            shape(parts, count, padded),
-            shape(parts, count, padded),
-            shape(1, count, padded),
-            shape(1, count, padded),
-        ),
-        place,
-        rates,
-        keep,
-        solution,
-        residual,
-        direction,
-        precond,
-        specs=[smem(), vmem()] + [hbm] * 5,
-        scratch=[pltpu.VMEM((count, wide), F32)] * 3
-        + [pltpu.VMEM((1, wide), F32), pltpu.SemaphoreType.DMA((5,))],
-    )
     pieces = call(
         functools.partial(normal_kernel, kinds, width, classes),
         [shape(parts, count, padded)] * classes,
@@ -521,13 +489,25 @@
         spread,
         steps,
         design_kept,
-        specs=[smem()] * 2 + [vmem(), hbm] + [vmem()] * 3,
-        scratch=[
-            pltpu.VMEM((blocks, SLOT, LANES), F32),
-            pltpu.VMEM((count, wide), F32),
-            pltpu.VMEM((length, LANES), F32),
-            pltpu.SemaphoreType.DMA,
-        ],
+        specs=[smem()] * 2 + [vmem()] * 5,
+        scratch=[pltpu.VMEM((blocks, SLOT, LANES), F32), pltpu.VMEM((count, wide), F32)],
+    )
+    diagonal_parts, remaining_parts, search_own, current_own = call(
+        functools.partial(slices_kernel, width, classes),
+        (
+            shape(parts, count, padded),
+            shape(parts, count, padded),
+            shape(1, count, padded),
+            shape(1, count, padded),
+        ),
+        place,
+        solution,
+        residual,
+        direction,
+        precond,
+        specs=[smem()] + [hbm] * 4,
+        scratch=[pltpu.VMEM((count, wide), F32)] * 3
+        + [pltpu.VMEM((1, wide), F32), pltpu.SemaphoreType.DMA((4,))],
     )
     arriving = [exchange(pieces[apart], "tm", apart) for apart in range(1, classes)]
     buffer = pieces[0] + sum(arriving[1:], arriving[0])

time: 54.1 us -> 52.3 us (0.967)
  waiting for transfers between devices: 21.4 us -> 23.3 us
  local copies, waits for them, and re-layouts: 3.77 us -> 1.91 us
  Pallas kernels: 9.36 us -> 7.61 us
    all_to_all x1, waiting for transfers between devices: 4.52 us -> 7.79 us  [shards(): everyone = lax.all_to_all(send, 'tm', 0, 0)]
    unnamed x15 -> x3, local copies, waits for them, and re-layouts: 3.77 us -> 1.91 us
    pallas_call x5, Pallas kernels: 9.36 us -> 7.61 us  [call(): pl.pallas_call(kernel, out_shape=outs, in_specs=specs or [vmem()] * len(a...]
    ppermute x9, waiting for transfers between devices: 16.9 us -> 15.5 us  [exchange(): return lax.ppermute(value, axis, [(at, at ^ bit) for at in range(size)])]
where the time goes in v5:
time: 52.3 us; the launch traced here: 52 us
  waiting for transfers between devices  23.3 us (45%)
  starting transfers between devices  17.6 us (34%)
  Pallas kernels  7.61 us (15%)
  local copies, waits for them, and re-layouts  1.91 us (4%)
  between operations  1.34 us (3%)
    ppermute x9, waiting for transfers between devices, exchange(): return lax.ppermute(value, axis, [(at, at ^ bit) for at in range(size)])  15.5 us
    ppermute x9, starting transfers between devices, exchange(): return lax.ppermute(value, axis, [(at, at ^ bit) for at in range(size)])  9.37 us
    all_to_all x1, starting transfers between devices, shards(): everyone = lax.all_to_all(send, 'tm', 0, 0)  8.2 us
    all_to_all x1, waiting for transfers between devices, shards(): everyone = lax.all_to_all(send, 'tm', 0, 0)  7.79 us
    pallas_call x5, Pallas kernels, call(): pl.pallas_call(kernel, out_shape=outs, in_specs=specs or [vmem()] * len(a...  7.61 us
    unnamed x3, local copies, waits for them, and re-layouts  1.91 us
  transfers between devices with their start and end apart: 10, of which 8 were waited for; matrix products, arithmetic and copies ran while one was open for 2% of the time, Pallas kernels for 3%

profile of v5, /device:TPU:0, one launch (start us, length us, event | category | flops | bytes accessed | tf_op | source)
XLA Modules:
  0.0 52.0 jit_solution(2306759263088011299)
XLA Ops:
  0.6 3.3 %shard_map.121 = (f32[80,128]{1,0:T(8,128)S(1)}, f32[37,128]{1,0:T(8,128)S(1)}, f32[64,128]{1,0:T(8,128)S(1)}, f32[48,1536]{1,0:T(8,128)S(1)}, bf16[256,5760]{1,0:T(8,128)(2,1)S(1)}) custom-call(s32[2,4]{1,0:T(2,128)} %bitcast.16, f32[2,2,4]{2,1,0:T(2,128)} %bitcast.14, f32[2,2,4]{2,1,0:T(2,128)} %bitcast.15, f32[4,9]{1,0:T(4,128)} %refs_3_.2, ...), custom_call_target="tpu_custom_call" | custom-call | tf_op jit(solution)/shard_map/pallas_call | solution.py:33
  4.0 0.5 %collective-permute-start = (f32[80,128]{1,0:T(8,128)S(1)}, f32[80,128]{1,0:T(8,128)S(1)}, u32[]{:S(2)}, u32[]{:S(2)}) collective-permute-start(f32[80,128]{1,0:T(8,128)S(1)} %get-tuple-element.24.refs_2_), channel_id=1, source_target_pairs={{0,1},{1,0},{2,3},{3,2},{4,5},{5,4},{6,7},{7,6},{8,9},{9,8},{10,11... | collective-permute-start | bytes 122888 | tf_op jit(solution)/shard_map/ppermute | solution.py:410
  5.1 0.2 collective-permute-done.refs_3_
  5.4 1.0 %shard_map.122 = (f32[16,16,128]{2,1,0:T(8,128)}, f32[64,128]{1,0:T(8,128)S(1)}, f32[16,128]{1,0:T(8,128)S(1)}) custom-call(s32[1]{0:T(128)S(6)} %copy.19.refs_0_.refs_1_, f32[37,128]{1,0:T(8,128)S(1)} %get-tuple-element.23.refs_1_, f32[80,128]{1,0:T(8,128)S(1)} %get-tuple-element.24.refs_2_, f32[80,128]{1,0:T(8,128)S(1)} %collective-permute-done.refs_3_), custom_call_target="tpu_custom_call" | custom-call | tf_op jit(solution)/shard_map/pallas_call | solution.py:33
  6.4 8.2 %all-to-all-start = ((f32[16,16,128]{2,1,0:T(8,128)}), f32[16,16,128]{2,1,0:T(8,128)S(1)}, u32[]{:S(2)}, u32[]{:S(2)}) async-start(f32[16,16,128]{2,1,0:T(8,128)} %get-tuple-element.25), calls=%async_computation | async-start | bytes 262144 | tf_op jit(solution)/shard_map/all_to_all | solution.py:481
  14.6 7.8 %all-to-all-done.refs_2_ = f32[16,16,128]{2,1,0:T(8,128)S(1)} async-done(((f32[16,16,128]{2,1,0:T(8,128)}), f32[16,16,128]{2,1,0:T(8,128)S(1)}, u32[]{:S(2)}, u32[]{:S(2)}) %all-to-all-start) | async-done | bytes 131104 | tf_op jit(solution)/shard_map/all_to_all | solution.py:481
  22.4 1.6 %shard_map.123 = (f32[4,16,384]{2,1,0:T(8,128)S(1)}, f32[4,16,384]{2,1,0:T(8,128)S(1)}, f32[4,16,384]{2,1,0:T(8,128)S(1)}, f32[4,16,384]{2,1,0:T(8,128)S(1)}) custom-call(s32[1]{0:T(128)} %bitcast.refs_0_, s32[1]{0:T(128)S(6)} %copy.19.refs_0_.refs_1_, f32[16,16,128]{2,1,0:T(8,128)S(1)} %all-to-all-done.refs_2_, f32[64,128]{1,0:T(8,128)S(1)} %get-tuple-element.26.refs_3_, ...), custom_call_target="tpu_custom_call" | custom-call | tf_op jit(solution)/shard_map/pallas_call | solution.py:33
  24.0 1.2 %collective-permute-start.1 = (f32[4,16,384]{2,1,0:T(8,128)S(1)}, f32[4,16,384]{2,1,0:T(8,128)S(1)}, u32[]{:S(2)}, u32[]{:S(2)}) collective-permute-start(f32[4,16,384]{2,1,0:T(8,128)S(1)} %get-tuple-element.31), channel_id=1, source_target_pairs={{0,2},{2,0},{4,6},{6,4},{8,10},{10,8},{12,14},{14,12},{16,18},{18,... | collective-permute-start | bytes 294920 | tf_op jit(solution)/shard_map/ppermute | solution.py:410
  25.2 0.2 collective-permute-start.2
  25.4 2.2 %collective-permute-start.3 = (f32[4,16,384]{2,1,0:T(8,128)S(1)}, f32[4,16,384]{2,1,0:T(8,128)S(1)}, u32[]{:S(2)}, u32[]{:S(2)}) collective-permute-start(f32[4,16,384]{2,1,0:T(8,128)S(1)} %get-tuple-element.33), channel_id=1, source_target_pairs={{0,6},{2,4},{4,2},{6,0},{8,14},{10,12},{12,10},{14,8},{16,22},{18,... | collective-permute-start | bytes 294920 | tf_op jit(solution)/shard_map/ppermute | solution.py:410
  27.6 2.1 %collective-permute-done.1 = f32[4,16,384]{2,1,0:T(8,128)S(1)} collective-permute-done((f32[4,16,384]{2,1,0:T(8,128)S(1)}, f32[4,16,384]{2,1,0:T(8,128)S(1)}, u32[]{:S(2)}, u32[]{:S(2)}) %collective-permute-start.1) | collective-permute-done | bytes 98336 | tf_op jit(solution)/shard_map/ppermute | solution.py:410
  29.7 1.4 %collective-permute-done.2 = f32[4,16,384]{2,1,0:T(8,128)S(1)} collective-permute-done((f32[4,16,384]{2,1,0:T(8,128)S(1)}, f32[4,16,384]{2,1,0:T(8,128)S(1)}, u32[]{:S(2)}, u32[]{:S(2)}) %collective-permute-start.2) | collective-permute-done | bytes 98336 | tf_op jit(solution)/shard_map/ppermute | solution.py:410
  31.1 0.0 collective-permute-done.3
  31.1 0.8 %collective-permute-start.4 = (f32[4,16,384]{2,1,0:T(8,128)S(1)}, f32[4,16,384]{2,1,0:T(8,128)S(1)}, u32[]{:S(2)}, u32[]{:S(2)}) collective-permute-start(f32[4,16,384]{2,1,0:T(8,128)S(1)} %add_add_fusion), channel_id=1, source_target_pairs={{0,8},{2,10},{4,12},{6,14},{8,0},{10,2},{12,4},{14,6},{16,24},{18,... | collective-permute-start | bytes 294920 | tf_op jit(solution)/shard_map/ppermute | solution.py:410
  31.9 3.9 %collective-permute-done.4 = f32[4,16,384]{2,1,0:T(8,128)S(1)} collective-permute-done((f32[4,16,384]{2,1,0:T(8,128)S(1)}, f32[4,16,384]{2,1,0:T(8,128)S(1)}, u32[]{:S(2)}, u32[]{:S(2)}) %collective-permute-start.4) | collective-permute-done | bytes 98336 | tf_op jit(solution)/shard_map/ppermute | solution.py:410
  35.8 1.6 %collective-permute-start.5 = (f32[4,16,384]{2,1,0:T(8,128)S(1)}, f32[4,16,384]{2,1,0:T(8,128)S(1)}, u32[]{:S(2)}, u32[]{:S(2)}) collective-permute-start(f32[4,16,384]{2,1,0:T(8,128)S(1)} %add.27.refs_1_), channel_id=1, source_target_pairs={{0,24},{2,26},{4,28},{6,30},{8,16},{10,18},{12,20},{14,22},{16,8},... | collective-permute-start | bytes 294920 | tf_op jit(solution)/shard_map/ppermute | solution.py:410
  37.4 1.4 %shard_map.124 = (f32[4,16,384]{2,1,0:T(8,128)S(1)}, f32[4,16,384]{2,1,0:T(8,128)S(1)}, f32[1,16,384]{2,1,0:T(8,128)S(1)}, f32[1,16,384]{2,1,0:T(8,128)S(1)}) custom-call(s32[1]{0:T(128)} %bitcast.refs_0_, f32[16,1,5760]{2,1,0:T(1,128)} %refs_1_.2, f32[16,1,5760]{2,1,0:T(1,128)} %refs_2_.1, f32[16,1,5760]{2,1,0:T(1,128)} %refs_3_.3, f32[1,5760]{1,0:T(1,128)} %refs_4_.3), custom_call_target="tpu_custom_call" | custom-call | tf_op jit(solution)/shard_map/pallas_call | solution.py:33
  38.8 3.5 %collective-permute-done.5.refs_2_ = f32[4,16,384]{2,1,0:T(8,128)S(1)} collective-permute-done((f32[4,16,384]{2,1,0:T(8,128)S(1)}, f32[4,16,384]{2,1,0:T(8,128)S(1)}, u32[]{:S(2)}, u32[]{:S(2)}) %collective-permute-start.5) | collective-permute-done | bytes 98336 | tf_op jit(solution)/shard_map/ppermute | solution.py:410
  42.3 0.3 shard_map.125
  42.5 1.3 %collective-permute-start.6 = (f32[16,128]{1,0:T(8,128)S(1)}, f32[16,128]{1,0:T(8,128)S(1)}, u32[]{:S(2)}, u32[]{:S(2)}) collective-permute-start(f32[16,128]{1,0:T(8,128)S(1)} %get-tuple-element.42), channel_id=1, source_target_pairs={{0,2},{2,0},{4,6},{6,4},{8,10},{10,8},{12,14},{14,12},{16,18},{18,... | collective-permute-start | bytes 24584 | tf_op jit(solution)/shard_map/ppermute | solution.py:410
  43.8 2.4 %collective-permute-done.6 = f32[16,128]{1,0:T(8,128)S(1)} collective-permute-done((f32[16,128]{1,0:T(8,128)S(1)}, f32[16,128]{1,0:T(8,128)S(1)}, u32[]{:S(2)}, u32[]{:S(2)}) %collective-permute-start.6) | collective-permute-done | bytes 8224 | tf_op jit(solution)/shard_map/ppermute | solution.py:410
  46.2 1.6 %collective-permute-start.7 = (f32[16,128]{1,0:T(8,128)S(1)}, f32[16,128]{1,0:T(8,128)S(1)}, u32[]{:S(2)}, u32[]{:S(2)}) collective-permute-start(f32[16,128]{1,0:T(8,128)S(1)} %add.28), channel_id=1, source_target_pairs={{0,4},{2,6},{4,0},{6,2},{8,12},{10,14},{12,8},{14,10},{16,20},{18,... | collective-permute-start | bytes 24584 | tf_op jit(solution)/shard_map/ppermute | solution.py:410
  47.8 2.0 %collective-permute-done.7 = f32[16,128]{1,0:T(8,128)S(1)} collective-permute-done((f32[16,128]{1,0:T(8,128)S(1)}, f32[16,128]{1,0:T(8,128)S(1)}, u32[]{:S(2)}, u32[]{:S(2)}) %collective-permute-start.7) | collective-permute-done | bytes 8224 | tf_op jit(solution)/shard_map/ppermute | solution.py:410
  49.9 0.0 collective-permute-start.8
  49.9 0.6 %copy.16 = f32[16,1,360]{2,1,0:T(1,128)} copy(f32[16,1,360]{2,0,1:T(8,128)S(1)} %get-tuple-element.50) | data formatting | bytes 46080
  50.5 0.6 %copy.17 = f32[16,1,360]{2,1,0:T(1,128)} copy(f32[16,1,360]{2,0,1:T(8,128)S(1)} %get-tuple-element.49) | data formatting | bytes 46080
  51.1 0.0 collective-permute-done.8
  51.1 0.1 fusion.1
  51.3 0.1 fusion
  51.3 0.6 %copy.18 = f32[16,1,360]{2,1,0:T(1,128)} copy(f32[16,1,360]{2,0,1:T(8,128)S(1)} %fusion) | data formatting | bytes 46080
  (5 shorter events, 0.1 us)
Async XLA Ops:
  4.0 1.4 %collective-permute-start = (f32[80,128]{1,0:T(8,128)S(1)}, f32[80,128]{1,0:T(8,128)S(1)}, u32[]{:S(2)}, u32[]{:S(2)}) collective-permute-start(f32[80,128]{1,0:T(8,128)S(1)} %get-tuple-element.24.refs_2_), channel_id=1, source_target_pairs={{0,1},{1,0},{2,3},{3,2},{4,5},{5,4},{6,7},{7,6},{8,9},{9,8},{10,11... | collective-permute-start | bytes 122888 | tf_op jit(solution)/shard_map/ppermute | solution.py:410
  6.4 16.0 %all-to-all-start = ((f32[16,16,128]{2,1,0:T(8,128)}), f32[16,16,128]{2,1,0:T(8,128)S(1)}, u32[]{:S(2)}, u32[]{:S(2)}) async-start(f32[16,16,128]{2,1,0:T(8,128)} %get-tuple-element.25), calls=%async_computation | async-start | bytes 262144 | tf_op jit(solution)/shard_map/all_to_all | solution.py:481
  24.0 5.7 %collective-permute-start.1 = (f32[4,16,384]{2,1,0:T(8,128)S(1)}, f32[4,16,384]{2,1,0:T(8,128)S(1)}, u32[]{:S(2)}, u32[]{:S(2)}) collective-permute-start(f32[4,16,384]{2,1,0:T(8,128)S(1)} %get-tuple-element.31), channel_id=1, source_target_pairs={{0,2},{2,0},{4,6},{6,4},{8,10},{10,8},{12,14},{14,12},{16,18},{18,... | collective-permute-start | bytes 294920 | tf_op jit(solution)/shard_map/ppermute | solution.py:410
  25.2 5.9 %collective-permute-start.2 = (f32[4,16,384]{2,1,0:T(8,128)S(1)}, f32[4,16,384]{2,1,0:T(8,128)S(1)}, u32[]{:S(2)}, u32[]{:S(2)}) collective-permute-start(f32[4,16,384]{2,1,0:T(8,128)S(1)} %get-tuple-element.32), channel_id=1, source_target_pairs={{0,4},{2,6},{4,0},{6,2},{8,12},{10,14},{12,8},{14,10},{16,20},{18,... | collective-permute-start | bytes 294920 | tf_op jit(solution)/shard_map/ppermute | solution.py:410
  25.4 5.7 %collective-permute-start.3 = (f32[4,16,384]{2,1,0:T(8,128)S(1)}, f32[4,16,384]{2,1,0:T(8,128)S(1)}, u32[]{:S(2)}, u32[]{:S(2)}) collective-permute-start(f32[4,16,384]{2,1,0:T(8,128)S(1)} %get-tuple-element.33), channel_id=1, source_target_pairs={{0,6},{2,4},{4,2},{6,0},{8,14},{10,12},{12,10},{14,8},{16,22},{18,... | collective-permute-start | bytes 294920 | tf_op jit(solution)/shard_map/ppermute | solution.py:410
  31.1 4.7 %collective-permute-start.4 = (f32[4,16,384]{2,1,0:T(8,128)S(1)}, f32[4,16,384]{2,1,0:T(8,128)S(1)}, u32[]{:S(2)}, u32[]{:S(2)}) collective-permute-start(f32[4,16,384]{2,1,0:T(8,128)S(1)} %add_add_fusion), channel_id=1, source_target_pairs={{0,8},{2,10},{4,12},{6,14},{8,0},{10,2},{12,4},{14,6},{16,24},{18,... | collective-permute-start | bytes 294920 | tf_op jit(solution)/shard_map/ppermute | solution.py:410
  35.8 6.5 %collective-permute-start.5 = (f32[4,16,384]{2,1,0:T(8,128)S(1)}, f32[4,16,384]{2,1,0:T(8,128)S(1)}, u32[]{:S(2)}, u32[]{:S(2)}) collective-permute-start(f32[4,16,384]{2,1,0:T(8,128)S(1)} %add.27.refs_1_), channel_id=1, source_target_pairs={{0,24},{2,26},{4,28},{6,30},{8,16},{10,18},{12,20},{14,22},{16,8},... | collective-permute-start | bytes 294920 | tf_op jit(solution)/shard_map/ppermute | solution.py:410
  42.5 3.7 %collective-permute-start.6 = (f32[16,128]{1,0:T(8,128)S(1)}, f32[16,128]{1,0:T(8,128)S(1)}, u32[]{:S(2)}, u32[]{:S(2)}) collective-permute-start(f32[16,128]{1,0:T(8,128)S(1)} %get-tuple-element.42), channel_id=1, source_target_pairs={{0,2},{2,0},{4,6},{6,4},{8,10},{10,8},{12,14},{14,12},{16,18},{18,... | collective-permute-start | bytes 24584 | tf_op jit(solution)/shard_map/ppermute | solution.py:410
  46.2 3.7 %collective-permute-start.7 = (f32[16,128]{1,0:T(8,128)S(1)}, f32[16,128]{1,0:T(8,128)S(1)}, u32[]{:S(2)}, u32[]{:S(2)}) collective-permute-start(f32[16,128]{1,0:T(8,128)S(1)} %add.28), channel_id=1, source_target_pairs={{0,4},{2,6},{4,0},{6,2},{8,12},{10,14},{12,8},{14,10},{16,20},{18,... | collective-permute-start | bytes 24584 | tf_op jit(solution)/shard_map/ppermute | solution.py:410
  49.9 1.3 %collective-permute-start.8 = (f32[16,128]{1,0:T(8,128)S(1)}, f32[16,128]{1,0:T(8,128)S(1)}, u32[]{:S(2)}, u32[]{:S(2)}) collective-permute-start(f32[16,128]{1,0:T(8,128)S(1)} %add.29), channel_id=1, source_target_pairs={{0,1},{1,0},{2,3},{3,2},{4,5},{5,4},{6,7},{7,6},{8,9},{9,8},{10,11... | collective-permute-start | bytes 24584 | tf_op jit(solution)/shard_map/ppermute | solution.py:410

commit v6 on v5

--- a/solution.py
+++ b/solution.py
@@ -150,6 +150,7 @@
 
 
 def predict_kernel(*refs):
+    _, *refs = refs
     orders_hbm, lives_hbm, ratios_hbm, taps_hbm = refs[:4]
     residual_hbm, direction_hbm, diagonal_hbm, design_hbm = refs[4:8]
     predicted_ref, rates_ref, spread_ref, steps_ref, design_ref = refs[8:13]
@@ -459,12 +460,13 @@
             shape(3 * SLOT, kinds * LANES),
             jax.ShapeDtypeStruct((components * length, wide), BF16),
         ),
+        place,
         *small,
         residual,
         direction,
         precond,
         design.reshape(components * length, wide),
-        specs=[hbm] * 8,
+        specs=[smem()] + [hbm] * 8,
         scratch=[pltpu.VMEM(each.shape, each.dtype) for each in small]
         + [pltpu.VMEM((count, wide), F32)] * 2
         + [pltpu.VMEM((1, wide), F32), pltpu.SemaphoreType.DMA((8,))],
@@ -512,8 +514,8 @@
     arriving = [exchange(pieces[apart], "tm", apart) for apart in range(1, classes)]
     buffer = pieces[0] + sum(arriving[1:], arriving[0])
     for bit in range(halved, bits - 1):
-        buffer = buffer + exchange(buffer, "tm", (2 << bit) - classes)
-    arriving = exchange(buffer, "tm", blocks - classes)
+        buffer = buffer + exchange(buffer, "tm", 1 << bit)
+    arriving = exchange(buffer, "tm", 1 << bits - 1)
     share, new_solution, new_residual, conditioned = call(
         functools.partial(update_kernel, width, classes),
         (

time: 52.3 us -> 51.5 us (0.985)
  blocking collectives: 0 us -> 15.8 us
  starting transfers between devices: 17.6 us -> 8.44 us
  waiting for transfers between devices: 23.3 us -> 16.6 us
  Pallas kernels: 7.61 us -> 6.99 us
    all_to_all x0 -> x1, blocking collectives: none -> 15.8 us  [shards(): everyone = lax.all_to_all(send, 'tm', 0, 0)]
    all_to_all x1 -> x0, starting transfers between devices: 8.2 us -> none  [shards(): everyone = lax.all_to_all(send, 'tm', 0, 0)]
    all_to_all x1 -> x0, waiting for transfers between devices: 7.79 us -> none  [shards(): everyone = lax.all_to_all(send, 'tm', 0, 0)]
    ppermute x9, waiting for transfers between devices: 15.5 us -> 16.6 us  [exchange(): return lax.ppermute(value, axis, [(at, at ^ bit) for at in range(size)])]
    ppermute x9, starting transfers between devices: 9.37 us -> 8.44 us  [exchange(): return lax.ppermute(value, axis, [(at, at ^ bit) for at in range(size)])]
    pallas_call x5, Pallas kernels: 7.61 us -> 6.99 us  [call(): pl.pallas_call(kernel, out_shape=outs, in_specs=specs or [vmem()] * len(a...]
  transfers between devices with their start and end apart: 10 -> 9, of which waited for: 8 -> 7; matrix products, arithmetic and copies ran while one was open for 2% -> 2% of each run, Pallas kernels for 3% -> 3%
where the time goes in v6:
time: 51.5 us; the launch traced here: 51.3 us
  waiting for transfers between devices  16.6 us (32%)
  blocking collectives  15.8 us (31%)
  starting transfers between devices  8.44 us (16%)
  Pallas kernels  6.99 us (14%)
  local copies, waits for them, and re-layouts  1.91 us (4%)
  between operations  1.33 us (3%)
    ppermute x9, waiting for transfers between devices, exchange(): return lax.ppermute(value, axis, [(at, at ^ bit) for at in range(size)])  16.6 us
    all_to_all x1, blocking collectives, shards(): everyone = lax.all_to_all(send, 'tm', 0, 0)  15.8 us
    ppermute x9, starting transfers between devices, exchange(): return lax.ppermute(value, axis, [(at, at ^ bit) for at in range(size)])  8.44 us
    pallas_call x5, Pallas kernels, call(): pl.pallas_call(kernel, out_shape=outs, in_specs=specs or [vmem()] * len(a...  6.99 us
    unnamed x3, local copies, waits for them, and re-layouts  1.91 us
  transfers between devices with their start and end apart: 9, of which 7 were waited for; matrix products, arithmetic and copies ran while one was open for 2% of the time, Pallas kernels for 3%

profile of v6, /device:TPU:0, one launch (start us, length us, event | category | flops | bytes accessed | tf_op | source)
XLA Modules:
  0.0 51.3 jit_solution(15447566961730762777)
XLA Ops:
  0.6 3.3 %shard_map.121 = (f32[80,128]{1,0:T(8,128)S(1)}, f32[37,128]{1,0:T(8,128)S(1)}, f32[64,128]{1,0:T(8,128)S(1)}, f32[48,1536]{1,0:T(8,128)S(1)}, bf16[256,5760]{1,0:T(8,128)(2,1)S(1)}) custom-call(s32[1]{0:T(128)} %bitcast.refs_0_, s32[2,4]{1,0:T(2,128)} %bitcast.16, f32[2,2,4]{2,1,0:T(2,128)} %bitcast.14, f32[2,2,4]{2,1,0:T(2,128)} %bitcast.15, ...), custom_call_target="tpu_custom_call" | custom-call | tf_op jit(solution)/shard_map/pallas_call | solution.py:33
  4.0 0.5 %collective-permute-start = (f32[80,128]{1,0:T(8,128)S(1)}, f32[80,128]{1,0:T(8,128)S(1)}, u32[]{:S(2)}, u32[]{:S(2)}) collective-permute-start(f32[80,128]{1,0:T(8,128)S(1)} %get-tuple-element.24.refs_2_), channel_id=1, source_target_pairs={{0,1},{1,0},{2,3},{3,2},{4,5},{5,4},{6,7},{7,6},{8,9},{9,8},{10,11... | collective-permute-start | bytes 122888 | tf_op jit(solution)/shard_map/ppermute | solution.py:411
  5.1 0.2 collective-permute-done.refs_3_
  5.4 0.4 shard_map.122
  5.7 15.8 %all_to_all.5.refs_2_ = f32[16,16,128]{2,1,0:T(8,128)S(1)} all-to-all(f32[16,16,128]{2,1,0:T(8,128)S(1)} %get-tuple-element.25), channel_id=1, replica_groups=mesh['tm'=16,'order'=2] {'tm'}, dimensions={0} | all-to-all | bytes 262144 | tf_op jit(solution)/shard_map/all_to_all | solution.py:483
  21.5 1.7 %shard_map.123 = (f32[4,16,384]{2,1,0:T(8,128)S(1)}, f32[4,16,384]{2,1,0:T(8,128)S(1)}, f32[4,16,384]{2,1,0:T(8,128)S(1)}, f32[4,16,384]{2,1,0:T(8,128)S(1)}) custom-call(s32[1]{0:T(128)} %bitcast.refs_0_, s32[1]{0:T(128)S(6)} %copy.19.refs_0_.refs_1_, f32[16,16,128]{2,1,0:T(8,128)S(1)} %all_to_all.5.refs_2_, f32[64,128]{1,0:T(8,128)S(1)} %get-tuple-element.26.refs_3_, ...), custom_call_target="tpu_custom_call" | custom-call | tf_op jit(solution)/shard_map/pallas_call | solution.py:33
  23.2 1.2 %collective-permute-start.1 = (f32[4,16,384]{2,1,0:T(8,128)S(1)}, f32[4,16,384]{2,1,0:T(8,128)S(1)}, u32[]{:S(2)}, u32[]{:S(2)}) collective-permute-start(f32[4,16,384]{2,1,0:T(8,128)S(1)} %get-tuple-element.31), channel_id=1, source_target_pairs={{0,2},{2,0},{4,6},{6,4},{8,10},{10,8},{12,14},{14,12},{16,18},{18,... | collective-permute-start | bytes 294920 | tf_op jit(solution)/shard_map/ppermute | solution.py:411
  24.3 0.2 collective-permute-start.2
  24.6 2.2 %collective-permute-start.3 = (f32[4,16,384]{2,1,0:T(8,128)S(1)}, f32[4,16,384]{2,1,0:T(8,128)S(1)}, u32[]{:S(2)}, u32[]{:S(2)}) collective-permute-start(f32[4,16,384]{2,1,0:T(8,128)S(1)} %get-tuple-element.33), channel_id=1, source_target_pairs={{0,6},{2,4},{4,2},{6,0},{8,14},{10,12},{12,10},{14,8},{16,22},{18,... | collective-permute-start | bytes 294920 | tf_op jit(solution)/shard_map/ppermute | solution.py:411
  26.7 2.1 %collective-permute-done.1 = f32[4,16,384]{2,1,0:T(8,128)S(1)} collective-permute-done((f32[4,16,384]{2,1,0:T(8,128)S(1)}, f32[4,16,384]{2,1,0:T(8,128)S(1)}, u32[]{:S(2)}, u32[]{:S(2)}) %collective-permute-start.1) | collective-permute-done | bytes 98336 | tf_op jit(solution)/shard_map/ppermute | solution.py:411
  28.9 1.4 %collective-permute-done.2 = f32[4,16,384]{2,1,0:T(8,128)S(1)} collective-permute-done((f32[4,16,384]{2,1,0:T(8,128)S(1)}, f32[4,16,384]{2,1,0:T(8,128)S(1)}, u32[]{:S(2)}, u32[]{:S(2)}) %collective-permute-start.2) | collective-permute-done | bytes 98336 | tf_op jit(solution)/shard_map/ppermute | solution.py:411
  30.2 0.0 collective-permute-done.3
  30.3 0.8 %collective-permute-start.4 = (f32[4,16,384]{2,1,0:T(8,128)S(1)}, f32[4,16,384]{2,1,0:T(8,128)S(1)}, u32[]{:S(2)}, u32[]{:S(2)}) collective-permute-start(f32[4,16,384]{2,1,0:T(8,128)S(1)} %add_add_fusion), channel_id=1, source_target_pairs={{0,8},{2,10},{4,12},{6,14},{8,0},{10,2},{12,4},{14,6},{16,24},{18,... | collective-permute-start | bytes 294920 | tf_op jit(solution)/shard_map/ppermute | solution.py:411
  31.0 3.9 %collective-permute-done.4 = f32[4,16,384]{2,1,0:T(8,128)S(1)} collective-permute-done((f32[4,16,384]{2,1,0:T(8,128)S(1)}, f32[4,16,384]{2,1,0:T(8,128)S(1)}, u32[]{:S(2)}, u32[]{:S(2)}) %collective-permute-start.4) | collective-permute-done | bytes 98336 | tf_op jit(solution)/shard_map/ppermute | solution.py:411
  35.0 0.9 %collective-permute-start.5 = (f32[4,16,384]{2,1,0:T(8,128)S(1)}, f32[4,16,384]{2,1,0:T(8,128)S(1)}, u32[]{:S(2)}, u32[]{:S(2)}) collective-permute-start(f32[4,16,384]{2,1,0:T(8,128)S(1)} %add.27.refs_1_), channel_id=1, source_target_pairs={{0,16},{2,18},{4,20},{6,22},{8,24},{10,26},{12,28},{14,30},{16,0},... | collective-permute-start | bytes 294920 | tf_op jit(solution)/shard_map/ppermute | solution.py:411
  35.9 1.4 %shard_map.124 = (f32[4,16,384]{2,1,0:T(8,128)S(1)}, f32[4,16,384]{2,1,0:T(8,128)S(1)}, f32[1,16,384]{2,1,0:T(8,128)S(1)}, f32[1,16,384]{2,1,0:T(8,128)S(1)}) custom-call(s32[1]{0:T(128)} %bitcast.refs_0_, f32[16,1,5760]{2,1,0:T(1,128)} %refs_1_.2, f32[16,1,5760]{2,1,0:T(1,128)} %refs_2_.1, f32[16,1,5760]{2,1,0:T(1,128)} %refs_3_.1, f32[1,5760]{1,0:T(1,128)} %refs_4_.3), custom_call_target="tpu_custom_call" | custom-call | tf_op jit(solution)/shard_map/pallas_call | solution.py:33
  37.3 4.4 %collective-permute-done.5.refs_2_ = f32[4,16,384]{2,1,0:T(8,128)S(1)} collective-permute-done((f32[4,16,384]{2,1,0:T(8,128)S(1)}, f32[4,16,384]{2,1,0:T(8,128)S(1)}, u32[]{:S(2)}, u32[]{:S(2)}) %collective-permute-start.5) | collective-permute-done | bytes 98336 | tf_op jit(solution)/shard_map/ppermute | solution.py:411
  41.6 0.3 shard_map.125
  41.9 1.3 %collective-permute-start.6 = (f32[16,128]{1,0:T(8,128)S(1)}, f32[16,128]{1,0:T(8,128)S(1)}, u32[]{:S(2)}, u32[]{:S(2)}) collective-permute-start(f32[16,128]{1,0:T(8,128)S(1)} %get-tuple-element.42), channel_id=1, source_target_pairs={{0,2},{2,0},{4,6},{6,4},{8,10},{10,8},{12,14},{14,12},{16,18},{18,... | collective-permute-start | bytes 24584 | tf_op jit(solution)/shard_map/ppermute | solution.py:411
  43.2 2.4 %collective-permute-done.6 = f32[16,128]{1,0:T(8,128)S(1)} collective-permute-done((f32[16,128]{1,0:T(8,128)S(1)}, f32[16,128]{1,0:T(8,128)S(1)}, u32[]{:S(2)}, u32[]{:S(2)}) %collective-permute-start.6) | collective-permute-done | bytes 8224 | tf_op jit(solution)/shard_map/ppermute | solution.py:411
  45.5 1.4 %collective-permute-start.7 = (f32[16,128]{1,0:T(8,128)S(1)}, f32[16,128]{1,0:T(8,128)S(1)}, u32[]{:S(2)}, u32[]{:S(2)}) collective-permute-start(f32[16,128]{1,0:T(8,128)S(1)} %add.28), channel_id=1, source_target_pairs={{0,4},{2,6},{4,0},{6,2},{8,12},{10,14},{12,8},{14,10},{16,20},{18,... | collective-permute-start | bytes 24584 | tf_op jit(solution)/shard_map/ppermute | solution.py:411
  47.0 2.2 %collective-permute-done.7 = f32[16,128]{1,0:T(8,128)S(1)} collective-permute-done((f32[16,128]{1,0:T(8,128)S(1)}, f32[16,128]{1,0:T(8,128)S(1)}, u32[]{:S(2)}, u32[]{:S(2)}) %collective-permute-start.7) | collective-permute-done | bytes 8224 | tf_op jit(solution)/shard_map/ppermute | solution.py:411
  49.2 0.0 collective-permute-start.8
  49.2 0.6 %copy.16 = f32[16,1,360]{2,1,0:T(1,128)} copy(f32[16,1,360]{2,0,1:T(8,128)S(1)} %get-tuple-element.50) | data formatting | bytes 46080
  49.8 0.6 %copy.17 = f32[16,1,360]{2,1,0:T(1,128)} copy(f32[16,1,360]{2,0,1:T(8,128)S(1)} %get-tuple-element.49) | data formatting | bytes 46080
  50.5 0.0 collective-permute-done.8
  50.5 0.1 fusion.1
  50.6 0.1 fusion
  50.7 0.6 %copy.18 = f32[16,1,360]{2,1,0:T(1,128)} copy(f32[16,1,360]{2,0,1:T(8,128)S(1)} %fusion) | data formatting | bytes 46080
  (5 shorter events, 0.0 us)
Async XLA Ops:
  4.0 1.4 %collective-permute-start = (f32[80,128]{1,0:T(8,128)S(1)}, f32[80,128]{1,0:T(8,128)S(1)}, u32[]{:S(2)}, u32[]{:S(2)}) collective-permute-start(f32[80,128]{1,0:T(8,128)S(1)} %get-tuple-element.24.refs_2_), channel_id=1, source_target_pairs={{0,1},{1,0},{2,3},{3,2},{4,5},{5,4},{6,7},{7,6},{8,9},{9,8},{10,11... | collective-permute-start | bytes 122888 | tf_op jit(solution)/shard_map/ppermute | solution.py:411
  23.2 5.7 %collective-permute-start.1 = (f32[4,16,384]{2,1,0:T(8,128)S(1)}, f32[4,16,384]{2,1,0:T(8,128)S(1)}, u32[]{:S(2)}, u32[]{:S(2)}) collective-permute-start(f32[4,16,384]{2,1,0:T(8,128)S(1)} %get-tuple-element.31), channel_id=1, source_target_pairs={{0,2},{2,0},{4,6},{6,4},{8,10},{10,8},{12,14},{14,12},{16,18},{18,... | collective-permute-start | bytes 294920 | tf_op jit(solution)/shard_map/ppermute | solution.py:411
  24.3 5.9 %collective-permute-start.2 = (f32[4,16,384]{2,1,0:T(8,128)S(1)}, f32[4,16,384]{2,1,0:T(8,128)S(1)}, u32[]{:S(2)}, u32[]{:S(2)}) collective-permute-start(f32[4,16,384]{2,1,0:T(8,128)S(1)} %get-tuple-element.32), channel_id=1, source_target_pairs={{0,4},{2,6},{4,0},{6,2},{8,12},{10,14},{12,8},{14,10},{16,20},{18,... | collective-permute-start | bytes 294920 | tf_op jit(solution)/shard_map/ppermute | solution.py:411
  24.6 5.7 %collective-permute-start.3 = (f32[4,16,384]{2,1,0:T(8,128)S(1)}, f32[4,16,384]{2,1,0:T(8,128)S(1)}, u32[]{:S(2)}, u32[]{:S(2)}) collective-permute-start(f32[4,16,384]{2,1,0:T(8,128)S(1)} %get-tuple-element.33), channel_id=1, source_target_pairs={{0,6},{2,4},{4,2},{6,0},{8,14},{10,12},{12,10},{14,8},{16,22},{18,... | collective-permute-start | bytes 294920 | tf_op jit(solution)/shard_map/ppermute | solution.py:411
  30.3 4.7 %collective-permute-start.4 = (f32[4,16,384]{2,1,0:T(8,128)S(1)}, f32[4,16,384]{2,1,0:T(8,128)S(1)}, u32[]{:S(2)}, u32[]{:S(2)}) collective-permute-start(f32[4,16,384]{2,1,0:T(8,128)S(1)} %add_add_fusion), channel_id=1, source_target_pairs={{0,8},{2,10},{4,12},{6,14},{8,0},{10,2},{12,4},{14,6},{16,24},{18,... | collective-permute-start | bytes 294920 | tf_op jit(solution)/shard_map/ppermute | solution.py:411
  35.0 6.6 %collective-permute-start.5 = (f32[4,16,384]{2,1,0:T(8,128)S(1)}, f32[4,16,384]{2,1,0:T(8,128)S(1)}, u32[]{:S(2)}, u32[]{:S(2)}) collective-permute-start(f32[4,16,384]{2,1,0:T(8,128)S(1)} %add.27.refs_1_), channel_id=1, source_target_pairs={{0,16},{2,18},{4,20},{6,22},{8,24},{10,26},{12,28},{14,30},{16,0},... | collective-permute-start | bytes 294920 | tf_op jit(solution)/shard_map/ppermute | solution.py:411
  41.9 3.7 %collective-permute-start.6 = (f32[16,128]{1,0:T(8,128)S(1)}, f32[16,128]{1,0:T(8,128)S(1)}, u32[]{:S(2)}, u32[]{:S(2)}) collective-permute-start(f32[16,128]{1,0:T(8,128)S(1)} %get-tuple-element.42), channel_id=1, source_target_pairs={{0,2},{2,0},{4,6},{6,4},{8,10},{10,8},{12,14},{14,12},{16,18},{18,... | collective-permute-start | bytes 24584 | tf_op jit(solution)/shard_map/ppermute | solution.py:411
  45.5 3.7 %collective-permute-start.7 = (f32[16,128]{1,0:T(8,128)S(1)}, f32[16,128]{1,0:T(8,128)S(1)}, u32[]{:S(2)}, u32[]{:S(2)}) collective-permute-start(f32[16,128]{1,0:T(8,128)S(1)} %add.28), channel_id=1, source_target_pairs={{0,4},{2,6},{4,0},{6,2},{8,12},{10,14},{12,8},{14,10},{16,20},{18,... | collective-permute-start | bytes 24584 | tf_op jit(solution)/shard_map/ppermute | solution.py:411
  49.2 1.3 %collective-permute-start.8 = (f32[16,128]{1,0:T(8,128)S(1)}, f32[16,128]{1,0:T(8,128)S(1)}, u32[]{:S(2)}, u32[]{:S(2)}) collective-permute-start(f32[16,128]{1,0:T(8,128)S(1)} %add.29), channel_id=1, source_target_pairs={{0,1},{1,0},{2,3},{3,2},{4,5},{5,4},{6,7},{7,6},{8,9},{9,8},{10,11... | collective-permute-start | bytes 24584 | tf_op jit(solution)/shard_map/ppermute | solution.py:411

commit v7 on v6

--- a/solution.py
+++ b/solution.py
@@ -358,20 +358,17 @@
     low = jnp.concatenate(
         [turned[at * count : (at + 1) * count] for at in range(half // count)], axis=1
     ).astype(BF16)
-    curve = lax.dot_general(
-        product,
-        jnp.ones((product.shape[0], LANES), F32),
-        (((0,), (0,)), ((), ())),
-        precision=HIGHEST,
-        preferred_element_type=F32,
-    )
-    curvature = curve[:count]
+    along = jnp.sum(product, axis=0, keepdims=True)
+    total = along
     for at in range(1, half // count):
-        curvature = curvature + curve[at * count : (at + 1) * count]
+        total = total + pltpu.roll(along, LANES - at * count, 1)
+    row = lax.broadcasted_iota(jnp.int32, (count, LANES), 0)
+    lane = lax.broadcasted_iota(jnp.int32, (count, LANES), 1)
+    curvature = jnp.sum(jnp.where(row == lane, total, 0.0), axis=1, keepdims=True)
     normal_ref[...] = jnp.dot(low, design_ref[...], preferred_element_type=F32)
     padded = out_refs[0].shape[-1]
     column = lax.broadcasted_iota(jnp.int32, (count, padded), 1)
-    curvature = jnp.broadcast_to(curvature[:, :1], (count, padded))
+    curvature = jnp.broadcast_to(curvature, (count, padded))
     low_bits = mine % first_bits
     for apart, out_ref in enumerate(out_refs):
         for at in range(out_ref.shape[0]):
@@ -404,6 +401,28 @@
     new_residual_ref[...] = changed
     conditioned_ref[...] = diagonal_ref[own] * changed
     new_solution_ref[...] = current_ref[0] + step * search_ref[0]
+
+
+def finish_kernel(parts, *refs):
+    energy_ref, conditioned_ref, search_ref = refs[:3]
+    early_refs, shares = (refs[3:5], refs[5 : 5 + parts])
+    out_hbm, scratch = (refs[5 + parts : 8 + parts], refs[8 + parts :])
+    width = scratch[0].shape[1]
+    sems = scratch[3]
+    copies = [
+        pltpu.make_async_copy(scratch[at], out_hbm[at].at[:, 0, :], sems.at[at]) for at in range(3)
+    ]
+    for source_ref, target_ref, copy in zip(early_refs, scratch, copies):
+        target_ref[...] = source_ref[:, :width]
+        copy.start()
+    energy_next = shares[0][...]
+    for share_ref in shares[1:]:
+        energy_next = energy_next + share_ref[...]
+    turn = (energy_next / energy_ref[...])[:, :1]
+    scratch[2][...] = (conditioned_ref[...] + turn * search_ref[0])[:, :width]
+    copies[2].start()
+    for copy in copies:
+        copy.wait()
 
 
 def exchange(value, axis, bit):
@@ -537,10 +556,17 @@
     )
     for bit in range(halved):
         share = share + exchange(share, "tm", 1 << bit)
-    energy_next = sum(over_order(share))
-    new_direction = conditioned + (energy_next / energy)[:, :1] * search_own[0]
-    return tuple(
-        vector[:, None, :width] for vector in (new_solution, new_residual, new_direction)
+    shares = over_order(share)
+    return call(
+        functools.partial(finish_kernel, len(shares)),
+        (pltpu.HBM((count, 1, width), F32),) * 3,
+        energy,
+        conditioned,
+        search_own,
+        new_solution,
+        new_residual,
+        *shares,
+        scratch=[pltpu.VMEM((count, width), F32)] * 3 + [pltpu.SemaphoreType.DMA((3,))],
     )
 
 

time: 51.5 us -> 51.4 us (level)
  waiting for transfers between devices: 16.6 us -> 18.8 us
  local copies, waits for them, and re-layouts: 1.91 us -> 0 us
  starting transfers between devices: 8.44 us -> 7.55 us
  Pallas kernels: 6.99 us -> 7.64 us
    ppermute x9, waiting for transfers between devices: 16.6 us -> 18.8 us  [exchange(): return lax.ppermute(value, axis, [(at, at ^ bit) for at in range(size)])]
    unnamed x3 -> x0, local copies, waits for them, and re-layouts: 1.91 us -> none
    ppermute x9, starting transfers between devices: 8.44 us -> 7.55 us  [exchange(): return lax.ppermute(value, axis, [(at, at ^ bit) for at in range(size)])]
    pallas_call x5 -> x6, Pallas kernels: 6.99 us -> 7.64 us  [call(): pl.pallas_call(kernel, out_shape=outs, in_specs=specs or [vmem()] * len(a...]
  transfers between devices with their start and end apart: 9 -> 9, of which waited for: 7 -> 9; matrix products, arithmetic and copies ran while one was open for 2% -> 0% of each run, Pallas kernels for 3% -> 3%
where the time goes in v7:
time: 51.4 us; the launch traced here: 51.2 us
  waiting for transfers between devices  18.8 us (37%)
  blocking collectives  15.8 us (31%)
  Pallas kernels  7.64 us (15%)
  starting transfers between devices  7.55 us (15%)
  between operations  1.33 us (3%)
    ppermute x9, waiting for transfers between devices, exchange(): return lax.ppermute(value, axis, [(at, at ^ bit) for at in range(size)])  18.8 us
    all_to_all x1, blocking collectives, shards(): everyone = lax.all_to_all(send, 'tm', 0, 0)  15.8 us
    pallas_call x6, Pallas kernels, call(): pl.pallas_call(kernel, out_shape=outs, in_specs=specs or [vmem()] * len(a...  7.64 us
    ppermute x9, starting transfers between devices, exchange(): return lax.ppermute(value, axis, [(at, at ^ bit) for at in range(size)])  7.55 us
  transfers between devices with their start and end apart: 9, of which 9 were waited for; matrix products, arithmetic and copies ran while one was open for 0% of the time, Pallas kernels for 3%

profile of v7, /device:TPU:0, one launch (start us, length us, event | category | flops | bytes accessed | tf_op | source)
XLA Modules:
  0.0 51.2 jit_solution(8358685150157715258)
XLA Ops:
  0.6 3.3 %shard_map.121 = (f32[80,128]{1,0:T(8,128)S(1)}, f32[37,128]{1,0:T(8,128)S(1)}, f32[64,128]{1,0:T(8,128)S(1)}, f32[48,1536]{1,0:T(8,128)S(1)}, bf16[256,5760]{1,0:T(8,128)(2,1)S(1)}) custom-call(s32[1]{0:T(128)} %bitcast.refs_0_, s32[2,4]{1,0:T(2,128)} %bitcast.8, f32[2,2,4]{2,1,0:T(2,128)} %bitcast.6, f32[2,2,4]{2,1,0:T(2,128)} %bitcast.7, f32[4,9]{1,0:T(4,128)} %refs_4_.2, ...), custom_call_target="tpu_custom_call" | custom-call | tf_op jit(solution)/shard_map/pallas_call | solution.py:33
  4.0 0.5 %collective-permute-start = (f32[80,128]{1,0:T(8,128)S(1)}, f32[80,128]{1,0:T(8,128)S(1)}, u32[]{:S(2)}, u32[]{:S(2)}) collective-permute-start(f32[80,128]{1,0:T(8,128)S(1)} %get-tuple-element.24.refs_2_), channel_id=1, source_target_pairs={{0,1},{1,0},{2,3},{3,2},{4,5},{5,4},{6,7},{7,6},{8,9},{9,8},{10,11... | collective-permute-start | bytes 122888 | tf_op jit(solution)/shard_map/ppermute | solution.py:430
  5.1 0.2 collective-permute-done.refs_3_
  5.4 0.4 shard_map.122
  5.7 15.8 %all_to_all.5.refs_2_ = f32[16,16,128]{2,1,0:T(8,128)S(1)} all-to-all(f32[16,16,128]{2,1,0:T(8,128)S(1)} %get-tuple-element.26), channel_id=1, replica_groups=mesh['tm'=16,'order'=2] {'tm'}, dimensions={0} | all-to-all | bytes 262144 | tf_op jit(solution)/shard_map/all_to_all | solution.py:502
  21.5 1.6 %shard_map.123 = (f32[4,16,384]{2,1,0:T(8,128)S(1)}, f32[4,16,384]{2,1,0:T(8,128)S(1)}, f32[4,16,384]{2,1,0:T(8,128)S(1)}, f32[4,16,384]{2,1,0:T(8,128)S(1)}) custom-call(s32[1]{0:T(128)} %bitcast.refs_0_, s32[1]{0:T(128)S(6)} %copy.13.refs_0_.refs_1_, f32[16,16,128]{2,1,0:T(8,128)S(1)} %all_to_all.5.refs_2_, f32[64,128]{1,0:T(8,128)S(1)} %get-tuple-element.27.refs_3_, ...), custom_call_target="tpu_custom_call" | custom-call | tf_op jit(solution)/shard_map/pallas_call | solution.py:33
  23.1 0.8 %collective-permute-start.3 = (f32[4,16,384]{2,1,0:T(8,128)S(1)}, f32[4,16,384]{2,1,0:T(8,128)S(1)}, u32[]{:S(2)}, u32[]{:S(2)}) collective-permute-start(f32[4,16,384]{2,1,0:T(8,128)S(1)} %get-tuple-element.34), channel_id=1, source_target_pairs={{0,6},{2,4},{4,2},{6,0},{8,14},{10,12},{12,10},{14,8},{16,22},{18,... | collective-permute-start | bytes 294920 | tf_op jit(solution)/shard_map/ppermute | solution.py:430
  23.9 1.5 %collective-permute-start.1 = (f32[4,16,384]{2,1,0:T(8,128)S(1)}, f32[4,16,384]{2,1,0:T(8,128)S(1)}, u32[]{:S(2)}, u32[]{:S(2)}) collective-permute-start(f32[4,16,384]{2,1,0:T(8,128)S(1)} %get-tuple-element.32), channel_id=1, source_target_pairs={{0,2},{2,0},{4,6},{6,4},{8,10},{10,8},{12,14},{14,12},{16,18},{18,... | collective-permute-start | bytes 294920 | tf_op jit(solution)/shard_map/ppermute | solution.py:430
  25.4 1.3 %collective-permute-start.2 = (f32[4,16,384]{2,1,0:T(8,128)S(1)}, f32[4,16,384]{2,1,0:T(8,128)S(1)}, u32[]{:S(2)}, u32[]{:S(2)}) collective-permute-start(f32[4,16,384]{2,1,0:T(8,128)S(1)} %get-tuple-element.33), channel_id=1, source_target_pairs={{0,4},{2,6},{4,0},{6,2},{8,12},{10,14},{12,8},{14,10},{16,20},{18,... | collective-permute-start | bytes 294920 | tf_op jit(solution)/shard_map/ppermute | solution.py:430
  26.7 2.0 %collective-permute-done.3 = f32[4,16,384]{2,1,0:T(8,128)S(1)} collective-permute-done((f32[4,16,384]{2,1,0:T(8,128)S(1)}, f32[4,16,384]{2,1,0:T(8,128)S(1)}, u32[]{:S(2)}, u32[]{:S(2)}) %collective-permute-start.3) | collective-permute-done | bytes 98336 | tf_op jit(solution)/shard_map/ppermute | solution.py:430
  28.7 0.4 collective-permute-done.1
  29.1 0.9 %collective-permute-done.2 = f32[4,16,384]{2,1,0:T(8,128)S(1)} collective-permute-done((f32[4,16,384]{2,1,0:T(8,128)S(1)}, f32[4,16,384]{2,1,0:T(8,128)S(1)}, u32[]{:S(2)}, u32[]{:S(2)}) %collective-permute-start.2) | collective-permute-done | bytes 98336 | tf_op jit(solution)/shard_map/ppermute | solution.py:430
  30.0 0.9 %collective-permute-start.4 = (f32[4,16,384]{2,1,0:T(8,128)S(1)}, f32[4,16,384]{2,1,0:T(8,128)S(1)}, u32[]{:S(2)}, u32[]{:S(2)}) collective-permute-start(f32[4,16,384]{2,1,0:T(8,128)S(1)} %add_add_fusion), channel_id=1, source_target_pairs={{0,8},{2,10},{4,12},{6,14},{8,0},{10,2},{12,4},{14,6},{16,24},{18,... | collective-permute-start | bytes 294920 | tf_op jit(solution)/shard_map/ppermute | solution.py:430
  31.0 4.1 %collective-permute-done.4 = f32[4,16,384]{2,1,0:T(8,128)S(1)} collective-permute-done((f32[4,16,384]{2,1,0:T(8,128)S(1)}, f32[4,16,384]{2,1,0:T(8,128)S(1)}, u32[]{:S(2)}, u32[]{:S(2)}) %collective-permute-start.4) | collective-permute-done | bytes 98336 | tf_op jit(solution)/shard_map/ppermute | solution.py:430
  35.1 1.1 %collective-permute-start.5 = (f32[4,16,384]{2,1,0:T(8,128)S(1)}, f32[4,16,384]{2,1,0:T(8,128)S(1)}, u32[]{:S(2)}, u32[]{:S(2)}) collective-permute-start(f32[4,16,384]{2,1,0:T(8,128)S(1)} %add.21.refs_1_), channel_id=1, source_target_pairs={{0,16},{2,18},{4,20},{6,22},{8,24},{10,26},{12,28},{14,30},{16,0},... | collective-permute-start | bytes 294920 | tf_op jit(solution)/shard_map/ppermute | solution.py:430
  36.2 1.4 %shard_map.124 = (f32[4,16,384]{2,1,0:T(8,128)S(1)}, f32[4,16,384]{2,1,0:T(8,128)S(1)}, f32[1,16,384]{2,1,0:T(8,128)S(1)}, f32[1,16,384]{2,1,0:T(8,128)S(1)}) custom-call(s32[1]{0:T(128)} %bitcast.refs_0_, f32[16,1,5760]{2,1,0:T(1,128)} %refs_1_.2, f32[16,1,5760]{2,1,0:T(1,128)} %refs_2_.1, f32[16,1,5760]{2,1,0:T(1,128)} %refs_3_.1, f32[1,5760]{1,0:T(1,128)} %refs_4_.3), custom_call_target="tpu_custom_call" | custom-call | tf_op jit(solution)/shard_map/pallas_call | solution.py:33
  37.6 4.2 %collective-permute-done.5.refs_2_ = f32[4,16,384]{2,1,0:T(8,128)S(1)} collective-permute-done((f32[4,16,384]{2,1,0:T(8,128)S(1)}, f32[4,16,384]{2,1,0:T(8,128)S(1)}, u32[]{:S(2)}, u32[]{:S(2)}) %collective-permute-start.5) | collective-permute-done | bytes 98336 | tf_op jit(solution)/shard_map/ppermute | solution.py:430
  41.7 0.3 shard_map.125
  42.0 0.5 %collective-permute-start.6 = (f32[16,128]{1,0:T(8,128)S(1)}, f32[16,128]{1,0:T(8,128)S(1)}, u32[]{:S(2)}, u32[]{:S(2)}) collective-permute-start(f32[16,128]{1,0:T(8,128)S(1)} %get-tuple-element.42), channel_id=1, source_target_pairs={{0,2},{2,0},{4,6},{6,4},{8,10},{10,8},{12,14},{14,12},{16,18},{18,... | collective-permute-start | bytes 24584 | tf_op jit(solution)/shard_map/ppermute | solution.py:430
  42.5 3.1 %collective-permute-done.6 = f32[16,128]{1,0:T(8,128)S(1)} collective-permute-done((f32[16,128]{1,0:T(8,128)S(1)}, f32[16,128]{1,0:T(8,128)S(1)}, u32[]{:S(2)}, u32[]{:S(2)}) %collective-permute-start.6) | collective-permute-done | bytes 8224 | tf_op jit(solution)/shard_map/ppermute | solution.py:430
  45.6 0.9 %collective-permute-start.7 = (f32[16,128]{1,0:T(8,128)S(1)}, f32[16,128]{1,0:T(8,128)S(1)}, u32[]{:S(2)}, u32[]{:S(2)}) collective-permute-start(f32[16,128]{1,0:T(8,128)S(1)} %add.22), channel_id=1, source_target_pairs={{0,4},{2,6},{4,0},{6,2},{8,12},{10,14},{12,8},{14,10},{16,20},{18,... | collective-permute-start | bytes 24584 | tf_op jit(solution)/shard_map/ppermute | solution.py:430
  46.6 2.7 %collective-permute-done.7 = f32[16,128]{1,0:T(8,128)S(1)} collective-permute-done((f32[16,128]{1,0:T(8,128)S(1)}, f32[16,128]{1,0:T(8,128)S(1)}, u32[]{:S(2)}, u32[]{:S(2)}) %collective-permute-start.7) | collective-permute-done | bytes 8224 | tf_op jit(solution)/shard_map/ppermute | solution.py:430
  49.3 0.0 collective-permute-start.8
  49.3 1.2 %collective-permute-done.8.refs_6_ = f32[16,128]{1,0:T(8,128)S(1)} collective-permute-done((f32[16,128]{1,0:T(8,128)S(1)}, f32[16,128]{1,0:T(8,128)S(1)}, u32[]{:S(2)}, u32[]{:S(2)}) %collective-permute-start.8) | collective-permute-done | bytes 8224 | tf_op jit(solution)/shard_map/ppermute | solution.py:430
  50.5 0.7 %shard_map.126 = (f32[16,1,360]{2,1,0:T(1,128)}, f32[16,1,360]{2,1,0:T(1,128)}, f32[16,1,360]{2,1,0:T(1,128)}) custom-call(f32[16,128]{1,0:T(8,128)S(1)} %get-tuple-element.25.refs_3_.refs_0_, f32[16,384]{1,0:T(8,128)S(1)} %get-tuple-element.39.refs_1_, f32[1,16,384]{2,1,0:T(8,128)S(1)} %get-tuple-element.38.refs_7_.refs_2_, ...), custom_call_target="tpu_custom_call" | custom-call | tf_op jit(solution)/shard_map/pallas_call | solution.py:33
  (4 shorter events, 0.0 us)
Async XLA Ops:
  4.0 1.4 %collective-permute-start = (f32[80,128]{1,0:T(8,128)S(1)}, f32[80,128]{1,0:T(8,128)S(1)}, u32[]{:S(2)}, u32[]{:S(2)}) collective-permute-start(f32[80,128]{1,0:T(8,128)S(1)} %get-tuple-element.24.refs_2_), channel_id=1, source_target_pairs={{0,1},{1,0},{2,3},{3,2},{4,5},{5,4},{6,7},{7,6},{8,9},{9,8},{10,11... | collective-permute-start | bytes 122888 | tf_op jit(solution)/shard_map/ppermute | solution.py:430
  23.1 5.6 %collective-permute-start.3 = (f32[4,16,384]{2,1,0:T(8,128)S(1)}, f32[4,16,384]{2,1,0:T(8,128)S(1)}, u32[]{:S(2)}, u32[]{:S(2)}) collective-permute-start(f32[4,16,384]{2,1,0:T(8,128)S(1)} %get-tuple-element.34), channel_id=1, source_target_pairs={{0,6},{2,4},{4,2},{6,0},{8,14},{10,12},{12,10},{14,8},{16,22},{18,... | collective-permute-start | bytes 294920 | tf_op jit(solution)/shard_map/ppermute | solution.py:430
  23.9 5.1 %collective-permute-start.1 = (f32[4,16,384]{2,1,0:T(8,128)S(1)}, f32[4,16,384]{2,1,0:T(8,128)S(1)}, u32[]{:S(2)}, u32[]{:S(2)}) collective-permute-start(f32[4,16,384]{2,1,0:T(8,128)S(1)} %get-tuple-element.32), channel_id=1, source_target_pairs={{0,2},{2,0},{4,6},{6,4},{8,10},{10,8},{12,14},{14,12},{16,18},{18,... | collective-permute-start | bytes 294920 | tf_op jit(solution)/shard_map/ppermute | solution.py:430
  25.4 4.6 %collective-permute-start.2 = (f32[4,16,384]{2,1,0:T(8,128)S(1)}, f32[4,16,384]{2,1,0:T(8,128)S(1)}, u32[]{:S(2)}, u32[]{:S(2)}) collective-permute-start(f32[4,16,384]{2,1,0:T(8,128)S(1)} %get-tuple-element.33), channel_id=1, source_target_pairs={{0,4},{2,6},{4,0},{6,2},{8,12},{10,14},{12,8},{14,10},{16,20},{18,... | collective-permute-start | bytes 294920 | tf_op jit(solution)/shard_map/ppermute | solution.py:430
  30.0 5.0 %collective-permute-start.4 = (f32[4,16,384]{2,1,0:T(8,128)S(1)}, f32[4,16,384]{2,1,0:T(8,128)S(1)}, u32[]{:S(2)}, u32[]{:S(2)}) collective-permute-start(f32[4,16,384]{2,1,0:T(8,128)S(1)} %add_add_fusion), channel_id=1, source_target_pairs={{0,8},{2,10},{4,12},{6,14},{8,0},{10,2},{12,4},{14,6},{16,24},{18,... | collective-permute-start | bytes 294920 | tf_op jit(solution)/shard_map/ppermute | solution.py:430
  35.1 6.6 %collective-permute-start.5 = (f32[4,16,384]{2,1,0:T(8,128)S(1)}, f32[4,16,384]{2,1,0:T(8,128)S(1)}, u32[]{:S(2)}, u32[]{:S(2)}) collective-permute-start(f32[4,16,384]{2,1,0:T(8,128)S(1)} %add.21.refs_1_), channel_id=1, source_target_pairs={{0,16},{2,18},{4,20},{6,22},{8,24},{10,26},{12,28},{14,30},{16,0},... | collective-permute-start | bytes 294920 | tf_op jit(solution)/shard_map/ppermute | solution.py:430
  42.0 3.7 %collective-permute-start.6 = (f32[16,128]{1,0:T(8,128)S(1)}, f32[16,128]{1,0:T(8,128)S(1)}, u32[]{:S(2)}, u32[]{:S(2)}) collective-permute-start(f32[16,128]{1,0:T(8,128)S(1)} %get-tuple-element.42), channel_id=1, source_target_pairs={{0,2},{2,0},{4,6},{6,4},{8,10},{10,8},{12,14},{14,12},{16,18},{18,... | collective-permute-start | bytes 24584 | tf_op jit(solution)/shard_map/ppermute | solution.py:430
  45.6 3.7 %collective-permute-start.7 = (f32[16,128]{1,0:T(8,128)S(1)}, f32[16,128]{1,0:T(8,128)S(1)}, u32[]{:S(2)}, u32[]{:S(2)}) collective-permute-start(f32[16,128]{1,0:T(8,128)S(1)} %add.22), channel_id=1, source_target_pairs={{0,4},{2,6},{4,0},{6,2},{8,12},{10,14},{12,8},{14,10},{16,20},{18,... | collective-permute-start | bytes 24584 | tf_op jit(solution)/shard_map/ppermute | solution.py:430
  49.3 1.2 %collective-permute-start.8 = (f32[16,128]{1,0:T(8,128)S(1)}, f32[16,128]{1,0:T(8,128)S(1)}, u32[]{:S(2)}, u32[]{:S(2)}) collective-permute-start(f32[16,128]{1,0:T(8,128)S(1)} %add.23.refs_5_), channel_id=1, source_target_pairs={{0,1},{1,0},{2,3},{3,2},{4,5},{5,4},{6,7},{7,6},{8,9},{9,8},{10,11... | collective-permute-start | bytes 24584 | tf_op jit(solution)/shard_map/ppermute | solution.py:430

commit v8 on v7

--- a/solution.py
+++ b/solution.py
@@ -306,18 +306,20 @@
 
 def normal_kernel(kinds, width, first_bits, *refs):
     place_ref, counts_ref, all_ref, keep_ref, spread_ref, steps_ref, design_ref = refs[:7]
-    out_refs, (entering_ref, normal_ref) = (refs[7:-2], refs[-2:])
+    out_refs, (entering_ref, cut_ref) = (refs[7:-2], refs[-2:])
     blocks = all_ref.shape[0]
     mine = place_ref[0]
     half = LANES // 2
 
     def apply(which, state):
-        total = None
+        terms = []
         for at in range(kinds):
             column = steps_ref[which * SLOT : (which + 1) * SLOT, at * LANES : (at + 1) * LANES]
-            term = column * state[at : at + 1]
-            total = term if total is None else total + term
-        return total
+            terms.append(column * state[at : at + 1])
+        while len(terms) > 1:
+            pairs = [sum(terms[at : at + 2][1:], terms[at]) for at in range(0, len(terms), 2)]
+            terms = pairs
+        return terms[0]
 
     def advance(block, state):
         entering_ref[block] = state
@@ -365,16 +367,23 @@
     row = lax.broadcasted_iota(jnp.int32, (count, LANES), 0)
     lane = lax.broadcasted_iota(jnp.int32, (count, LANES), 1)
     curvature = jnp.sum(jnp.where(row == lane, total, 0.0), axis=1, keepdims=True)
-    normal_ref[...] = jnp.dot(low, design_ref[...], preferred_element_type=F32)
+    normal = jnp.dot(low, design_ref[...], preferred_element_type=F32)
     padded = out_refs[0].shape[-1]
     column = lax.broadcasted_iota(jnp.int32, (count, padded), 1)
     curvature = jnp.broadcast_to(curvature, (count, padded))
     low_bits = mine % first_bits
+    wide = normal.shape[1]
+    window = min(padded + LANES, wide)
+    for block in range(wide // width):
+        start = block * width
+        base = min(start // LANES * LANES, wide - window)
+        part = normal[:, base : base + window]
+        if start != base:
+            part = pltpu.roll(part, window - (start - base), 1)
+        cut_ref[block] = jnp.where(column < width, part[:, :padded], curvature)
     for apart, out_ref in enumerate(out_refs):
         for at in range(out_ref.shape[0]):
-            block = at * first_bits + (low_bits ^ apart)
-            part = column_block(normal_ref, block, width, padded)
-            out_ref[at] = jnp.where(column < width, part, curvature)
+            out_ref[at] = cut_ref[at * first_bits + (low_bits ^ apart)]
 
 
 def update_kernel(width, first_bits, *refs):
@@ -511,7 +520,7 @@
         steps,
         design_kept,
         specs=[smem()] * 2 + [vmem()] * 5,
-        scratch=[pltpu.VMEM((blocks, SLOT, LANES), F32), pltpu.VMEM((count, wide), F32)],
+        scratch=[pltpu.VMEM((blocks, SLOT, LANES), F32), pltpu.VMEM((blocks, count, padded), F32)],
     )
     diagonal_parts, remaining_parts, search_own, current_own = call(
         functools.partial(slices_kernel, width, classes),

time: 51.4 us -> 51.2 us (level)
  no operation moved by 1% of the time
where the time goes in v8:
time: 51.2 us; the launch traced here: 51 us
  waiting for transfers between devices  18.8 us (37%)
  blocking collectives  15.8 us (31%)
  starting transfers between devices  7.55 us (15%)
  Pallas kernels  7.44 us (15%)
  between operations  1.33 us (3%)
    ppermute x9, waiting for transfers between devices, exchange(): return lax.ppermute(value, axis, [(at, at ^ bit) for at in range(size)])  18.8 us
    all_to_all x1, blocking collectives, shards(): everyone = lax.all_to_all(send, 'tm', 0, 0)  15.8 us
    ppermute x9, starting transfers between devices, exchange(): return lax.ppermute(value, axis, [(at, at ^ bit) for at in range(size)])  7.55 us
    pallas_call x6, Pallas kernels, call(): pl.pallas_call(kernel, out_shape=outs, in_specs=specs or [vmem()] * len(a...  7.44 us
  transfers between devices with their start and end apart: 9, of which 9 were waited for; matrix products, arithmetic and copies ran while one was open for 0% of the time, Pallas kernels for 3%

profile of v8, /device:TPU:0, one launch (start us, length us, event | category | flops | bytes accessed | tf_op | source)
XLA Modules:
  0.0 51.0 jit_solution(4983813255711639706)
XLA Ops:
  0.6 3.3 %shard_map.121 = (f32[80,128]{1,0:T(8,128)S(1)}, f32[37,128]{1,0:T(8,128)S(1)}, f32[64,128]{1,0:T(8,128)S(1)}, f32[48,1536]{1,0:T(8,128)S(1)}, bf16[256,5760]{1,0:T(8,128)(2,1)S(1)}) custom-call(s32[1]{0:T(128)} %bitcast.refs_0_, s32[2,4]{1,0:T(2,128)} %bitcast.8, f32[2,2,4]{2,1,0:T(2,128)} %bitcast.6, f32[2,2,4]{2,1,0:T(2,128)} %bitcast.7, f32[4,9]{1,0:T(4,128)} %refs_4_.2, ...), custom_call_target="tpu_custom_call" | custom-call | tf_op jit(solution)/shard_map/pallas_call | solution.py:33
  4.0 0.5 %collective-permute-start = (f32[80,128]{1,0:T(8,128)S(1)}, f32[80,128]{1,0:T(8,128)S(1)}, u32[]{:S(2)}, u32[]{:S(2)}) collective-permute-start(f32[80,128]{1,0:T(8,128)S(1)} %get-tuple-element.24.refs_2_), channel_id=1, source_target_pairs={{0,1},{1,0},{2,3},{3,2},{4,5},{5,4},{6,7},{7,6},{8,9},{9,8},{10,11... | collective-permute-start | bytes 122888 | tf_op jit(solution)/shard_map/ppermute | solution.py:439
  5.1 0.2 collective-permute-done.refs_3_
  5.4 0.4 shard_map.122
  5.7 15.8 %all_to_all.5.refs_2_ = f32[16,16,128]{2,1,0:T(8,128)S(1)} all-to-all(f32[16,16,128]{2,1,0:T(8,128)S(1)} %get-tuple-element.26), channel_id=1, replica_groups=mesh['tm'=16,'order'=2] {'tm'}, dimensions={0} | all-to-all | bytes 262144 | tf_op jit(solution)/shard_map/all_to_all | solution.py:511
  21.5 1.4 %shard_map.123 = (f32[4,16,384]{2,1,0:T(8,128)S(1)}, f32[4,16,384]{2,1,0:T(8,128)S(1)}, f32[4,16,384]{2,1,0:T(8,128)S(1)}, f32[4,16,384]{2,1,0:T(8,128)S(1)}) custom-call(s32[1]{0:T(128)} %bitcast.refs_0_, s32[1]{0:T(128)S(6)} %copy.13.refs_0_.refs_1_, f32[16,16,128]{2,1,0:T(8,128)S(1)} %all_to_all.5.refs_2_, f32[64,128]{1,0:T(8,128)S(1)} %get-tuple-element.27.refs_3_, ...), custom_call_target="tpu_custom_call" | custom-call | tf_op jit(solution)/shard_map/pallas_call | solution.py:33
  22.9 0.8 %collective-permute-start.3 = (f32[4,16,384]{2,1,0:T(8,128)S(1)}, f32[4,16,384]{2,1,0:T(8,128)S(1)}, u32[]{:S(2)}, u32[]{:S(2)}) collective-permute-start(f32[4,16,384]{2,1,0:T(8,128)S(1)} %get-tuple-element.34), channel_id=1, source_target_pairs={{0,6},{2,4},{4,2},{6,0},{8,14},{10,12},{12,10},{14,8},{16,22},{18,... | collective-permute-start | bytes 294920 | tf_op jit(solution)/shard_map/ppermute | solution.py:439
  23.7 1.5 %collective-permute-start.1 = (f32[4,16,384]{2,1,0:T(8,128)S(1)}, f32[4,16,384]{2,1,0:T(8,128)S(1)}, u32[]{:S(2)}, u32[]{:S(2)}) collective-permute-start(f32[4,16,384]{2,1,0:T(8,128)S(1)} %get-tuple-element.32), channel_id=1, source_target_pairs={{0,2},{2,0},{4,6},{6,4},{8,10},{10,8},{12,14},{14,12},{16,18},{18,... | collective-permute-start | bytes 294920 | tf_op jit(solution)/shard_map/ppermute | solution.py:439
  25.2 1.3 %collective-permute-start.2 = (f32[4,16,384]{2,1,0:T(8,128)S(1)}, f32[4,16,384]{2,1,0:T(8,128)S(1)}, u32[]{:S(2)}, u32[]{:S(2)}) collective-permute-start(f32[4,16,384]{2,1,0:T(8,128)S(1)} %get-tuple-element.33), channel_id=1, source_target_pairs={{0,4},{2,6},{4,0},{6,2},{8,12},{10,14},{12,8},{14,10},{16,20},{18,... | collective-permute-start | bytes 294920 | tf_op jit(solution)/shard_map/ppermute | solution.py:439
  26.5 2.0 %collective-permute-done.3 = f32[4,16,384]{2,1,0:T(8,128)S(1)} collective-permute-done((f32[4,16,384]{2,1,0:T(8,128)S(1)}, f32[4,16,384]{2,1,0:T(8,128)S(1)}, u32[]{:S(2)}, u32[]{:S(2)}) %collective-permute-start.3) | collective-permute-done | bytes 98336 | tf_op jit(solution)/shard_map/ppermute | solution.py:439
  28.5 0.4 collective-permute-done.1
  28.9 0.9 %collective-permute-done.2 = f32[4,16,384]{2,1,0:T(8,128)S(1)} collective-permute-done((f32[4,16,384]{2,1,0:T(8,128)S(1)}, f32[4,16,384]{2,1,0:T(8,128)S(1)}, u32[]{:S(2)}, u32[]{:S(2)}) %collective-permute-start.2) | collective-permute-done | bytes 98336 | tf_op jit(solution)/shard_map/ppermute | solution.py:439
  29.8 0.9 %collective-permute-start.4 = (f32[4,16,384]{2,1,0:T(8,128)S(1)}, f32[4,16,384]{2,1,0:T(8,128)S(1)}, u32[]{:S(2)}, u32[]{:S(2)}) collective-permute-start(f32[4,16,384]{2,1,0:T(8,128)S(1)} %add_add_fusion), channel_id=1, source_target_pairs={{0,8},{2,10},{4,12},{6,14},{8,0},{10,2},{12,4},{14,6},{16,24},{18,... | collective-permute-start | bytes 294920 | tf_op jit(solution)/shard_map/ppermute | solution.py:439
  30.8 4.1 %collective-permute-done.4 = f32[4,16,384]{2,1,0:T(8,128)S(1)} collective-permute-done((f32[4,16,384]{2,1,0:T(8,128)S(1)}, f32[4,16,384]{2,1,0:T(8,128)S(1)}, u32[]{:S(2)}, u32[]{:S(2)}) %collective-permute-start.4) | collective-permute-done | bytes 98336 | tf_op jit(solution)/shard_map/ppermute | solution.py:439
  34.9 1.1 %collective-permute-start.5 = (f32[4,16,384]{2,1,0:T(8,128)S(1)}, f32[4,16,384]{2,1,0:T(8,128)S(1)}, u32[]{:S(2)}, u32[]{:S(2)}) collective-permute-start(f32[4,16,384]{2,1,0:T(8,128)S(1)} %add.21.refs_1_), channel_id=1, source_target_pairs={{0,16},{2,18},{4,20},{6,22},{8,24},{10,26},{12,28},{14,30},{16,0},... | collective-permute-start | bytes 294920 | tf_op jit(solution)/shard_map/ppermute | solution.py:439
  36.0 1.4 %shard_map.124 = (f32[4,16,384]{2,1,0:T(8,128)S(1)}, f32[4,16,384]{2,1,0:T(8,128)S(1)}, f32[1,16,384]{2,1,0:T(8,128)S(1)}, f32[1,16,384]{2,1,0:T(8,128)S(1)}) custom-call(s32[1]{0:T(128)} %bitcast.refs_0_, f32[16,1,5760]{2,1,0:T(1,128)} %refs_1_.2, f32[16,1,5760]{2,1,0:T(1,128)} %refs_2_.1, f32[16,1,5760]{2,1,0:T(1,128)} %refs_3_.1, f32[1,5760]{1,0:T(1,128)} %refs_4_.3), custom_call_target="tpu_custom_call" | custom-call | tf_op jit(solution)/shard_map/pallas_call | solution.py:33
  37.4 4.2 %collective-permute-done.5.refs_2_ = f32[4,16,384]{2,1,0:T(8,128)S(1)} collective-permute-done((f32[4,16,384]{2,1,0:T(8,128)S(1)}, f32[4,16,384]{2,1,0:T(8,128)S(1)}, u32[]{:S(2)}, u32[]{:S(2)}) %collective-permute-start.5) | collective-permute-done | bytes 98336 | tf_op jit(solution)/shard_map/ppermute | solution.py:439
  41.5 0.3 shard_map.125
  41.8 0.5 %collective-permute-start.6 = (f32[16,128]{1,0:T(8,128)S(1)}, f32[16,128]{1,0:T(8,128)S(1)}, u32[]{:S(2)}, u32[]{:S(2)}) collective-permute-start(f32[16,128]{1,0:T(8,128)S(1)} %get-tuple-element.42), channel_id=1, source_target_pairs={{0,2},{2,0},{4,6},{6,4},{8,10},{10,8},{12,14},{14,12},{16,18},{18,... | collective-permute-start | bytes 24584 | tf_op jit(solution)/shard_map/ppermute | solution.py:439
  42.3 3.1 %collective-permute-done.6 = f32[16,128]{1,0:T(8,128)S(1)} collective-permute-done((f32[16,128]{1,0:T(8,128)S(1)}, f32[16,128]{1,0:T(8,128)S(1)}, u32[]{:S(2)}, u32[]{:S(2)}) %collective-permute-start.6) | collective-permute-done | bytes 8224 | tf_op jit(solution)/shard_map/ppermute | solution.py:439
  45.4 0.9 %collective-permute-start.7 = (f32[16,128]{1,0:T(8,128)S(1)}, f32[16,128]{1,0:T(8,128)S(1)}, u32[]{:S(2)}, u32[]{:S(2)}) collective-permute-start(f32[16,128]{1,0:T(8,128)S(1)} %add.22), channel_id=1, source_target_pairs={{0,4},{2,6},{4,0},{6,2},{8,12},{10,14},{12,8},{14,10},{16,20},{18,... | collective-permute-start | bytes 24584 | tf_op jit(solution)/shard_map/ppermute | solution.py:439
  46.4 2.7 %collective-permute-done.7 = f32[16,128]{1,0:T(8,128)S(1)} collective-permute-done((f32[16,128]{1,0:T(8,128)S(1)}, f32[16,128]{1,0:T(8,128)S(1)}, u32[]{:S(2)}, u32[]{:S(2)}) %collective-permute-start.7) | collective-permute-done | bytes 8224 | tf_op jit(solution)/shard_map/ppermute | solution.py:439
  49.1 0.0 collective-permute-start.8
  49.1 1.2 %collective-permute-done.8.refs_6_ = f32[16,128]{1,0:T(8,128)S(1)} collective-permute-done((f32[16,128]{1,0:T(8,128)S(1)}, f32[16,128]{1,0:T(8,128)S(1)}, u32[]{:S(2)}, u32[]{:S(2)}) %collective-permute-start.8) | collective-permute-done | bytes 8224 | tf_op jit(solution)/shard_map/ppermute | solution.py:439
  50.3 0.7 %shard_map.126 = (f32[16,1,360]{2,1,0:T(1,128)}, f32[16,1,360]{2,1,0:T(1,128)}, f32[16,1,360]{2,1,0:T(1,128)}) custom-call(f32[16,128]{1,0:T(8,128)S(1)} %get-tuple-element.25.refs_3_.refs_0_, f32[16,384]{1,0:T(8,128)S(1)} %get-tuple-element.39.refs_1_, f32[1,16,384]{2,1,0:T(8,128)S(1)} %get-tuple-element.38.refs_7_.refs_2_, ...), custom_call_target="tpu_custom_call" | custom-call | tf_op jit(solution)/shard_map/pallas_call | solution.py:33
  (4 shorter events, 0.0 us)
Async XLA Ops:
  4.0 1.4 %collective-permute-start = (f32[80,128]{1,0:T(8,128)S(1)}, f32[80,128]{1,0:T(8,128)S(1)}, u32[]{:S(2)}, u32[]{:S(2)}) collective-permute-start(f32[80,128]{1,0:T(8,128)S(1)} %get-tuple-element.24.refs_2_), channel_id=1, source_target_pairs={{0,1},{1,0},{2,3},{3,2},{4,5},{5,4},{6,7},{7,6},{8,9},{9,8},{10,11... | collective-permute-start | bytes 122888 | tf_op jit(solution)/shard_map/ppermute | solution.py:439
  22.9 5.6 %collective-permute-start.3 = (f32[4,16,384]{2,1,0:T(8,128)S(1)}, f32[4,16,384]{2,1,0:T(8,128)S(1)}, u32[]{:S(2)}, u32[]{:S(2)}) collective-permute-start(f32[4,16,384]{2,1,0:T(8,128)S(1)} %get-tuple-element.34), channel_id=1, source_target_pairs={{0,6},{2,4},{4,2},{6,0},{8,14},{10,12},{12,10},{14,8},{16,22},{18,... | collective-permute-start | bytes 294920 | tf_op jit(solution)/shard_map/ppermute | solution.py:439
  23.7 5.2 %collective-permute-start.1 = (f32[4,16,384]{2,1,0:T(8,128)S(1)}, f32[4,16,384]{2,1,0:T(8,128)S(1)}, u32[]{:S(2)}, u32[]{:S(2)}) collective-permute-start(f32[4,16,384]{2,1,0:T(8,128)S(1)} %get-tuple-element.32), channel_id=1, source_target_pairs={{0,2},{2,0},{4,6},{6,4},{8,10},{10,8},{12,14},{14,12},{16,18},{18,... | collective-permute-start | bytes 294920 | tf_op jit(solution)/shard_map/ppermute | solution.py:439
  25.2 4.6 %collective-permute-start.2 = (f32[4,16,384]{2,1,0:T(8,128)S(1)}, f32[4,16,384]{2,1,0:T(8,128)S(1)}, u32[]{:S(2)}, u32[]{:S(2)}) collective-permute-start(f32[4,16,384]{2,1,0:T(8,128)S(1)} %get-tuple-element.33), channel_id=1, source_target_pairs={{0,4},{2,6},{4,0},{6,2},{8,12},{10,14},{12,8},{14,10},{16,20},{18,... | collective-permute-start | bytes 294920 | tf_op jit(solution)/shard_map/ppermute | solution.py:439
  29.8 5.0 %collective-permute-start.4 = (f32[4,16,384]{2,1,0:T(8,128)S(1)}, f32[4,16,384]{2,1,0:T(8,128)S(1)}, u32[]{:S(2)}, u32[]{:S(2)}) collective-permute-start(f32[4,16,384]{2,1,0:T(8,128)S(1)} %add_add_fusion), channel_id=1, source_target_pairs={{0,8},{2,10},{4,12},{6,14},{8,0},{10,2},{12,4},{14,6},{16,24},{18,... | collective-permute-start | bytes 294920 | tf_op jit(solution)/shard_map/ppermute | solution.py:439
  34.9 6.6 %collective-permute-start.5 = (f32[4,16,384]{2,1,0:T(8,128)S(1)}, f32[4,16,384]{2,1,0:T(8,128)S(1)}, u32[]{:S(2)}, u32[]{:S(2)}) collective-permute-start(f32[4,16,384]{2,1,0:T(8,128)S(1)} %add.21.refs_1_), channel_id=1, source_target_pairs={{0,16},{2,18},{4,20},{6,22},{8,24},{10,26},{12,28},{14,30},{16,0},... | collective-permute-start | bytes 294920 | tf_op jit(solution)/shard_map/ppermute | solution.py:439
  41.8 3.7 %collective-permute-start.6 = (f32[16,128]{1,0:T(8,128)S(1)}, f32[16,128]{1,0:T(8,128)S(1)}, u32[]{:S(2)}, u32[]{:S(2)}) collective-permute-start(f32[16,128]{1,0:T(8,128)S(1)} %get-tuple-element.42), channel_id=1, source_target_pairs={{0,2},{2,0},{4,6},{6,4},{8,10},{10,8},{12,14},{14,12},{16,18},{18,... | collective-permute-start | bytes 24584 | tf_op jit(solution)/shard_map/ppermute | solution.py:439
  45.4 3.7 %collective-permute-start.7 = (f32[16,128]{1,0:T(8,128)S(1)}, f32[16,128]{1,0:T(8,128)S(1)}, u32[]{:S(2)}, u32[]{:S(2)}) collective-permute-start(f32[16,128]{1,0:T(8,128)S(1)} %add.22), channel_id=1, source_target_pairs={{0,4},{2,6},{4,0},{6,2},{8,12},{10,14},{12,8},{14,10},{16,20},{18,... | collective-permute-start | bytes 24584 | tf_op jit(solution)/shard_map/ppermute | solution.py:439
  49.1 1.2 %collective-permute-start.8 = (f32[16,128]{1,0:T(8,128)S(1)}, f32[16,128]{1,0:T(8,128)S(1)}, u32[]{:S(2)}, u32[]{:S(2)}) collective-permute-start(f32[16,128]{1,0:T(8,128)S(1)} %add.23.refs_5_), channel_id=1, source_target_pairs={{0,1},{1,0},{2,3},{3,2},{4,5},{5,4},{6,7},{7,6},{8,9},{9,8},{10,11... | collective-permute-start | bytes 24584 | tf_op jit(solution)/shard_map/ppermute | solution.py:439

commit v9 on v8

--- a/solution.py
+++ b/solution.py
@@ -44,6 +44,11 @@
 
 def shape(*dims):
     return jax.ShapeDtypeStruct(dims, F32)
+
+
+def halves(value):
+    high = value.astype(BF16)
+    return (high, (value - high.astype(F32)).astype(BF16))
 
 
 def column_block(source_ref, block, width, padded):
@@ -228,7 +233,9 @@
     filtered, ends = forward_block(nothing, units[: sections + 1], history, poles, zeros, taps)
     local, heads = backward_block(filtered, None, poles, zeros, taps)
     reply, replies = backward_block(nothing, units, poles, zeros, taps)
-    spread_ref[...] = jnp.where(lane < half, pltpu.roll(local, half, 1), reply)
+    spread = jnp.where(lane < half, pltpu.roll(local, half, 1), reply)
+    spread_high, spread_low = halves(spread)
+    spread_ref[...] = jnp.concatenate([spread_high, spread_high, spread_low], axis=1)
     stacked = jnp.concatenate([pack(ends), pack(heads), pack(replies)], axis=0)
     source = lax.broadcasted_iota(jnp.int32, (LANES, kinds * LANES), 0)
     target = lax.broadcasted_iota(jnp.int32, (LANES, kinds * LANES), 1)
@@ -344,10 +351,10 @@
         jnp.where(own, jnp.concatenate([state] * groups, axis=0), 0.0)
         for state in (entering, leaving)
     ]
+    state_high, state_low = halves(jnp.concatenate(expanded, axis=0))
     correction = jnp.dot(
         spread_ref[...],
-        jnp.concatenate(expanded, axis=0),
-        precision=HIGHEST,
+        jnp.concatenate([state_high, state_low, state_high], axis=0),
         preferred_element_type=F32,
     )
     kept = keep_ref[...]
@@ -484,7 +491,7 @@
         (
             shape(length + count, LANES),
             shape(sections * (levels + 1) + taps_count, LANES),
-            shape(length, LANES),
+            jax.ShapeDtypeStruct((length, 3 * LANES), BF16),
             shape(3 * SLOT, kinds * LANES),
             jax.ShapeDtypeStruct((components * length, wide), BF16),
         ),

time: 51.2 us -> 51.1 us (level)
  no operation moved by 1% of the time
where the time goes in v9:
time: 51.1 us; the launch traced here: 50.9 us
  waiting for transfers between devices  18.6 us (36%)
  blocking collectives  15.8 us (31%)
  starting transfers between devices  7.77 us (15%)
  Pallas kernels  7.33 us (14%)
  between operations  1.33 us (3%)
    ppermute x9, waiting for transfers between devices, exchange(): return lax.ppermute(value, axis, [(at, at ^ bit) for at in range(size)])  18.6 us
    all_to_all x1, blocking collectives, shards(): everyone = lax.all_to_all(send, 'tm', 0, 0)  15.8 us
    ppermute x9, starting transfers between devices, exchange(): return lax.ppermute(value, axis, [(at, at ^ bit) for at in range(size)])  7.77 us
    pallas_call x6, Pallas kernels, call(): pl.pallas_call(kernel, out_shape=outs, in_specs=specs or [vmem()] * len(a...  7.33 us
  transfers between devices with their start and end apart: 9, of which 9 were waited for; matrix products, arithmetic and copies ran while one was open for 0% of the time, Pallas kernels for 3%

profile of v9, /device:TPU:0, one launch (start us, length us, event | category | flops | bytes accessed | tf_op | source)
XLA Modules:
  0.0 50.9 jit_solution(13408268782045272003)
XLA Ops:
  0.6 3.3 %shard_map.121 = (f32[80,128]{1,0:T(8,128)S(1)}, f32[37,128]{1,0:T(8,128)S(1)}, bf16[64,384]{1,0:T(8,128)(2,1)S(1)}, f32[48,1536]{1,0:T(8,128)S(1)}, bf16[256,5760]{1,0:T(8,128)(2,1)S(1)}) custom-call(s32[1]{0:T(128)} %bitcast.refs_0_, s32[2,4]{1,0:T(2,128)} %bitcast.8, f32[2,2,4]{2,1,0:T(2,128)} %bitcast.6, f32[2,2,4]{2,1,0:T(2,128)} %bitcast.7, ...), custom_call_target="tpu_custom_call" | custom-call | tf_op jit(solution)/shard_map/pallas_call | solution.py:33
  4.0 0.5 %collective-permute-start = (f32[80,128]{1,0:T(8,128)S(1)}, f32[80,128]{1,0:T(8,128)S(1)}, u32[]{:S(2)}, u32[]{:S(2)}) collective-permute-start(f32[80,128]{1,0:T(8,128)S(1)} %get-tuple-element.24.refs_2_), channel_id=1, source_target_pairs={{0,1},{1,0},{2,3},{3,2},{4,5},{5,4},{6,7},{7,6},{8,9},{9,8},{10,11... | collective-permute-start | bytes 122888 | tf_op jit(solution)/shard_map/ppermute | solution.py:446
  5.1 0.2 collective-permute-done.refs_3_
  5.4 0.4 shard_map.122
  5.7 15.8 %all_to_all.5.refs_2_ = f32[16,16,128]{2,1,0:T(8,128)S(1)} all-to-all(f32[16,16,128]{2,1,0:T(8,128)S(1)} %get-tuple-element.26), channel_id=1, replica_groups=mesh['tm'=16,'order'=2] {'tm'}, dimensions={0} | all-to-all | bytes 262144 | tf_op jit(solution)/shard_map/all_to_all | solution.py:518
  21.5 1.3 %shard_map.123 = (f32[4,16,384]{2,1,0:T(8,128)S(1)}, f32[4,16,384]{2,1,0:T(8,128)S(1)}, f32[4,16,384]{2,1,0:T(8,128)S(1)}, f32[4,16,384]{2,1,0:T(8,128)S(1)}) custom-call(s32[1]{0:T(128)} %bitcast.refs_0_, s32[1]{0:T(128)S(6)} %copy.13.refs_0_.refs_1_, f32[16,16,128]{2,1,0:T(8,128)S(1)} %all_to_all.5.refs_2_, f32[64,128]{1,0:T(8,128)S(1)} %get-tuple-element.27.refs_3_, ...), custom_call_target="tpu_custom_call" | custom-call | tf_op jit(solution)/shard_map/pallas_call | solution.py:33
  22.8 0.8 %collective-permute-start.3 = (f32[4,16,384]{2,1,0:T(8,128)S(1)}, f32[4,16,384]{2,1,0:T(8,128)S(1)}, u32[]{:S(2)}, u32[]{:S(2)}) collective-permute-start(f32[4,16,384]{2,1,0:T(8,128)S(1)} %get-tuple-element.34), channel_id=1, source_target_pairs={{0,6},{2,4},{4,2},{6,0},{8,14},{10,12},{12,10},{14,8},{16,22},{18,... | collective-permute-start | bytes 294920 | tf_op jit(solution)/shard_map/ppermute | solution.py:446
  23.6 1.5 %collective-permute-start.1 = (f32[4,16,384]{2,1,0:T(8,128)S(1)}, f32[4,16,384]{2,1,0:T(8,128)S(1)}, u32[]{:S(2)}, u32[]{:S(2)}) collective-permute-start(f32[4,16,384]{2,1,0:T(8,128)S(1)} %get-tuple-element.32), channel_id=1, source_target_pairs={{0,2},{2,0},{4,6},{6,4},{8,10},{10,8},{12,14},{14,12},{16,18},{18,... | collective-permute-start | bytes 294920 | tf_op jit(solution)/shard_map/ppermute | solution.py:446
  25.1 1.3 %collective-permute-start.2 = (f32[4,16,384]{2,1,0:T(8,128)S(1)}, f32[4,16,384]{2,1,0:T(8,128)S(1)}, u32[]{:S(2)}, u32[]{:S(2)}) collective-permute-start(f32[4,16,384]{2,1,0:T(8,128)S(1)} %get-tuple-element.33), channel_id=1, source_target_pairs={{0,4},{2,6},{4,0},{6,2},{8,12},{10,14},{12,8},{14,10},{16,20},{18,... | collective-permute-start | bytes 294920 | tf_op jit(solution)/shard_map/ppermute | solution.py:446
  26.4 2.0 %collective-permute-done.3 = f32[4,16,384]{2,1,0:T(8,128)S(1)} collective-permute-done((f32[4,16,384]{2,1,0:T(8,128)S(1)}, f32[4,16,384]{2,1,0:T(8,128)S(1)}, u32[]{:S(2)}, u32[]{:S(2)}) %collective-permute-start.3) | collective-permute-done | bytes 98336 | tf_op jit(solution)/shard_map/ppermute | solution.py:446
  28.4 0.4 collective-permute-done.1
  28.8 0.9 %collective-permute-done.2 = f32[4,16,384]{2,1,0:T(8,128)S(1)} collective-permute-done((f32[4,16,384]{2,1,0:T(8,128)S(1)}, f32[4,16,384]{2,1,0:T(8,128)S(1)}, u32[]{:S(2)}, u32[]{:S(2)}) %collective-permute-start.2) | collective-permute-done | bytes 98336 | tf_op jit(solution)/shard_map/ppermute | solution.py:446
  29.7 0.9 %collective-permute-start.4 = (f32[4,16,384]{2,1,0:T(8,128)S(1)}, f32[4,16,384]{2,1,0:T(8,128)S(1)}, u32[]{:S(2)}, u32[]{:S(2)}) collective-permute-start(f32[4,16,384]{2,1,0:T(8,128)S(1)} %add_add_fusion), channel_id=1, source_target_pairs={{0,8},{2,10},{4,12},{6,14},{8,0},{10,2},{12,4},{14,6},{16,24},{18,... | collective-permute-start | bytes 294920 | tf_op jit(solution)/shard_map/ppermute | solution.py:446
  30.7 4.1 %collective-permute-done.4 = f32[4,16,384]{2,1,0:T(8,128)S(1)} collective-permute-done((f32[4,16,384]{2,1,0:T(8,128)S(1)}, f32[4,16,384]{2,1,0:T(8,128)S(1)}, u32[]{:S(2)}, u32[]{:S(2)}) %collective-permute-start.4) | collective-permute-done | bytes 98336 | tf_op jit(solution)/shard_map/ppermute | solution.py:446
  34.8 1.1 %collective-permute-start.5 = (f32[4,16,384]{2,1,0:T(8,128)S(1)}, f32[4,16,384]{2,1,0:T(8,128)S(1)}, u32[]{:S(2)}, u32[]{:S(2)}) collective-permute-start(f32[4,16,384]{2,1,0:T(8,128)S(1)} %add.21.refs_1_), channel_id=1, source_target_pairs={{0,16},{2,18},{4,20},{6,22},{8,24},{10,26},{12,28},{14,30},{16,0},... | collective-permute-start | bytes 294920 | tf_op jit(solution)/shard_map/ppermute | solution.py:446
  35.9 1.4 %shard_map.124 = (f32[4,16,384]{2,1,0:T(8,128)S(1)}, f32[4,16,384]{2,1,0:T(8,128)S(1)}, f32[1,16,384]{2,1,0:T(8,128)S(1)}, f32[1,16,384]{2,1,0:T(8,128)S(1)}) custom-call(s32[1]{0:T(128)} %bitcast.refs_0_, f32[16,1,5760]{2,1,0:T(1,128)} %refs_1_.2, f32[16,1,5760]{2,1,0:T(1,128)} %refs_2_.1, f32[16,1,5760]{2,1,0:T(1,128)} %refs_3_.1, f32[1,5760]{1,0:T(1,128)} %refs_4_.3), custom_call_target="tpu_custom_call" | custom-call | tf_op jit(solution)/shard_map/pallas_call | solution.py:33
  37.3 4.2 %collective-permute-done.5.refs_2_ = f32[4,16,384]{2,1,0:T(8,128)S(1)} collective-permute-done((f32[4,16,384]{2,1,0:T(8,128)S(1)}, f32[4,16,384]{2,1,0:T(8,128)S(1)}, u32[]{:S(2)}, u32[]{:S(2)}) %collective-permute-start.5) | collective-permute-done | bytes 98336 | tf_op jit(solution)/shard_map/ppermute | solution.py:446
  41.4 0.3 shard_map.125
  41.7 0.5 %collective-permute-start.6 = (f32[16,128]{1,0:T(8,128)S(1)}, f32[16,128]{1,0:T(8,128)S(1)}, u32[]{:S(2)}, u32[]{:S(2)}) collective-permute-start(f32[16,128]{1,0:T(8,128)S(1)} %get-tuple-element.42), channel_id=1, source_target_pairs={{0,2},{2,0},{4,6},{6,4},{8,10},{10,8},{12,14},{14,12},{16,18},{18,... | collective-permute-start | bytes 24584 | tf_op jit(solution)/shard_map/ppermute | solution.py:446
  42.2 3.1 %collective-permute-done.6 = f32[16,128]{1,0:T(8,128)S(1)} collective-permute-done((f32[16,128]{1,0:T(8,128)S(1)}, f32[16,128]{1,0:T(8,128)S(1)}, u32[]{:S(2)}, u32[]{:S(2)}) %collective-permute-start.6) | collective-permute-done | bytes 8224 | tf_op jit(solution)/shard_map/ppermute | solution.py:446
  45.3 1.2 %collective-permute-start.7 = (f32[16,128]{1,0:T(8,128)S(1)}, f32[16,128]{1,0:T(8,128)S(1)}, u32[]{:S(2)}, u32[]{:S(2)}) collective-permute-start(f32[16,128]{1,0:T(8,128)S(1)} %add.22), channel_id=1, source_target_pairs={{0,4},{2,6},{4,0},{6,2},{8,12},{10,14},{12,8},{14,10},{16,20},{18,... | collective-permute-start | bytes 24584 | tf_op jit(solution)/shard_map/ppermute | solution.py:446
  46.5 2.5 %collective-permute-done.7 = f32[16,128]{1,0:T(8,128)S(1)} collective-permute-done((f32[16,128]{1,0:T(8,128)S(1)}, f32[16,128]{1,0:T(8,128)S(1)}, u32[]{:S(2)}, u32[]{:S(2)}) %collective-permute-start.7) | collective-permute-done | bytes 8224 | tf_op jit(solution)/shard_map/ppermute | solution.py:446
  49.0 0.0 collective-permute-start.8
  49.0 1.2 %collective-permute-done.8.refs_6_ = f32[16,128]{1,0:T(8,128)S(1)} collective-permute-done((f32[16,128]{1,0:T(8,128)S(1)}, f32[16,128]{1,0:T(8,128)S(1)}, u32[]{:S(2)}, u32[]{:S(2)}) %collective-permute-start.8) | collective-permute-done | bytes 8224 | tf_op jit(solution)/shard_map/ppermute | solution.py:446
  50.2 0.7 %shard_map.126 = (f32[16,1,360]{2,1,0:T(1,128)}, f32[16,1,360]{2,1,0:T(1,128)}, f32[16,1,360]{2,1,0:T(1,128)}) custom-call(f32[16,128]{1,0:T(8,128)S(1)} %get-tuple-element.25.refs_3_.refs_0_, f32[16,384]{1,0:T(8,128)S(1)} %get-tuple-element.39.refs_1_, f32[1,16,384]{2,1,0:T(8,128)S(1)} %get-tuple-element.38.refs_7_.refs_2_, ...), custom_call_target="tpu_custom_call" | custom-call | tf_op jit(solution)/shard_map/pallas_call | solution.py:33
  (4 shorter events, 0.1 us)
Async XLA Ops:
  4.0 1.4 %collective-permute-start = (f32[80,128]{1,0:T(8,128)S(1)}, f32[80,128]{1,0:T(8,128)S(1)}, u32[]{:S(2)}, u32[]{:S(2)}) collective-permute-start(f32[80,128]{1,0:T(8,128)S(1)} %get-tuple-element.24.refs_2_), channel_id=1, source_target_pairs={{0,1},{1,0},{2,3},{3,2},{4,5},{5,4},{6,7},{7,6},{8,9},{9,8},{10,11... | collective-permute-start | bytes 122888 | tf_op jit(solution)/shard_map/ppermute | solution.py:446
  22.8 5.6 %collective-permute-start.3 = (f32[4,16,384]{2,1,0:T(8,128)S(1)}, f32[4,16,384]{2,1,0:T(8,128)S(1)}, u32[]{:S(2)}, u32[]{:S(2)}) collective-permute-start(f32[4,16,384]{2,1,0:T(8,128)S(1)} %get-tuple-element.34), channel_id=1, source_target_pairs={{0,6},{2,4},{4,2},{6,0},{8,14},{10,12},{12,10},{14,8},{16,22},{18,... | collective-permute-start | bytes 294920 | tf_op jit(solution)/shard_map/ppermute | solution.py:446
  23.6 5.2 %collective-permute-start.1 = (f32[4,16,384]{2,1,0:T(8,128)S(1)}, f32[4,16,384]{2,1,0:T(8,128)S(1)}, u32[]{:S(2)}, u32[]{:S(2)}) collective-permute-start(f32[4,16,384]{2,1,0:T(8,128)S(1)} %get-tuple-element.32), channel_id=1, source_target_pairs={{0,2},{2,0},{4,6},{6,4},{8,10},{10,8},{12,14},{14,12},{16,18},{18,... | collective-permute-start | bytes 294920 | tf_op jit(solution)/shard_map/ppermute | solution.py:446
  25.1 4.6 %collective-permute-start.2 = (f32[4,16,384]{2,1,0:T(8,128)S(1)}, f32[4,16,384]{2,1,0:T(8,128)S(1)}, u32[]{:S(2)}, u32[]{:S(2)}) collective-permute-start(f32[4,16,384]{2,1,0:T(8,128)S(1)} %get-tuple-element.33), channel_id=1, source_target_pairs={{0,4},{2,6},{4,0},{6,2},{8,12},{10,14},{12,8},{14,10},{16,20},{18,... | collective-permute-start | bytes 294920 | tf_op jit(solution)/shard_map/ppermute | solution.py:446
  29.7 5.0 %collective-permute-start.4 = (f32[4,16,384]{2,1,0:T(8,128)S(1)}, f32[4,16,384]{2,1,0:T(8,128)S(1)}, u32[]{:S(2)}, u32[]{:S(2)}) collective-permute-start(f32[4,16,384]{2,1,0:T(8,128)S(1)} %add_add_fusion), channel_id=1, source_target_pairs={{0,8},{2,10},{4,12},{6,14},{8,0},{10,2},{12,4},{14,6},{16,24},{18,... | collective-permute-start | bytes 294920 | tf_op jit(solution)/shard_map/ppermute | solution.py:446
  34.8 6.6 %collective-permute-start.5 = (f32[4,16,384]{2,1,0:T(8,128)S(1)}, f32[4,16,384]{2,1,0:T(8,128)S(1)}, u32[]{:S(2)}, u32[]{:S(2)}) collective-permute-start(f32[4,16,384]{2,1,0:T(8,128)S(1)} %add.21.refs_1_), channel_id=1, source_target_pairs={{0,16},{2,18},{4,20},{6,22},{8,24},{10,26},{12,28},{14,30},{16,0},... | collective-permute-start | bytes 294920 | tf_op jit(solution)/shard_map/ppermute | solution.py:446
  41.7 3.7 %collective-permute-start.6 = (f32[16,128]{1,0:T(8,128)S(1)}, f32[16,128]{1,0:T(8,128)S(1)}, u32[]{:S(2)}, u32[]{:S(2)}) collective-permute-start(f32[16,128]{1,0:T(8,128)S(1)} %get-tuple-element.42), channel_id=1, source_target_pairs={{0,2},{2,0},{4,6},{6,4},{8,10},{10,8},{12,14},{14,12},{16,18},{18,... | collective-permute-start | bytes 24584 | tf_op jit(solution)/shard_map/ppermute | solution.py:446
  45.3 3.7 %collective-permute-start.7 = (f32[16,128]{1,0:T(8,128)S(1)}, f32[16,128]{1,0:T(8,128)S(1)}, u32[]{:S(2)}, u32[]{:S(2)}) collective-permute-start(f32[16,128]{1,0:T(8,128)S(1)} %add.22), channel_id=1, source_target_pairs={{0,4},{2,6},{4,0},{6,2},{8,12},{10,14},{12,8},{14,10},{16,20},{18,... | collective-permute-start | bytes 24584 | tf_op jit(solution)/shard_map/ppermute | solution.py:446
  49.0 1.2 %collective-permute-start.8 = (f32[16,128]{1,0:T(8,128)S(1)}, f32[16,128]{1,0:T(8,128)S(1)}, u32[]{:S(2)}, u32[]{:S(2)}) collective-permute-start(f32[16,128]{1,0:T(8,128)S(1)} %add.23.refs_5_), channel_id=1, source_target_pairs={{0,1},{1,0},{2,3},{3,2},{4,5},{5,4},{6,7},{7,6},{8,9},{9,8},{10,11... | collective-permute-start | bytes 24584 | tf_op jit(solution)/shard_map/ppermute | solution.py:446

commit v10 on v8

--- a/solution.py
+++ b/solution.py
@@ -234,8 +234,15 @@
     target = lax.broadcasted_iota(jnp.int32, (LANES, kinds * LANES), 1)
     within = target % LANES
     wanted = half + within // SLOT * SLOT + target // LANES
-    pick = jnp.where((within < half) & (source == wanted), 1.0, 0.0)
-    steps_ref[...] = jnp.dot(stacked, pick, precision=HIGHEST, preferred_element_type=F32)
+    pick = jnp.where((within < half) & (source == wanted), 1.0, 0.0).astype(BF16)
+    top = stacked.astype(BF16)
+    left = stacked - top.astype(F32)
+    centre = left.astype(BF16)
+    bottom = (left - centre.astype(F32)).astype(BF16)
+    thirds = jnp.concatenate([top, centre, bottom], axis=0)
+    picked = jnp.dot(thirds, pick, preferred_element_type=F32)
+    depth = stacked.shape[0]
+    steps_ref[...] = picked[:depth] + (picked[depth : 2 * depth] + picked[2 * depth :])
 
     copies[0].wait()
     search = search_ref[...]

time: 51.2 us -> 51.1 us (level)
  no operation moved by 1% of the time
where the time goes in v10:
time: 51.1 us; the launch traced here: 51 us
  waiting for transfers between devices  18.8 us (37%)
  blocking collectives  15.8 us (31%)
  starting transfers between devices  7.55 us (15%)
  Pallas kernels  7.41 us (15%)
  between operations  1.33 us (3%)
    ppermute x9, waiting for transfers between devices, exchange(): return lax.ppermute(value, axis, [(at, at ^ bit) for at in range(size)])  18.8 us
    all_to_all x1, blocking collectives, shards(): everyone = lax.all_to_all(send, 'tm', 0, 0)  15.8 us
    ppermute x9, starting transfers between devices, exchange(): return lax.ppermute(value, axis, [(at, at ^ bit) for at in range(size)])  7.55 us
    pallas_call x6, Pallas kernels, call(): pl.pallas_call(kernel, out_shape=outs, in_specs=specs or [vmem()] * len(a...  7.41 us
  transfers between devices with their start and end apart: 9, of which 9 were waited for; matrix products, arithmetic and copies ran while one was open for 0% of the time, Pallas kernels for 3%

profile of v10, /device:TPU:0, one launch (start us, length us, event | category | flops | bytes accessed | tf_op | source)
XLA Modules:
  0.0 51.0 jit_solution(13791652564179590347)
XLA Ops:
  0.6 3.3 %shard_map.121 = (f32[80,128]{1,0:T(8,128)S(1)}, f32[37,128]{1,0:T(8,128)S(1)}, f32[64,128]{1,0:T(8,128)S(1)}, f32[48,1536]{1,0:T(8,128)S(1)}, bf16[256,5760]{1,0:T(8,128)(2,1)S(1)}) custom-call(s32[1]{0:T(128)} %bitcast.refs_0_, s32[2,4]{1,0:T(2,128)} %bitcast.8, f32[2,2,4]{2,1,0:T(2,128)} %bitcast.6, f32[2,2,4]{2,1,0:T(2,128)} %bitcast.7, f32[4,9]{1,0:T(4,128)} %refs_4_.2, ...), custom_call_target="tpu_custom_call" | custom-call | tf_op jit(solution)/shard_map/pallas_call | solution.py:33
  3.9 0.5 %collective-permute-start = (f32[80,128]{1,0:T(8,128)S(1)}, f32[80,128]{1,0:T(8,128)S(1)}, u32[]{:S(2)}, u32[]{:S(2)}) collective-permute-start(f32[80,128]{1,0:T(8,128)S(1)} %get-tuple-element.24.refs_2_), channel_id=1, source_target_pairs={{0,1},{1,0},{2,3},{3,2},{4,5},{5,4},{6,7},{7,6},{8,9},{9,8},{10,11... | collective-permute-start | bytes 122888 | tf_op jit(solution)/shard_map/ppermute | solution.py:446
  5.1 0.2 collective-permute-done.refs_3_
  5.3 0.4 shard_map.122
  5.7 15.8 %all_to_all.5.refs_2_ = f32[16,16,128]{2,1,0:T(8,128)S(1)} all-to-all(f32[16,16,128]{2,1,0:T(8,128)S(1)} %get-tuple-element.26), channel_id=1, replica_groups=mesh['tm'=16,'order'=2] {'tm'}, dimensions={0} | all-to-all | bytes 262144 | tf_op jit(solution)/shard_map/all_to_all | solution.py:518
  21.5 1.4 %shard_map.123 = (f32[4,16,384]{2,1,0:T(8,128)S(1)}, f32[4,16,384]{2,1,0:T(8,128)S(1)}, f32[4,16,384]{2,1,0:T(8,128)S(1)}, f32[4,16,384]{2,1,0:T(8,128)S(1)}) custom-call(s32[1]{0:T(128)} %bitcast.refs_0_, s32[1]{0:T(128)S(6)} %copy.13.refs_0_.refs_1_, f32[16,16,128]{2,1,0:T(8,128)S(1)} %all_to_all.5.refs_2_, f32[64,128]{1,0:T(8,128)S(1)} %get-tuple-element.27.refs_3_, ...), custom_call_target="tpu_custom_call" | custom-call | tf_op jit(solution)/shard_map/pallas_call | solution.py:33
  22.9 0.8 %collective-permute-start.3 = (f32[4,16,384]{2,1,0:T(8,128)S(1)}, f32[4,16,384]{2,1,0:T(8,128)S(1)}, u32[]{:S(2)}, u32[]{:S(2)}) collective-permute-start(f32[4,16,384]{2,1,0:T(8,128)S(1)} %get-tuple-element.34), channel_id=1, source_target_pairs={{0,6},{2,4},{4,2},{6,0},{8,14},{10,12},{12,10},{14,8},{16,22},{18,... | collective-permute-start | bytes 294920 | tf_op jit(solution)/shard_map/ppermute | solution.py:446
  23.7 1.5 %collective-permute-start.1 = (f32[4,16,384]{2,1,0:T(8,128)S(1)}, f32[4,16,384]{2,1,0:T(8,128)S(1)}, u32[]{:S(2)}, u32[]{:S(2)}) collective-permute-start(f32[4,16,384]{2,1,0:T(8,128)S(1)} %get-tuple-element.32), channel_id=1, source_target_pairs={{0,2},{2,0},{4,6},{6,4},{8,10},{10,8},{12,14},{14,12},{16,18},{18,... | collective-permute-start | bytes 294920 | tf_op jit(solution)/shard_map/ppermute | solution.py:446
  25.1 1.3 %collective-permute-start.2 = (f32[4,16,384]{2,1,0:T(8,128)S(1)}, f32[4,16,384]{2,1,0:T(8,128)S(1)}, u32[]{:S(2)}, u32[]{:S(2)}) collective-permute-start(f32[4,16,384]{2,1,0:T(8,128)S(1)} %get-tuple-element.33), channel_id=1, source_target_pairs={{0,4},{2,6},{4,0},{6,2},{8,12},{10,14},{12,8},{14,10},{16,20},{18,... | collective-permute-start | bytes 294920 | tf_op jit(solution)/shard_map/ppermute | solution.py:446
  26.4 2.0 %collective-permute-done.3 = f32[4,16,384]{2,1,0:T(8,128)S(1)} collective-permute-done((f32[4,16,384]{2,1,0:T(8,128)S(1)}, f32[4,16,384]{2,1,0:T(8,128)S(1)}, u32[]{:S(2)}, u32[]{:S(2)}) %collective-permute-start.3) | collective-permute-done | bytes 98336 | tf_op jit(solution)/shard_map/ppermute | solution.py:446
  28.5 0.4 collective-permute-done.1
  28.8 0.9 %collective-permute-done.2 = f32[4,16,384]{2,1,0:T(8,128)S(1)} collective-permute-done((f32[4,16,384]{2,1,0:T(8,128)S(1)}, f32[4,16,384]{2,1,0:T(8,128)S(1)}, u32[]{:S(2)}, u32[]{:S(2)}) %collective-permute-start.2) | collective-permute-done | bytes 98336 | tf_op jit(solution)/shard_map/ppermute | solution.py:446
  29.8 0.9 %collective-permute-start.4 = (f32[4,16,384]{2,1,0:T(8,128)S(1)}, f32[4,16,384]{2,1,0:T(8,128)S(1)}, u32[]{:S(2)}, u32[]{:S(2)}) collective-permute-start(f32[4,16,384]{2,1,0:T(8,128)S(1)} %add_add_fusion), channel_id=1, source_target_pairs={{0,8},{2,10},{4,12},{6,14},{8,0},{10,2},{12,4},{14,6},{16,24},{18,... | collective-permute-start | bytes 294920 | tf_op jit(solution)/shard_map/ppermute | solution.py:446
  30.7 4.1 %collective-permute-done.4 = f32[4,16,384]{2,1,0:T(8,128)S(1)} collective-permute-done((f32[4,16,384]{2,1,0:T(8,128)S(1)}, f32[4,16,384]{2,1,0:T(8,128)S(1)}, u32[]{:S(2)}, u32[]{:S(2)}) %collective-permute-start.4) | collective-permute-done | bytes 98336 | tf_op jit(solution)/shard_map/ppermute | solution.py:446
  34.9 1.1 %collective-permute-start.5 = (f32[4,16,384]{2,1,0:T(8,128)S(1)}, f32[4,16,384]{2,1,0:T(8,128)S(1)}, u32[]{:S(2)}, u32[]{:S(2)}) collective-permute-start(f32[4,16,384]{2,1,0:T(8,128)S(1)} %add.21.refs_1_), channel_id=1, source_target_pairs={{0,16},{2,18},{4,20},{6,22},{8,24},{10,26},{12,28},{14,30},{16,0},... | collective-permute-start | bytes 294920 | tf_op jit(solution)/shard_map/ppermute | solution.py:446
  35.9 1.4 %shard_map.124 = (f32[4,16,384]{2,1,0:T(8,128)S(1)}, f32[4,16,384]{2,1,0:T(8,128)S(1)}, f32[1,16,384]{2,1,0:T(8,128)S(1)}, f32[1,16,384]{2,1,0:T(8,128)S(1)}) custom-call(s32[1]{0:T(128)} %bitcast.refs_0_, f32[16,1,5760]{2,1,0:T(1,128)} %refs_1_.2, f32[16,1,5760]{2,1,0:T(1,128)} %refs_2_.1, f32[16,1,5760]{2,1,0:T(1,128)} %refs_3_.1, f32[1,5760]{1,0:T(1,128)} %refs_4_.3), custom_call_target="tpu_custom_call" | custom-call | tf_op jit(solution)/shard_map/pallas_call | solution.py:33
  37.3 4.2 %collective-permute-done.5.refs_2_ = f32[4,16,384]{2,1,0:T(8,128)S(1)} collective-permute-done((f32[4,16,384]{2,1,0:T(8,128)S(1)}, f32[4,16,384]{2,1,0:T(8,128)S(1)}, u32[]{:S(2)}, u32[]{:S(2)}) %collective-permute-start.5) | collective-permute-done | bytes 98336 | tf_op jit(solution)/shard_map/ppermute | solution.py:446
  41.5 0.3 shard_map.125
  41.7 0.5 %collective-permute-start.6 = (f32[16,128]{1,0:T(8,128)S(1)}, f32[16,128]{1,0:T(8,128)S(1)}, u32[]{:S(2)}, u32[]{:S(2)}) collective-permute-start(f32[16,128]{1,0:T(8,128)S(1)} %get-tuple-element.42), channel_id=1, source_target_pairs={{0,2},{2,0},{4,6},{6,4},{8,10},{10,8},{12,14},{14,12},{16,18},{18,... | collective-permute-start | bytes 24584 | tf_op jit(solution)/shard_map/ppermute | solution.py:446
  42.3 3.1 %collective-permute-done.6 = f32[16,128]{1,0:T(8,128)S(1)} collective-permute-done((f32[16,128]{1,0:T(8,128)S(1)}, f32[16,128]{1,0:T(8,128)S(1)}, u32[]{:S(2)}, u32[]{:S(2)}) %collective-permute-start.6) | collective-permute-done | bytes 8224 | tf_op jit(solution)/shard_map/ppermute | solution.py:446
  45.4 0.9 %collective-permute-start.7 = (f32[16,128]{1,0:T(8,128)S(1)}, f32[16,128]{1,0:T(8,128)S(1)}, u32[]{:S(2)}, u32[]{:S(2)}) collective-permute-start(f32[16,128]{1,0:T(8,128)S(1)} %add.22), channel_id=1, source_target_pairs={{0,4},{2,6},{4,0},{6,2},{8,12},{10,14},{12,8},{14,10},{16,20},{18,... | collective-permute-start | bytes 24584 | tf_op jit(solution)/shard_map/ppermute | solution.py:446
  46.3 2.7 %collective-permute-done.7 = f32[16,128]{1,0:T(8,128)S(1)} collective-permute-done((f32[16,128]{1,0:T(8,128)S(1)}, f32[16,128]{1,0:T(8,128)S(1)}, u32[]{:S(2)}, u32[]{:S(2)}) %collective-permute-start.7) | collective-permute-done | bytes 8224 | tf_op jit(solution)/shard_map/ppermute | solution.py:446
  49.1 0.0 collective-permute-start.8
  49.1 1.2 %collective-permute-done.8.refs_6_ = f32[16,128]{1,0:T(8,128)S(1)} collective-permute-done((f32[16,128]{1,0:T(8,128)S(1)}, f32[16,128]{1,0:T(8,128)S(1)}, u32[]{:S(2)}, u32[]{:S(2)}) %collective-permute-start.8) | collective-permute-done | bytes 8224 | tf_op jit(solution)/shard_map/ppermute | solution.py:446
  50.2 0.7 %shard_map.126 = (f32[16,1,360]{2,1,0:T(1,128)}, f32[16,1,360]{2,1,0:T(1,128)}, f32[16,1,360]{2,1,0:T(1,128)}) custom-call(f32[16,128]{1,0:T(8,128)S(1)} %get-tuple-element.25.refs_3_.refs_0_, f32[16,384]{1,0:T(8,128)S(1)} %get-tuple-element.39.refs_1_, f32[1,16,384]{2,1,0:T(8,128)S(1)} %get-tuple-element.38.refs_7_.refs_2_, ...), custom_call_target="tpu_custom_call" | custom-call | tf_op jit(solution)/shard_map/pallas_call | solution.py:33
  (4 shorter events, 0.0 us)
Async XLA Ops:
  3.9 1.4 %collective-permute-start = (f32[80,128]{1,0:T(8,128)S(1)}, f32[80,128]{1,0:T(8,128)S(1)}, u32[]{:S(2)}, u32[]{:S(2)}) collective-permute-start(f32[80,128]{1,0:T(8,128)S(1)} %get-tuple-element.24.refs_2_), channel_id=1, source_target_pairs={{0,1},{1,0},{2,3},{3,2},{4,5},{5,4},{6,7},{7,6},{8,9},{9,8},{10,11... | collective-permute-start | bytes 122888 | tf_op jit(solution)/shard_map/ppermute | solution.py:446
  22.9 5.6 %collective-permute-start.3 = (f32[4,16,384]{2,1,0:T(8,128)S(1)}, f32[4,16,384]{2,1,0:T(8,128)S(1)}, u32[]{:S(2)}, u32[]{:S(2)}) collective-permute-start(f32[4,16,384]{2,1,0:T(8,128)S(1)} %get-tuple-element.34), channel_id=1, source_target_pairs={{0,6},{2,4},{4,2},{6,0},{8,14},{10,12},{12,10},{14,8},{16,22},{18,... | collective-permute-start | bytes 294920 | tf_op jit(solution)/shard_map/ppermute | solution.py:446
  23.7 5.2 %collective-permute-start.1 = (f32[4,16,384]{2,1,0:T(8,128)S(1)}, f32[4,16,384]{2,1,0:T(8,128)S(1)}, u32[]{:S(2)}, u32[]{:S(2)}) collective-permute-start(f32[4,16,384]{2,1,0:T(8,128)S(1)} %get-tuple-element.32), channel_id=1, source_target_pairs={{0,2},{2,0},{4,6},{6,4},{8,10},{10,8},{12,14},{14,12},{16,18},{18,... | collective-permute-start | bytes 294920 | tf_op jit(solution)/shard_map/ppermute | solution.py:446
  25.1 4.6 %collective-permute-start.2 = (f32[4,16,384]{2,1,0:T(8,128)S(1)}, f32[4,16,384]{2,1,0:T(8,128)S(1)}, u32[]{:S(2)}, u32[]{:S(2)}) collective-permute-start(f32[4,16,384]{2,1,0:T(8,128)S(1)} %get-tuple-element.33), channel_id=1, source_target_pairs={{0,4},{2,6},{4,0},{6,2},{8,12},{10,14},{12,8},{14,10},{16,20},{18,... | collective-permute-start | bytes 294920 | tf_op jit(solution)/shard_map/ppermute | solution.py:446
  29.8 5.0 %collective-permute-start.4 = (f32[4,16,384]{2,1,0:T(8,128)S(1)}, f32[4,16,384]{2,1,0:T(8,128)S(1)}, u32[]{:S(2)}, u32[]{:S(2)}) collective-permute-start(f32[4,16,384]{2,1,0:T(8,128)S(1)} %add_add_fusion), channel_id=1, source_target_pairs={{0,8},{2,10},{4,12},{6,14},{8,0},{10,2},{12,4},{14,6},{16,24},{18,... | collective-permute-start | bytes 294920 | tf_op jit(solution)/shard_map/ppermute | solution.py:446
  34.9 6.6 %collective-permute-start.5 = (f32[4,16,384]{2,1,0:T(8,128)S(1)}, f32[4,16,384]{2,1,0:T(8,128)S(1)}, u32[]{:S(2)}, u32[]{:S(2)}) collective-permute-start(f32[4,16,384]{2,1,0:T(8,128)S(1)} %add.21.refs_1_), channel_id=1, source_target_pairs={{0,16},{2,18},{4,20},{6,22},{8,24},{10,26},{12,28},{14,30},{16,0},... | collective-permute-start | bytes 294920 | tf_op jit(solution)/shard_map/ppermute | solution.py:446
  41.7 3.7 %collective-permute-start.6 = (f32[16,128]{1,0:T(8,128)S(1)}, f32[16,128]{1,0:T(8,128)S(1)}, u32[]{:S(2)}, u32[]{:S(2)}) collective-permute-start(f32[16,128]{1,0:T(8,128)S(1)} %get-tuple-element.42), channel_id=1, source_target_pairs={{0,2},{2,0},{4,6},{6,4},{8,10},{10,8},{12,14},{14,12},{16,18},{18,... | collective-permute-start | bytes 24584 | tf_op jit(solution)/shard_map/ppermute | solution.py:446
  45.4 3.7 %collective-permute-start.7 = (f32[16,128]{1,0:T(8,128)S(1)}, f32[16,128]{1,0:T(8,128)S(1)}, u32[]{:S(2)}, u32[]{:S(2)}) collective-permute-start(f32[16,128]{1,0:T(8,128)S(1)} %add.22), channel_id=1, source_target_pairs={{0,4},{2,6},{4,0},{6,2},{8,12},{10,14},{12,8},{14,10},{16,20},{18,... | collective-permute-start | bytes 24584 | tf_op jit(solution)/shard_map/ppermute | solution.py:446
  49.1 1.2 %collective-permute-start.8 = (f32[16,128]{1,0:T(8,128)S(1)}, f32[16,128]{1,0:T(8,128)S(1)}, u32[]{:S(2)}, u32[]{:S(2)}) collective-permute-start(f32[16,128]{1,0:T(8,128)S(1)} %add.23.refs_5_), channel_id=1, source_target_pairs={{0,1},{1,0},{2,3},{3,2},{4,5},{5,4},{6,7},{7,6},{8,9},{9,8},{10,11... | collective-permute-start | bytes 24584 | tf_op jit(solution)/shard_map/ppermute | solution.py:446

commit v11 on v9

--- a/solution.py
+++ b/solution.py
@@ -241,8 +241,15 @@
     target = lax.broadcasted_iota(jnp.int32, (LANES, kinds * LANES), 1)
     within = target % LANES
     wanted = half + within // SLOT * SLOT + target // LANES
-    pick = jnp.where((within < half) & (source == wanted), 1.0, 0.0)
-    steps_ref[...] = jnp.dot(stacked, pick, precision=HIGHEST, preferred_element_type=F32)
+    pick = jnp.where((within < half) & (source == wanted), 1.0, 0.0).astype(BF16)
+    top = stacked.astype(BF16)
+    left = stacked - top.astype(F32)
+    centre = left.astype(BF16)
+    bottom = (left - centre.astype(F32)).astype(BF16)
+    thirds = jnp.concatenate([top, centre, bottom], axis=0)
+    picked = jnp.dot(thirds, pick, preferred_element_type=F32)
+    depth = stacked.shape[0]
+    steps_ref[...] = picked[:depth] + (picked[depth : 2 * depth] + picked[2 * depth :])
 
     copies[0].wait()
     search = search_ref[...]

time: 51.1 us -> 51 us (level)
  no operation moved by 1% of the time
where the time goes in v11:
time: 51 us; the launch traced here: 50.9 us
  waiting for transfers between devices  18.6 us (36%)
  blocking collectives  15.8 us (31%)
  starting transfers between devices  7.79 us (15%)
  Pallas kernels  7.3 us (14%)
  between operations  1.33 us (3%)
    ppermute x9, waiting for transfers between devices, exchange(): return lax.ppermute(value, axis, [(at, at ^ bit) for at in range(size)])  18.6 us
    all_to_all x1, blocking collectives, shards(): everyone = lax.all_to_all(send, 'tm', 0, 0)  15.8 us
    ppermute x9, starting transfers between devices, exchange(): return lax.ppermute(value, axis, [(at, at ^ bit) for at in range(size)])  7.79 us
    pallas_call x6, Pallas kernels, call(): pl.pallas_call(kernel, out_shape=outs, in_specs=specs or [vmem()] * len(a...  7.3 us
  transfers between devices with their start and end apart: 9, of which 9 were waited for; matrix products, arithmetic and copies ran while one was open for 0% of the time, Pallas kernels for 3%

profile of v11, /device:TPU:0, one launch (start us, length us, event | category | flops | bytes accessed | tf_op | source)
XLA Modules:
  0.0 50.9 jit_solution(1368125822516990414)
XLA Ops:
  0.6 3.3 %shard_map.121 = (f32[80,128]{1,0:T(8,128)S(1)}, f32[37,128]{1,0:T(8,128)S(1)}, bf16[64,384]{1,0:T(8,128)(2,1)S(1)}, f32[48,1536]{1,0:T(8,128)S(1)}, bf16[256,5760]{1,0:T(8,128)(2,1)S(1)}) custom-call(s32[1]{0:T(128)} %bitcast.refs_0_, s32[2,4]{1,0:T(2,128)} %bitcast.8, f32[2,2,4]{2,1,0:T(2,128)} %bitcast.6, f32[2,2,4]{2,1,0:T(2,128)} %bitcast.7, ...), custom_call_target="tpu_custom_call" | custom-call | tf_op jit(solution)/shard_map/pallas_call | solution.py:33
  3.9 0.5 %collective-permute-start = (f32[80,128]{1,0:T(8,128)S(1)}, f32[80,128]{1,0:T(8,128)S(1)}, u32[]{:S(2)}, u32[]{:S(2)}) collective-permute-start(f32[80,128]{1,0:T(8,128)S(1)} %get-tuple-element.24.refs_2_), channel_id=1, source_target_pairs={{0,1},{1,0},{2,3},{3,2},{4,5},{5,4},{6,7},{7,6},{8,9},{9,8},{10,11... | collective-permute-start | bytes 122888 | tf_op jit(solution)/shard_map/ppermute | solution.py:453
  5.1 0.2 collective-permute-done.refs_3_
  5.3 0.4 shard_map.122
  5.7 15.8 %all_to_all.5.refs_2_ = f32[16,16,128]{2,1,0:T(8,128)S(1)} all-to-all(f32[16,16,128]{2,1,0:T(8,128)S(1)} %get-tuple-element.26), channel_id=1, replica_groups=mesh['tm'=16,'order'=2] {'tm'}, dimensions={0} | all-to-all | bytes 262144 | tf_op jit(solution)/shard_map/all_to_all | solution.py:525
  21.5 1.3 %shard_map.123 = (f32[4,16,384]{2,1,0:T(8,128)S(1)}, f32[4,16,384]{2,1,0:T(8,128)S(1)}, f32[4,16,384]{2,1,0:T(8,128)S(1)}, f32[4,16,384]{2,1,0:T(8,128)S(1)}) custom-call(s32[1]{0:T(128)} %bitcast.refs_0_, s32[1]{0:T(128)S(6)} %copy.13.refs_0_.refs_1_, f32[16,16,128]{2,1,0:T(8,128)S(1)} %all_to_all.5.refs_2_, f32[64,128]{1,0:T(8,128)S(1)} %get-tuple-element.27.refs_3_, ...), custom_call_target="tpu_custom_call" | custom-call | tf_op jit(solution)/shard_map/pallas_call | solution.py:33
  22.8 0.8 %collective-permute-start.3 = (f32[4,16,384]{2,1,0:T(8,128)S(1)}, f32[4,16,384]{2,1,0:T(8,128)S(1)}, u32[]{:S(2)}, u32[]{:S(2)}) collective-permute-start(f32[4,16,384]{2,1,0:T(8,128)S(1)} %get-tuple-element.34), channel_id=1, source_target_pairs={{0,6},{2,4},{4,2},{6,0},{8,14},{10,12},{12,10},{14,8},{16,22},{18,... | collective-permute-start | bytes 294920 | tf_op jit(solution)/shard_map/ppermute | solution.py:453
  23.6 1.5 %collective-permute-start.1 = (f32[4,16,384]{2,1,0:T(8,128)S(1)}, f32[4,16,384]{2,1,0:T(8,128)S(1)}, u32[]{:S(2)}, u32[]{:S(2)}) collective-permute-start(f32[4,16,384]{2,1,0:T(8,128)S(1)} %get-tuple-element.32), channel_id=1, source_target_pairs={{0,2},{2,0},{4,6},{6,4},{8,10},{10,8},{12,14},{14,12},{16,18},{18,... | collective-permute-start | bytes 294920 | tf_op jit(solution)/shard_map/ppermute | solution.py:453
  25.0 1.3 %collective-permute-start.2 = (f32[4,16,384]{2,1,0:T(8,128)S(1)}, f32[4,16,384]{2,1,0:T(8,128)S(1)}, u32[]{:S(2)}, u32[]{:S(2)}) collective-permute-start(f32[4,16,384]{2,1,0:T(8,128)S(1)} %get-tuple-element.33), channel_id=1, source_target_pairs={{0,4},{2,6},{4,0},{6,2},{8,12},{10,14},{12,8},{14,10},{16,20},{18,... | collective-permute-start | bytes 294920 | tf_op jit(solution)/shard_map/ppermute | solution.py:453
  26.3 2.0 %collective-permute-done.3 = f32[4,16,384]{2,1,0:T(8,128)S(1)} collective-permute-done((f32[4,16,384]{2,1,0:T(8,128)S(1)}, f32[4,16,384]{2,1,0:T(8,128)S(1)}, u32[]{:S(2)}, u32[]{:S(2)}) %collective-permute-start.3) | collective-permute-done | bytes 98336 | tf_op jit(solution)/shard_map/ppermute | solution.py:453
  28.4 0.4 collective-permute-done.1
  28.7 0.9 %collective-permute-done.2 = f32[4,16,384]{2,1,0:T(8,128)S(1)} collective-permute-done((f32[4,16,384]{2,1,0:T(8,128)S(1)}, f32[4,16,384]{2,1,0:T(8,128)S(1)}, u32[]{:S(2)}, u32[]{:S(2)}) %collective-permute-start.2) | collective-permute-done | bytes 98336 | tf_op jit(solution)/shard_map/ppermute | solution.py:453
  29.7 0.9 %collective-permute-start.4 = (f32[4,16,384]{2,1,0:T(8,128)S(1)}, f32[4,16,384]{2,1,0:T(8,128)S(1)}, u32[]{:S(2)}, u32[]{:S(2)}) collective-permute-start(f32[4,16,384]{2,1,0:T(8,128)S(1)} %add_add_fusion), channel_id=1, source_target_pairs={{0,8},{2,10},{4,12},{6,14},{8,0},{10,2},{12,4},{14,6},{16,24},{18,... | collective-permute-start | bytes 294920 | tf_op jit(solution)/shard_map/ppermute | solution.py:453
  30.6 4.1 %collective-permute-done.4 = f32[4,16,384]{2,1,0:T(8,128)S(1)} collective-permute-done((f32[4,16,384]{2,1,0:T(8,128)S(1)}, f32[4,16,384]{2,1,0:T(8,128)S(1)}, u32[]{:S(2)}, u32[]{:S(2)}) %collective-permute-start.4) | collective-permute-done | bytes 98336 | tf_op jit(solution)/shard_map/ppermute | solution.py:453
  34.7 1.1 %collective-permute-start.5 = (f32[4,16,384]{2,1,0:T(8,128)S(1)}, f32[4,16,384]{2,1,0:T(8,128)S(1)}, u32[]{:S(2)}, u32[]{:S(2)}) collective-permute-start(f32[4,16,384]{2,1,0:T(8,128)S(1)} %add.21.refs_1_), channel_id=1, source_target_pairs={{0,16},{2,18},{4,20},{6,22},{8,24},{10,26},{12,28},{14,30},{16,0},... | collective-permute-start | bytes 294920 | tf_op jit(solution)/shard_map/ppermute | solution.py:453
  35.8 1.4 %shard_map.124 = (f32[4,16,384]{2,1,0:T(8,128)S(1)}, f32[4,16,384]{2,1,0:T(8,128)S(1)}, f32[1,16,384]{2,1,0:T(8,128)S(1)}, f32[1,16,384]{2,1,0:T(8,128)S(1)}) custom-call(s32[1]{0:T(128)} %bitcast.refs_0_, f32[16,1,5760]{2,1,0:T(1,128)} %refs_1_.2, f32[16,1,5760]{2,1,0:T(1,128)} %refs_2_.1, f32[16,1,5760]{2,1,0:T(1,128)} %refs_3_.1, f32[1,5760]{1,0:T(1,128)} %refs_4_.3), custom_call_target="tpu_custom_call" | custom-call | tf_op jit(solution)/shard_map/pallas_call | solution.py:33
  37.2 4.2 %collective-permute-done.5.refs_2_ = f32[4,16,384]{2,1,0:T(8,128)S(1)} collective-permute-done((f32[4,16,384]{2,1,0:T(8,128)S(1)}, f32[4,16,384]{2,1,0:T(8,128)S(1)}, u32[]{:S(2)}, u32[]{:S(2)}) %collective-permute-start.5) | collective-permute-done | bytes 98336 | tf_op jit(solution)/shard_map/ppermute | solution.py:453
  41.4 0.3 shard_map.125
  41.6 0.5 %collective-permute-start.6 = (f32[16,128]{1,0:T(8,128)S(1)}, f32[16,128]{1,0:T(8,128)S(1)}, u32[]{:S(2)}, u32[]{:S(2)}) collective-permute-start(f32[16,128]{1,0:T(8,128)S(1)} %get-tuple-element.42), channel_id=1, source_target_pairs={{0,2},{2,0},{4,6},{6,4},{8,10},{10,8},{12,14},{14,12},{16,18},{18,... | collective-permute-start | bytes 24584 | tf_op jit(solution)/shard_map/ppermute | solution.py:453
  42.2 3.1 %collective-permute-done.6 = f32[16,128]{1,0:T(8,128)S(1)} collective-permute-done((f32[16,128]{1,0:T(8,128)S(1)}, f32[16,128]{1,0:T(8,128)S(1)}, u32[]{:S(2)}, u32[]{:S(2)}) %collective-permute-start.6) | collective-permute-done | bytes 8224 | tf_op jit(solution)/shard_map/ppermute | solution.py:453
  45.3 1.2 %collective-permute-start.7 = (f32[16,128]{1,0:T(8,128)S(1)}, f32[16,128]{1,0:T(8,128)S(1)}, u32[]{:S(2)}, u32[]{:S(2)}) collective-permute-start(f32[16,128]{1,0:T(8,128)S(1)} %add.22), channel_id=1, source_target_pairs={{0,4},{2,6},{4,0},{6,2},{8,12},{10,14},{12,8},{14,10},{16,20},{18,... | collective-permute-start | bytes 24584 | tf_op jit(solution)/shard_map/ppermute | solution.py:453
  46.5 2.5 %collective-permute-done.7 = f32[16,128]{1,0:T(8,128)S(1)} collective-permute-done((f32[16,128]{1,0:T(8,128)S(1)}, f32[16,128]{1,0:T(8,128)S(1)}, u32[]{:S(2)}, u32[]{:S(2)}) %collective-permute-start.7) | collective-permute-done | bytes 8224 | tf_op jit(solution)/shard_map/ppermute | solution.py:453
  49.0 0.0 collective-permute-start.8
  49.0 1.2 %collective-permute-done.8.refs_6_ = f32[16,128]{1,0:T(8,128)S(1)} collective-permute-done((f32[16,128]{1,0:T(8,128)S(1)}, f32[16,128]{1,0:T(8,128)S(1)}, u32[]{:S(2)}, u32[]{:S(2)}) %collective-permute-start.8) | collective-permute-done | bytes 8224 | tf_op jit(solution)/shard_map/ppermute | solution.py:453
  50.1 0.7 %shard_map.126 = (f32[16,1,360]{2,1,0:T(1,128)}, f32[16,1,360]{2,1,0:T(1,128)}, f32[16,1,360]{2,1,0:T(1,128)}) custom-call(f32[16,128]{1,0:T(8,128)S(1)} %get-tuple-element.25.refs_3_.refs_0_, f32[16,384]{1,0:T(8,128)S(1)} %get-tuple-element.39.refs_1_, f32[1,16,384]{2,1,0:T(8,128)S(1)} %get-tuple-element.38.refs_7_.refs_2_, ...), custom_call_target="tpu_custom_call" | custom-call | tf_op jit(solution)/shard_map/pallas_call | solution.py:33
  (4 shorter events, 0.0 us)
Async XLA Ops:
  3.9 1.4 %collective-permute-start = (f32[80,128]{1,0:T(8,128)S(1)}, f32[80,128]{1,0:T(8,128)S(1)}, u32[]{:S(2)}, u32[]{:S(2)}) collective-permute-start(f32[80,128]{1,0:T(8,128)S(1)} %get-tuple-element.24.refs_2_), channel_id=1, source_target_pairs={{0,1},{1,0},{2,3},{3,2},{4,5},{5,4},{6,7},{7,6},{8,9},{9,8},{10,11... | collective-permute-start | bytes 122888 | tf_op jit(solution)/shard_map/ppermute | solution.py:453
  22.8 5.6 %collective-permute-start.3 = (f32[4,16,384]{2,1,0:T(8,128)S(1)}, f32[4,16,384]{2,1,0:T(8,128)S(1)}, u32[]{:S(2)}, u32[]{:S(2)}) collective-permute-start(f32[4,16,384]{2,1,0:T(8,128)S(1)} %get-tuple-element.34), channel_id=1, source_target_pairs={{0,6},{2,4},{4,2},{6,0},{8,14},{10,12},{12,10},{14,8},{16,22},{18,... | collective-permute-start | bytes 294920 | tf_op jit(solution)/shard_map/ppermute | solution.py:453
  23.6 5.2 %collective-permute-start.1 = (f32[4,16,384]{2,1,0:T(8,128)S(1)}, f32[4,16,384]{2,1,0:T(8,128)S(1)}, u32[]{:S(2)}, u32[]{:S(2)}) collective-permute-start(f32[4,16,384]{2,1,0:T(8,128)S(1)} %get-tuple-element.32), channel_id=1, source_target_pairs={{0,2},{2,0},{4,6},{6,4},{8,10},{10,8},{12,14},{14,12},{16,18},{18,... | collective-permute-start | bytes 294920 | tf_op jit(solution)/shard_map/ppermute | solution.py:453
  25.0 4.6 %collective-permute-start.2 = (f32[4,16,384]{2,1,0:T(8,128)S(1)}, f32[4,16,384]{2,1,0:T(8,128)S(1)}, u32[]{:S(2)}, u32[]{:S(2)}) collective-permute-start(f32[4,16,384]{2,1,0:T(8,128)S(1)} %get-tuple-element.33), channel_id=1, source_target_pairs={{0,4},{2,6},{4,0},{6,2},{8,12},{10,14},{12,8},{14,10},{16,20},{18,... | collective-permute-start | bytes 294920 | tf_op jit(solution)/shard_map/ppermute | solution.py:453
  29.7 5.0 %collective-permute-start.4 = (f32[4,16,384]{2,1,0:T(8,128)S(1)}, f32[4,16,384]{2,1,0:T(8,128)S(1)}, u32[]{:S(2)}, u32[]{:S(2)}) collective-permute-start(f32[4,16,384]{2,1,0:T(8,128)S(1)} %add_add_fusion), channel_id=1, source_target_pairs={{0,8},{2,10},{4,12},{6,14},{8,0},{10,2},{12,4},{14,6},{16,24},{18,... | collective-permute-start | bytes 294920 | tf_op jit(solution)/shard_map/ppermute | solution.py:453
  34.7 6.6 %collective-permute-start.5 = (f32[4,16,384]{2,1,0:T(8,128)S(1)}, f32[4,16,384]{2,1,0:T(8,128)S(1)}, u32[]{:S(2)}, u32[]{:S(2)}) collective-permute-start(f32[4,16,384]{2,1,0:T(8,128)S(1)} %add.21.refs_1_), channel_id=1, source_target_pairs={{0,16},{2,18},{4,20},{6,22},{8,24},{10,26},{12,28},{14,30},{16,0},... | collective-permute-start | bytes 294920 | tf_op jit(solution)/shard_map/ppermute | solution.py:453
  41.6 3.7 %collective-permute-start.6 = (f32[16,128]{1,0:T(8,128)S(1)}, f32[16,128]{1,0:T(8,128)S(1)}, u32[]{:S(2)}, u32[]{:S(2)}) collective-permute-start(f32[16,128]{1,0:T(8,128)S(1)} %get-tuple-element.42), channel_id=1, source_target_pairs={{0,2},{2,0},{4,6},{6,4},{8,10},{10,8},{12,14},{14,12},{16,18},{18,... | collective-permute-start | bytes 24584 | tf_op jit(solution)/shard_map/ppermute | solution.py:453
  45.3 3.7 %collective-permute-start.7 = (f32[16,128]{1,0:T(8,128)S(1)}, f32[16,128]{1,0:T(8,128)S(1)}, u32[]{:S(2)}, u32[]{:S(2)}) collective-permute-start(f32[16,128]{1,0:T(8,128)S(1)} %add.22), channel_id=1, source_target_pairs={{0,4},{2,6},{4,0},{6,2},{8,12},{10,14},{12,8},{14,10},{16,20},{18,... | collective-permute-start | bytes 24584 | tf_op jit(solution)/shard_map/ppermute | solution.py:453
  49.0 1.2 %collective-permute-start.8 = (f32[16,128]{1,0:T(8,128)S(1)}, f32[16,128]{1,0:T(8,128)S(1)}, u32[]{:S(2)}, u32[]{:S(2)}) collective-permute-start(f32[16,128]{1,0:T(8,128)S(1)} %add.23.refs_5_), channel_id=1, source_target_pairs={{0,1},{1,0},{2,3},{3,2},{4,5},{5,4},{6,7},{7,6},{8,9},{9,8},{10,11... | collective-permute-start | bytes 24584 | tf_op jit(solution)/shard_map/ppermute | solution.py:453
